TPU v7x, 256 devices: a whole 4x4x8 slice. The times are simulated.
256 devices in a mesh: tensor: 8 (over x, core), req: 32 (over y, z).
Axes of the slice: x: 4, y: 4, z: 8, core: 2. Of those that a mesh axis runs over, the one named last changes fastest.
Arguments:
- attention_output: bfloat16 [16384, 4096], P('req', 'tensor'), may hold values from -6 to 6
- residual: bfloat16 [16384, 8192], P('req', 'tensor'), may hold values from -6 to 6
- projection_weight: bfloat16 [4096, 8192], P('tensor'), may hold values from -0.09375 to 0.09375
- adapter_down_maps: bfloat16 [256, 4096, 64], P('req', 'tensor'), may hold values from -0.09375 to 0.09375
- adapter_up_maps: bfloat16 [256, 64, 8192], P('req', None, 'tensor'), may hold values from -0.75 to 0.75
- adapter_pool_slot: int32 [256], replicated, may hold values from 0 to 255, as said below
- request_adapter_id: int32 [32, 32], replicated, may hold values from 0 to 255, as said below
- request_token_length: int32 [32, 32], P('req'), may hold values from 1 to 32, 512 in all within a row
Outputs:
- mixed: bfloat16 [16384, 8192], P('req', 'tensor')
Inputs may be any that keep to these rules, and one draw needn't show every extreme that they name: `adapter_pool_slot`: each slot appears once; the slot s lies on index s // 8 of req, its owner. `request_adapter_id`: the 32 requests of one group use adapters with 32 distinct owners. `request_token_length`: each group's lengths sum to 512; in each group the largest is exactly 32.
All inputs are finite; a program needn't handle non-finite values.
Results may differ from a plain program's by a relative error of at most 0.014.
Values may be sent and summed in bfloat16 or wider, within the bound.
No kernel may reach another device: no remote copies, remote signals or barrier semaphores. Data moves between devices by JAX's collectives and lax.ppermute only.
A program may use at most 128 MiB of HBM per device.

v0:
```python
import jax
import jax.numpy as jnp
from jax import lax
from jax.sharding import PartitionSpec as P


def per_device(
    attention_output,
    residual,
    projection_weight,
    adapter_down_maps,
    adapter_up_maps,
    adapter_pool_slot,
    request_adapter_id,
    request_token_length,
):
    groups = lax.axis_size("req")
    me_index = lax.axis_index("req")
    tok_rows = attention_output.shape[0]
    features = attention_output.shape[1]
    pooled_adapter_rows = adapter_down_maps.shape[0]
    lengths = request_token_length[0]
    requests = lengths.shape[0]
    ends = jnp.cumsum(lengths)
    starts = ends - lengths
    my_ids = lax.dynamic_index_in_dim(request_adapter_id, me_index, 0, keepdims=False)
    my_owner = jnp.take(adapter_pool_slot, my_ids) // pooled_adapter_rows
    positions = jnp.arange(tok_rows, dtype=jnp.int32)
    tok_req = jnp.sum((positions[:, None] >= ends[None, :]).astype(jnp.int32), 1)
    req_hot = tok_req[:, None] == jnp.arange(requests, dtype=jnp.int32)[None, :]
    tok_owner = jnp.sum(jnp.where(req_hot, my_owner[None, :], 0), 1)
    tok_start = jnp.sum(jnp.where(req_hot, starts[None, :], 0), 1)
    all_slots = jnp.take(adapter_pool_slot, request_adapter_id)
    mine = all_slots // pooled_adapter_rows == me_index
    block_row_index = jnp.sum(jnp.where(mine, all_slots % pooled_adapter_rows, 0), 1)
    selected_down_map = jnp.take(adapter_down_maps, block_row_index, axis=0)
    selected_up_map = jnp.take(adapter_up_maps, block_row_index, axis=0)
    most_rows = 2 * tok_rows // requests
    owner_hot = my_owner[None, :] == jnp.arange(groups, dtype=jnp.int32)[:, None]
    first = jnp.sum(jnp.where(owner_hot, starts[None, :], 0), 1)
    count = jnp.sum(jnp.where(owner_hot, lengths[None, :], 0), 1)
    slot_pos = jnp.arange(most_rows, dtype=jnp.int32)
    source = first[:, None] + slot_pos[None, :]
    valid = slot_pos[None, :] < count[:, None]
    padded = jnp.concatenate([attention_output, jnp.zeros((1, features), jnp.bfloat16)], 0)
    outgoing = jnp.take(padded, jnp.where(valid, source, tok_rows), axis=0)
    partial_value = jnp.dot(attention_output, projection_weight, preferred_element_type=jnp.float32)
    base = lax.psum_scatter(
        partial_value.astype(jnp.bfloat16), "tensor", scatter_dimension=1, tiled=True
    ).astype(jnp.float32)
    reduced_rows = jnp.einsum(
        "sdy,syj->sdj",
        lax.all_to_all(outgoing, "req", split_axis=0, concat_axis=0, tiled=True),
        selected_down_map,
        preferred_element_type=jnp.float32,
    )
    reduced_rows = lax.psum(reduced_rows.astype(jnp.bfloat16), "tensor").astype(jnp.float32)
    raised_output = jnp.einsum(
        "iut,itb->iub",
        reduced_rows.astype(jnp.bfloat16),
        selected_up_map,
        preferred_element_type=jnp.float32,
    )
    returned = lax.all_to_all(
        raised_output.astype(jnp.bfloat16), "req", split_axis=0, concat_axis=0, tiled=True
    ).astype(raised_output.dtype)
    flat = returned.reshape(groups * most_rows, returned.shape[2])
    delta = jnp.take(flat, tok_owner * most_rows + positions - tok_start, axis=0)
    return (residual.astype(jnp.float32) + base + delta).astype(jnp.bfloat16)


def solution(mesh):
    in_specs = (
        P("req", "tensor"),
        P("req", "tensor"),
        P("tensor", None),
        P("req", "tensor", None),
        P("req", None, "tensor"),
        P(),
        P(),
        P("req", None),
    )
    out_specs = P("req", "tensor")
    return jax.shard_map(
        per_device, mesh=mesh, in_specs=in_specs, out_specs=out_specs, check_vma=False
    )
```

profile of v0, /device:TPU:6, one launch (start us, length us, event | category | flops | bytes accessed | tf_op | source)
XLA Modules:
  0.0 203.0 jit_solution(16693608785722491008)
XLA Ops:
  6.5 0.8 fusion.22
  7.3 0.7 copy.11
  8.1 0.1 reduce-window.4
  8.1 0.1 reduce
  8.2 1.4 gather_fusion
  9.6 0.7 fusion.24
  10.3 0.8 select_reduce_fusion.3
  11.1 0.1 fusion.19
  11.2 0.1 compare_select_fusion.1
  11.3 0.1 reshape.232
  11.4 1.1 concatenate.3
  12.5 4.0 %gather_fusion.1 = bf16[1024,512]{1,0:T(8,128)(2,1)S(1)} fusion(bf16[513,512]{1,0:T(8,128)(2,1)S(1)} %concatenate.3, s32[1024]{0:T(1024)S(1)} %broadcast_clamp_fusion), kind=kCustom, calls=%fused_computation.1 | custom fusion | bytes 2101248 | tf_op jit(solution)/shard_map/jit(_take)/gather | solution.py:46
  16.5 1.2 broadcast_select_fusion
  17.6 11.5 %all-to-all-start = ((bf16[32,32,512]{2,1,0:T(8,128)(2,1)}), bf16[32,32,512]{2,1,0:T(8,128)(2,1)S(1)}, u32[]{:S(2)}, u32[]{:S(2)}) async-start(bf16[32,32,512]{2,1,0:T(8,128)(2,1)} %broadcast_select_fusion), calls=%async_computation.1 | async-start | bytes 2097152 | tf_op jit(solution)/shard_map/all_to_all | solution.py:53
  29.2 0.1 reshape.240
  29.3 6.8 %gather_fusion.2 = s32[1024]{0:T(1024)S(1)} fusion(s32[256]{0:T(256)S(1)} %copy-done.1, s32[1024]{0:T(1024)S(1)} %broadcast_clamp_fusion.1), kind=kCustom, calls=%fused_computation.2 | custom fusion | bytes 12288 | tf_op jit(solution)/shard_map/jit(_take)/gather | solution.py:33
  36.1 0.1 reshape.239
  36.2 0.1 fusion.16
  36.4 2.0 %gather_fusion.3 = bf16[32,512,64]{1,2,0:T(8,128)(2,1)} fusion(bf16[8,512,64]{1,2,0:T(8,128)(2,1)S(1)} %copy-done.2, s32[1024]{0:T(1024)S(1)} %pad_clamp_fusion.1), kind=kCustom, calls=%fused_computation.3 | custom fusion | bytes 4194432 | tf_op jit(solution)/shard_map/jit(_take)/gather | solution.py:36
  38.4 19.3 %all-to-all-done = bf16[32,32,512]{2,1,0:T(8,128)(2,1)S(1)} async-done(((bf16[32,32,512]{2,1,0:T(8,128)(2,1)}), bf16[32,32,512]{2,1,0:T(8,128)(2,1)S(1)}, u32[]{:S(2)}, u32[]{:S(2)}) %all-to-all-start) | async-done | bytes 1048608 | tf_op jit(solution)/shard_map/all_to_all | solution.py:53
  57.7 3.1 %fusion.10 = bf16[32,32,64]{2,1,0:T(8,128)(2,1)} fusion(bf16[32,32,512]{2,1,0:T(8,128)(2,1)S(1)} %all-to-all-done, bf16[32,512,64]{1,2,0:T(8,128)(2,1)} %gather_fusion.3, pred[32]{0:T(512)(128)(4,1)S(1)} %compare_and_fusion), kind=kOutput, calls=%fused_computation.17 | convolution fusion | flops 68222976 | bytes 3276832 | tf_op jit(solution)/shard_map/sdy,syj->sdj/dot_general | solution.py:51
  60.9 10.1 %convolution_convert_fusion = bf16[512,8192]{1,0:T(8,128)(2,1)} fusion(bf16[512,512]{1,0:T(8,128)(2,1)S(1)} %copy-done.3, bf16[512,8192]{1,0:T(8,128)(2,1)} %param.10), kind=kOutput, calls=%fused_computation.6 | convolution fusion | flops 4299161600 | bytes 17301504 | tf_op jit(solution)/shard_map/dot_general | solution.py:47
  71.0 2.8 %gather_fusion.4 = bf16[32,64,1024]{2,1,0:T(8,128)(2,1)} fusion(bf16[8,64,1024]{2,1,0:T(8,128)(2,1)S(1)} %copy-done, s32[1024]{0:T(1024)S(1)} %pad_clamp_fusion.1), kind=kCustom, calls=%fused_computation.4 | custom fusion | bytes 8388736 | tf_op jit(solution)/shard_map/jit(_take)/gather | solution.py:37
  73.8 46.8 %all-reduce.3.cloned.1.call-done = bf16[32,32,64]{2,1,0:T(8,128)(2,1)} async-done(((bf16[32,32,64]{2,1,0:T(8,128)(2,1)}), bf16[32,32,64]{2,1,0:T(8,128)(2,1)}) %all-reduce.3.cloned.1.call-update) | async-done | bytes 131088 | tf_op jit(solution)/shard_map/psum | solution.py:57
  120.6 4.4 %fusion.7 = bf16[32,32,1024]{2,1,0:T(8,128)(2,1)} fusion(bf16[32,32,64]{2,1,0:T(8,128)(2,1)} %all-reduce.3.cloned.1.call-done, bf16[32,64,1024]{2,1,0:T(8,128)(2,1)} %gather_fusion.4, pred[32]{0:T(512)(128)(4,1)S(1)} %compare_and_fusion), kind=kOutput, calls=%fused_computation.16 | convolution fusion | flops 137363456 | bytes 6422560 | tf_op jit(solution)/shard_map/iut,itb->iub/dot_general | solution.py:58
  125.1 9.8 %all-to-all-start.1 = ((bf16[32,32,1024]{2,1,0:T(8,128)(2,1)}), bf16[32,32,1024]{2,1,0:T(8,128)(2,1)S(1)}, u32[]{:S(2)}, u32[]{:S(2)}) async-start(bf16[32,32,1024]{2,1,0:T(8,128)(2,1)} %fusion.7), calls=%async_computation.2 | async-start | bytes 4194304 | tf_op jit(solution)/shard_map/all_to_all | solution.py:64
  134.9 0.1 convert_reduce_fusion
  135.0 0.1 select_reduce_fusion.1
  135.2 50.4 %all-to-all-done.1 = bf16[32,32,1024]{2,1,0:T(8,128)(2,1)S(1)} async-done(((bf16[32,32,1024]{2,1,0:T(8,128)(2,1)}), bf16[32,32,1024]{2,1,0:T(8,128)(2,1)S(1)}, u32[]{:S(2)}, u32[]{:S(2)}) %all-to-all-start.1) | async-done | bytes 2097184 | tf_op jit(solution)/shard_map/all_to_all | solution.py:64
  185.6 2.6 %bitcast_convert_fusion = f32[1024,1024]{1,0:T(8,128)} fusion(bf16[32,32,1024]{2,1,0:T(8,128)(2,1)S(1)} %all-to-all-done.1), kind=kLoop, calls=%fused_computation.10 | loop fusion | flops 1048576 | bytes 6291456 | tf_op jit(solution)/shard_map/reshape | solution.py:67
  188.2 5.0 %gather_fusion.5 = f32[512,1024]{1,0:T(8,128)S(1)} fusion(f32[1024,1024]{1,0:T(8,128)} %bitcast_convert_fusion, s32[1024]{0:T(1024)S(1)} %pad_clamp_fusion), kind=kCustom, calls=%fused_computation.5 | custom fusion | bytes 4196352 | tf_op jit(solution)/shard_map/jit(_take)/gather | solution.py:68
  193.2 2.9 %add_convert_fusion = bf16[512,1024]{1,0:T(8,128)(2,1)} fusion(f32[512,1024]{1,0:T(8,128)S(1)} %gather_fusion.5, bf16[512,1024]{1,0:T(8,128)(2,1)} %reduce-scatter.2.cloned.1.call-done, bf16[512,1024]{1,0:T(8,128)(2,1)} %param.9, pred[512]{0:T(512)(128)(4,1)S(1)} %compare_and_fusion.1), kind=kLoop, calls=%fused_computation.11 | loop fusion | flops 3145728 | bytes 5243392 | tf_op jit(solution)/shard_map/convert_element_type | solution.py:69
  (26 shorter events, 0.2 us)
Async XLA Ops:
  6.5 64.5 %copy-start = (bf16[8,64,1024]{2,1,0:T(8,128)(2,1)S(1)}, bf16[8,64,1024]{2,1,0:T(8,128)(2,1)}, u32[]{:S(2)}) copy-start(bf16[8,64,1024]{2,1,0:T(8,128)(2,1)} %param.12) | copy-start | bytes 3145732
  16.4 12.7 %copy-start.4 = (s32[32,32]{1,0:T(8,128)S(1)}, s32[32,32]{1,0:T(8,128)}, u32[]{:S(2)}) copy-start(s32[32,32]{1,0:T(8,128)} %param.14) | copy-start | bytes 12292
  16.4 12.8 %copy-start.1 = (s32[256]{0:T(256)S(1)}, s32[256]{0:T(256)}, u32[]{:S(2)}) copy-start(s32[256]{0:T(256)} %param.13) | copy-start | bytes 3076
  17.6 40.1 %all-to-all-start = ((bf16[32,32,512]{2,1,0:T(8,128)(2,1)}), bf16[32,32,512]{2,1,0:T(8,128)(2,1)S(1)}, u32[]{:S(2)}, u32[]{:S(2)}) async-start(bf16[32,32,512]{2,1,0:T(8,128)(2,1)} %broadcast_select_fusion), calls=%async_computation.1 | async-start | bytes 2097152 | tf_op jit(solution)/shard_map/all_to_all | solution.py:53
  29.1 91.5 %all-reduce.3.cloned.1.call-start = ((), (), s32[]{:S(2)}) async-start(), calls=%async_computation.4 | async-start | bytes 524288 | tf_op jit(solution)/shard_map/psum | solution.py:57
  29.3 7.1 %copy-start.2 = (bf16[8,512,64]{1,2,0:T(8,128)(2,1)S(1)}, bf16[8,512,64]{1,2,0:T(8,128)(2,1)}, u32[]{:S(2)}) copy-start(bf16[8,512,64]{1,2,0:T(8,128)(2,1)} %param.11) | copy-start | bytes 1572868
  38.4 22.5 %copy-start.3 = (bf16[512,512]{1,0:T(8,128)(2,1)S(1)}, bf16[512,512]{1,0:T(8,128)(2,1)}, u32[]{:S(2)}) copy-start(bf16[512,512]{1,0:T(8,128)(2,1)} %param.8) | copy-start | bytes 1572868
  60.8 132.4 %reduce-scatter.2.cloned.1.call-start = ((), (), s32[]{:S(2)}) async-start(), calls=%async_computation.3 | async-start | bytes 9437184 | tf_op jit(solution)/shard_map/reduce_scatter | solution.py:48
  125.1 60.5 %all-to-all-start.1 = ((bf16[32,32,1024]{2,1,0:T(8,128)(2,1)}), bf16[32,32,1024]{2,1,0:T(8,128)(2,1)S(1)}, u32[]{:S(2)}, u32[]{:S(2)}) async-start(bf16[32,32,1024]{2,1,0:T(8,128)(2,1)} %fusion.7), calls=%async_computation.2 | async-start | bytes 4194304 | tf_op jit(solution)/shard_map/all_to_all | solution.py:64
Sparse Core Ops, SparseCore 0:
  61.0 59.6 all-reduce.2
  123.2 54.4 reduce-scatter.1
where the time goes:
time: 204 us; the launch traced here: 203 us
  waiting for transfers between devices  117 us (57%)
  local copies, waits for them, and re-layouts  24.1 us (12%)
  starting transfers between devices  21.4 us (10%)
  matrix products  17.6 us (9%)
  between operations  13.6 us (7%)
  other arithmetic  9.67 us (5%)
    all_to_all x1, waiting for transfers between devices, per_device(): lax.all_to_all(raised_output.astype(jnp.bfloat16), 'req', split_axis=0, c...  50.4 us
    psum x1, waiting for transfers between devices, per_device(): lax.psum(reduced_rows.astype(jnp.bfloat16), 'tensor').astype(jnp.float32)  46.8 us
    all_to_all x1, waiting for transfers between devices, per_device(): lax.all_to_all(outgoing, 'req', split_axis=0, concat_axis=0, tiled=True)  19.3 us
    all_to_all x1, starting transfers between devices, per_device(): lax.all_to_all(outgoing, 'req', split_axis=0, concat_axis=0, tiled=True)  11.5 us
    dot_general x1, matrix products, per_device(): jnp.dot(attention_output, projection_weight, preferred_element_type=jnp.f...  10.1 us
    all_to_all x1, starting transfers between devices, per_device(): lax.all_to_all(raised_output.astype(jnp.bfloat16), 'req', split_axis=0, c...  9.85 us
    gather x2, local copies, waits for them, and re-layouts, per_device(): all_slots = jnp.take(adapter_pool_slot, request_adapter_id)  6.9 us
    gather x1, local copies, waits for them, and re-layouts, per_device(): jnp.take(flat, tok_owner * most_rows + positions - tok_start, axis=0)  5.01 us
  transfers between devices with their start and end apart: 4, of which 3 were waited for; matrix products, arithmetic and copies ran while one was open for 17% of the time, Pallas kernels for 0%

commit v1 on v0

v1 whole, which is shorter than its diff:
```python
import functools

import jax
import jax.numpy as jnp
from jax import lax
from jax.experimental import pallas as pl
from jax.experimental.pallas import tpu as pltpu
from jax.sharding import PartitionSpec as P


BF = jnp.bfloat16
F32 = jnp.float32
VM = pl.BlockSpec(memory_space=pltpu.VMEM)
SM = pl.BlockSpec(memory_space=pltpu.SMEM)


def cost(flops, nbytes):
    return pl.CostEstimate(flops=int(flops), transcendentals=0, bytes_accessed=int(nbytes))


def pack_kernel(me_ref, len_ref, id_ref, slot_ref, x_ref, out_ref, sel_ref, *, pool, most):
    requests = len_ref.shape[1]
    tokens = x_ref.shape[0]
    rows = lax.broadcasted_iota(jnp.int32, (most, tokens), 0)
    ahead = lax.broadcasted_iota(jnp.int32, (most, tokens), 1) - rows
    me = me_ref[0]
    start = jnp.int32(0)
    for r in range(requests):
        owner = lax.div(slot_ref[id_ref[me, r]], jnp.int32(pool))
        count = len_ref[0, r]
        hit = (ahead == start) & (rows < count)
        at = pl.multiple_of(owner * most, most)
        sel_ref[pl.ds(at, most), :] = jnp.where(hit, 1.0, 0.0).astype(BF)
        start = start + count
    out_ref[...] = jnp.dot(sel_ref[...], x_ref[...], preferred_element_type=F32).astype(BF)


def unpack_matrix_kernel(me_ref, len_ref, id_ref, slot_ref, sel_ref, *, pool, most):
    requests = len_ref.shape[1]
    tokens = sel_ref.shape[0]
    lanes = 128
    per = lanes // most
    tok = lax.broadcasted_iota(jnp.int32, (tokens, lanes), 0)
    lane = lax.broadcasted_iota(jnp.int32, (tokens, lanes), 1)
    behind = tok - lane
    sel_ref[...] = jnp.zeros_like(sel_ref)
    me = me_ref[0]
    start = jnp.int32(0)
    for r in range(requests):
        owner = lax.div(slot_ref[id_ref[me, r]], jnp.int32(pool))
        count = len_ref[0, r]
        block = lax.div(owner, jnp.int32(per))
        off = (owner - block * per) * most
        hit = (behind == start - off) & (tok >= start) & (tok < start + count)
        at = pl.ds(pl.multiple_of(block * lanes, lanes), lanes)
        sel_ref[:, at] = sel_ref[:, at] + jnp.where(hit, 1.0, 0.0).astype(BF)
        start = start + count


def down_kernel(idx_ref, x_ref, d_ref, out_ref, *, pool):
    rank = out_ref.shape[0]
    every = lax.dot_general(d_ref[...], x_ref[...], (((1,), (1,)), ((), ())), preferred_element_type=F32)
    idx = idx_ref[...]
    acc = jnp.zeros(out_ref.shape, F32)
    for a in range(pool):
        acc = acc + jnp.where(idx == a, every[a * rank:(a + 1) * rank], 0.0)
    out_ref[...] = acc.astype(BF)


def up_kernel(idx_ref, l_ref, r_ref, u_ref, out_ref, *, pool):
    low = (l_ref[...].astype(F32) + r_ref[...].astype(F32)).astype(BF).astype(F32)
    idx = idx_ref[...]
    spread = jnp.concatenate([jnp.where(idx == a, low, 0.0).astype(BF) for a in range(pool)], 0)
    out_ref[...] = lax.dot_general(
        spread, u_ref[...], (((0,), (0,)), ((), ())), preferred_element_type=F32
    ).astype(BF)


def pair_dot_kernel(t_ref, x_ref, w_ref, out_ref):
    out_ref[0] = jnp.dot(x_ref[...], w_ref[...], preferred_element_type=F32).astype(BF)


def own_dot_kernel(t_ref, x_ref, w_ref, p_ref, ka_ref, sa_ref, kb_ref, sb_ref):
    half = x_ref.shape[0] // 2
    both = (jnp.dot(x_ref[...], w_ref[...], preferred_element_type=F32) + p_ref[0].astype(F32)).astype(BF)
    top, low = both[:half], both[half:]
    j = pl.program_id(0)

    @pl.when(j == 0)
    def _():
        ka_ref[0] = top
        kb_ref[0] = low

    @pl.when(j == 1)
    def _():
        sa_ref[0] = top
        kb_ref[1] = low

    @pl.when(j == 2)
    def _():
        ka_ref[1] = top
        sb_ref[0] = low

    @pl.when(j == 3)
    def _():
        sa_ref[1] = top
        sb_ref[1] = low


def final_kernel(sel_ref, ret_ref, res_ref, ka_ref, ra_ref, za_ref, kb_ref, rb_ref, zb_ref, out_ref):
    half = res_ref.shape[0] // 2
    delta = jnp.dot(sel_ref[...], ret_ref[...], preferred_element_type=F32)
    base_a = ka_ref[0].astype(F32) + ra_ref[0].astype(F32) + za_ref[...].astype(F32)
    base_b = kb_ref[0].astype(F32) + rb_ref[0].astype(F32) + zb_ref[...].astype(F32)
    out_ref[:half] = (res_ref[:half].astype(F32) + base_a + delta[:half]).astype(BF)
    out_ref[half:] = (res_ref[half:].astype(F32) + base_b + delta[half:]).astype(BF)


def one_block(x, residual, weight, down, up, pool_slot, req_id, req_len):
    groups = lax.axis_size("req")
    n_t = lax.axis_size("tensor")
    me = lax.axis_index("req").astype(jnp.int32)
    t = lax.axis_index("tensor").astype(jnp.int32)
    tokens, features = x.shape
    pool = down.shape[0]
    rank = down.shape[2]
    cols = residual.shape[1]
    requests = req_len.shape[1]
    most = 2 * tokens // requests
    slots = groups * most
    half = tokens // 2
    me1 = me.reshape(1)
    t1 = t.reshape(1)
    xor = lambda m: [(i, i ^ m) for i in range(n_t)]
    sds = jax.ShapeDtypeStruct

    outgoing = pl.pallas_call(
        functools.partial(pack_kernel, pool=pool, most=most),
        out_shape=sds((slots, features), BF),
        in_specs=[SM, SM, SM, SM, VM],
        out_specs=VM,
        scratch_shapes=[pltpu.VMEM((slots, tokens), BF)],
        cost_estimate=cost(2 * slots * tokens * features, 2 * (slots + tokens) * features),
        name="pack",
    )(me1, req_len, req_id, pool_slot, x)
    arrived = lax.all_to_all(outgoing.reshape(groups, most, features), "req", split_axis=0, concat_axis=0, tiled=True)

    x, _ = lax.optimization_barrier((x, outgoing))

    def blocks(j):
        return j ^ (j >> 1)

    k = n_t // 2
    wide = 2 * tokens * features * cols * k
    to_pair = pl.pallas_call(
        pair_dot_kernel,
        out_shape=sds((k, tokens, cols), BF),
        grid_spec=pltpu.PrefetchScalarGridSpec(
            num_scalar_prefetch=1,
            grid=(k,),
            in_specs=[
                pl.BlockSpec((tokens, features), lambda j, t_ref: (0, 0)),
                pl.BlockSpec((features, cols), lambda j, t_ref: (0, t_ref[0] ^ 1 ^ (2 * blocks(j)))),
            ],
            out_specs=pl.BlockSpec((1, tokens, cols), lambda j, t_ref: (j, 0, 0)),
        ),
        cost_estimate=cost(wide, 2 * k * cols * (tokens + features)),
        name="pair_dot",
    )(t1, x, weight)
    from_pair = lax.ppermute(to_pair, "tensor", xor(1))

    piece = sds((2, half, cols), BF)
    keep = pl.BlockSpec((2, half, cols), lambda j, t_ref: (0, 0, 0))
    ka, sa, kb, sb = pl.pallas_call(
        own_dot_kernel,
        out_shape=[piece] * 4,
        grid_spec=pltpu.PrefetchScalarGridSpec(
            num_scalar_prefetch=1,
            grid=(k,),
            in_specs=[
                pl.BlockSpec((tokens, features), lambda j, t_ref: (0, 0)),
                pl.BlockSpec((features, cols), lambda j, t_ref: (0, t_ref[0] ^ (2 * blocks(j)))),
                pl.BlockSpec((1, tokens, cols), lambda j, t_ref: (j, 0, 0)),
            ],
            out_specs=[keep] * 4,
        ),
        cost_estimate=cost(wide, 2 * k * cols * (2 * tokens + features)),
        name="own_dot",
    )(t1, x, weight, from_pair)

    ids = jnp.arange(pool_slot.shape[0], dtype=jnp.int32)
    held = me * pool + jnp.arange(pool, dtype=jnp.int32)
    id_of = jnp.sum(jnp.where(pool_slot[None, :] == held[:, None], ids[None, :], 0), 1)
    uses = req_id[:, :, None] == id_of[None, None, :]
    idx = jnp.sum(jnp.where(uses, jnp.arange(pool, dtype=jnp.int32), 0), (1, 2))
    idx = jnp.broadcast_to(idx[:, None], (groups, most)).reshape(1, slots)

    sel = pl.pallas_call(
        functools.partial(unpack_matrix_kernel, pool=pool, most=most),
        out_shape=sds((tokens, slots), BF),
        in_specs=[SM, SM, SM, SM],
        out_specs=VM,
        cost_estimate=cost(8 * slots * tokens, 2 * slots * tokens),
        name="unpack_matrix",
    )(me1, req_len, req_id, pool_slot)

    arrived, idx, sel, ka, sa, kb, sb = lax.optimization_barrier((arrived, idx, sel, ka, sa, kb, sb))
    low = pl.pallas_call(
        functools.partial(down_kernel, pool=pool),
        out_shape=sds((rank, slots), BF),
        in_specs=[VM, VM, VM],
        out_specs=VM,
        cost_estimate=cost(2 * slots * pool * rank * features, 2 * slots * features),
        name="down",
    )(idx, arrived.reshape(slots, features), jnp.swapaxes(down, 1, 2).reshape(pool * rank, features))
    for m in (1, 2):
        other = lax.ppermute(low, "tensor", xor(m))
        low = (low.astype(F32) + other.astype(F32)).astype(BF)
    other = lax.ppermute(low, "tensor", xor(6))

    step = slots // 4
    raised = pl.pallas_call(
        functools.partial(up_kernel, pool=pool),
        out_shape=sds((slots, cols), BF),
        grid=(4,),
        in_specs=[
            pl.BlockSpec((1, step), lambda i: (0, i)),
            pl.BlockSpec((rank, step), lambda i: (0, i)),
            pl.BlockSpec((rank, step), lambda i: (0, i)),
            pl.BlockSpec((pool * rank, cols), lambda i: (0, 0)),
        ],
        out_specs=pl.BlockSpec((step, cols), lambda i: (i, 0)),
        cost_estimate=cost(2 * slots * pool * rank * cols, 2 * slots * cols),
        name="up",
    )(idx, low, other, up.reshape(pool * rank, cols))
    raised, sa, sb = lax.optimization_barrier((raised, sa, sb))
    returned = lax.all_to_all(
        raised.reshape(groups, most, cols), "req", split_axis=0, concat_axis=0, tiled=True
    )

    ra = lax.ppermute(sa, "tensor", xor(2))
    rb = lax.ppermute(sb, "tensor", xor(6))
    za = lax.ppermute((ka[1].astype(F32) + ra[1].astype(F32)).astype(BF), "tensor", xor(6))
    zb = lax.ppermute((kb[1].astype(F32) + rb[1].astype(F32)).astype(BF), "tensor", xor(2))

    wide = cols // 4
    lead = pl.BlockSpec((1, half, wide), lambda i: (0, 0, i))
    flat = pl.BlockSpec((half, wide), lambda i: (0, i))
    return pl.pallas_call(
        final_kernel,
        out_shape=sds((tokens, cols), BF),
        grid=(4,),
        in_specs=[
            pl.BlockSpec((tokens, slots), lambda i: (0, 0)),
            pl.BlockSpec((slots, wide), lambda i: (0, i)),
            pl.BlockSpec((tokens, wide), lambda i: (0, i)),
            lead, lead, flat, lead, lead, flat,
        ],
        out_specs=pl.BlockSpec((tokens, wide), lambda i: (0, i)),
        cost_estimate=cost(2 * tokens * slots * cols, 2 * cols * (slots + 4 * tokens)),
        name="final",
    )(sel, returned.reshape(slots, cols), residual, ka, ra, za, kb, rb, zb)


def solution(mesh):
    in_specs = (
        P("req", "tensor"),
        P("req", "tensor"),
        P("tensor", None),
        P("req", "tensor", None),
        P("req", None, "tensor"),
        P(),
        P(),
        P("req", None),
    )
    return jax.shard_map(one_block, mesh=mesh, in_specs=in_specs, out_specs=P("req", "tensor"), check_vma=False)
```

time: 204 us -> 135 us (0.66)
  waiting for transfers between devices: 117 us -> 69.7 us
  Pallas kernels: 0 us -> 37.1 us
  local copies, waits for them, and re-layouts: 24.1 us -> 4.54 us
  matrix products: 17.6 us -> 0 us
  between operations: 13.6 us -> 0.12 us
  other arithmetic: 9.67 us -> 3.67 us
    psum x1 -> x0, waiting for transfers between devices: 46.8 us -> none  [per_device(): lax.psum(reduced_rows.astype(jnp.bfloat16), 'tensor').astype(jnp.float32)]
    all_to_all x2, waiting for transfers between devices: 69.8 us -> 23.1 us  [the longest x1 12.8 us: one_block(): lax.all_to_all(outgoing.reshape(groups, most, features), 'req', split_axi...]
    ppermute x0 -> x8, waiting for transfers between devices: none -> 46.6 us  [the longest x1 23.9 us: one_block(): rb = lax.ppermute(sb, 'tensor', xor(6))]
    pallas_call x0 -> x7, Pallas kernels: none -> 37.1 us  [the longest x1 7.96 us: one_block(): pl.pallas_call(own_dot_kernel, out_shape=[piece] * 4, grid_spec=pltpu.Pre...]
    gather x7 -> x0, local copies, waits for them, and re-layouts: 22.1 us -> none  [the longest x2 6.9 us: per_device(): all_slots = jnp.take(adapter_pool_slot, request_adapter_id)]
    dot_general x3 -> x0, matrix products: 17.6 us -> none  [the longest x1 10.1 us: per_device(): jnp.dot(attention_output, projection_weight, preferred_element_type=jnp.f...]
    all_to_all x2, starting transfers between devices: 21.3 us -> 16.7 us  [the longest x1 11.5 us: one_block(): lax.all_to_all(outgoing.reshape(groups, most, features), 'req', split_axi...]
    unnamed x10 -> x22, local copies, waits for them, and re-layouts: 0.02 us -> 3.78 us
  transfers between devices with their start and end apart: 4 -> 10, of which waited for: 3 -> 8; matrix products, arithmetic and copies ran while one was open for 17% -> 3% of each run, Pallas kernels for 0% -> 11%
where the time goes in v1:
time: 135 us
  waiting for transfers between devices  69.7 us (52%)
  Pallas kernels  37.1 us (27%)
  starting transfers between devices  19.4 us (14%)
  local copies, waits for them, and re-layouts  4.54 us (3%)
  other arithmetic  3.67 us (3%)
    ppermute x1, waiting for transfers between devices, one_block(): rb = lax.ppermute(sb, 'tensor', xor(6))  23.9 us
    all_to_all x1, waiting for transfers between devices, one_block(): lax.all_to_all(outgoing.reshape(groups, most, features), 'req', split_axi...  12.8 us
    all_to_all x1, starting transfers between devices, one_block(): lax.all_to_all(outgoing.reshape(groups, most, features), 'req', split_axi...  11.5 us
    all_to_all x1, waiting for transfers between devices, one_block(): lax.all_to_all(raised.reshape(groups, most, cols), 'req', split_axis=0, c...  10.3 us
    ppermute x1, waiting for transfers between devices, one_block(): lax.ppermute((kb[1].astype(F32) + rb[1].astype(F32)).astype(BF), 'tensor'...  10 us
    pallas_call x1, Pallas kernels, one_block(): pl.pallas_call(own_dot_kernel, out_shape=[piece] * 4, grid_spec=pltpu.Pre...  7.96 us
    pallas_call x1, Pallas kernels, one_block(): pl.pallas_call(functools.partial(unpack_matrix_kernel, pool=pool, most=mo...  6.71 us
    ppermute x2, waiting for transfers between devices, one_block(): other = lax.ppermute(low, 'tensor', xor(m))  6.29 us
  transfers between devices with their start and end apart: 10, of which 8 were waited for; matrix products, arithmetic and copies ran while one was open for 3% of the time, Pallas kernels for 11%

profile of v1, /device:TPU:6, one launch (start us, length us, event | category | flops | bytes accessed | tf_op | source)
XLA Modules:
  0.0 134.5 jit_solution(14439834837371830758)
XLA Ops:
  0.0 2.9 %pack.1 = bf16[1024,512]{1,0:T(8,128)(2,1)} custom-call(s32[1]{0:T(128)} %bitcast.me_ref, s32[1,32]{1,0:T(1,128)} %len_ref.3, s32[32,32]{1,0:T(8,128)} %id_ref.3, s32[256]{0:T(256)} %slot_ref.3, bf16[512,512]{1,0:T(8,128)(2,1)} %x_ref.3), custom_call_target="tpu_custom_call" | custom-call | flops 536870912 | bytes 1572864 | tf_op jit(solution)/shard_map/pack/pallas_call | solution.py:137
  2.9 6.3 %pair_dot.1 = bf16[4,512,1024]{2,1,0:T(8,128)(2,1)} custom-call(s32[1]{0:T(128)} %bitcast.2.t_ref, bf16[512,512]{1,0:T(8,128)(2,1)} %x_ref.3, bf16[512,8192]{1,0:T(8,128)(2,1)} %w_ref.3), custom_call_target="tpu_custom_call" | custom-call | flops 2147483648 | bytes 8388608 | tf_op jit(solution)/shard_map/pair_dot/pallas_call | solution.py:155
  9.2 11.5 %all-to-all-start = ((bf16[32,32,512]{2,1,0:T(8,128)(2,1)}), bf16[32,32,512]{2,1,0:T(8,128)(2,1)S(1)}, u32[]{:S(2)}, u32[]{:S(2)}) async-start(bf16[32,32,512]{2,1,0:T(8,128)(2,1)} %bitcast.1), calls=%async_computation | async-start | bytes 2097152 | tf_op jit(solution)/shard_map/all_to_all | solution.py:146
  20.7 0.2 select_reduce_fusion.1
  20.9 0.7 select_reduce_fusion
  21.7 0.7 reshape.45.idx_ref
  22.4 6.7 %unpack_matrix.1.sel_ref = bf16[512,1024]{1,0:T(8,128)(2,1)} custom-call(s32[1]{0:T(128)} %bitcast.me_ref, s32[1,32]{1,0:T(1,128)} %len_ref.3, s32[32,32]{1,0:T(8,128)} %id_ref.3, s32[256]{0:T(256)} %slot_ref.3), custom_call_target="tpu_custom_call" | custom-call | flops 4194304 | bytes 1048576 | tf_op jit(solution)/shard_map/unpack_matrix/pallas_call | solution.py:198
  29.1 8.0 %own_dot.1 = (bf16[2,256,1024]{2,1,0:T(8,128)(2,1)}, bf16[2,256,1024]{2,1,0:T(8,128)(2,1)}, bf16[2,256,1024]{2,1,0:T(8,128)(2,1)}, bf16[2,256,1024]{2,1,0:T(8,128)(2,1)}) custom-call(s32[1]{0:T(128)} %bitcast.2.t_ref, bf16[512,512]{1,0:T(8,128)(2,1)} %x_ref.3, bf16[512,8192]{1,0:T(8,128)(2,1)} %w_ref.3, bf16[4,512,1024]{2,1,0:T(8,128)(2,1)} %collective-permute-done.p_ref), custom_call_target="tpu_custom_call" | custom-call | flops 2147483648 | bytes 12582912 | tf_op jit(solution)/shard_map/own_dot/pallas_call | solution.py:174
  37.1 12.8 %all-to-all-done = bf16[32,32,512]{2,1,0:T(8,128)(2,1)S(1)} async-done(((bf16[32,32,512]{2,1,0:T(8,128)(2,1)}), bf16[32,32,512]{2,1,0:T(8,128)(2,1)S(1)}, u32[]{:S(2)}, u32[]{:S(2)}) %all-to-all-start) | async-done | bytes 1048608 | tf_op jit(solution)/shard_map/all_to_all | solution.py:146
  49.9 1.0 copy-done.4
  50.9 2.8 %down.1 = bf16[64,1024]{1,0:T(8,128)(2,1)} custom-call(s32[1,1024]{1,0:T(1,128)} %reshape.45.idx_ref, bf16[1024,512]{1,0:T(8,128)(2,1)} %bitcast.16, bf16[512,512]{1,0:T(8,128)(2,1)} %bitcast.18), custom_call_target="tpu_custom_call" | custom-call | flops 536870912 | bytes 1048576 | tf_op jit(solution)/shard_map/down/pallas_call | solution.py:208
  53.6 1.6 %collective-permute-done.1 = bf16[64,1024]{1,0:T(8,128)(2,1)S(1)} collective-permute-done((bf16[64,1024]{1,0:T(8,128)(2,1)}, bf16[64,1024]{1,0:T(8,128)(2,1)S(1)}, u32[]{:S(2)}, u32[]{:S(2)}) %collective-permute-start.1) | collective-permute-done | bytes 131104 | tf_op jit(solution)/shard_map/ppermute | solution.py:217
  55.2 0.9 add_convert_fusion.3
  56.1 0.9 collective-permute-start.2
  57.0 4.7 %collective-permute-done.2 = bf16[64,1024]{1,0:T(8,128)(2,1)S(1)} collective-permute-done((bf16[64,1024]{1,0:T(8,128)(2,1)S(1)}, bf16[64,1024]{1,0:T(8,128)(2,1)S(1)}, u32[]{:S(2)}, u32[]{:S(2)}) %collective-permute-start.2) | collective-permute-done | bytes 131104 | tf_op jit(solution)/shard_map/ppermute | solution.py:217
  61.8 0.6 collective-permute-start.3
  62.4 5.7 %collective-permute-done.3.r_ref = bf16[64,1024]{1,0:T(8,128)(2,1)S(1)} collective-permute-done((bf16[64,1024]{1,0:T(8,128)(2,1)S(1)}, bf16[64,1024]{1,0:T(8,128)(2,1)S(1)}, u32[]{:S(2)}, u32[]{:S(2)}) %collective-permute-start.3) | collective-permute-done | bytes 131104 | tf_op jit(solution)/shard_map/ppermute | solution.py:219
  68.1 0.6 copy-done.10
  68.7 4.7 %up.1 = bf16[1024,1024]{1,0:T(8,128)(2,1)} custom-call(s32[1,1024]{1,0:T(1,128)} %reshape.45.idx_ref, bf16[64,1024]{1,0:T(8,128)(2,1)} %copy-done.7, bf16[64,1024]{1,0:T(8,128)(2,1)} %copy-done.10, bf16[512,1024]{1,0:T(8,128)(2,1)} %bitcast.17), custom_call_target="tpu_custom_call" | custom-call | flops 1073741824 | bytes 2097152 | tf_op jit(solution)/shard_map/up/pallas_call | solution.py:222
  73.5 5.2 %all-to-all-start.1 = ((bf16[32,32,1024]{2,1,0:T(8,128)(2,1)}), bf16[32,32,1024]{2,1,0:T(8,128)(2,1)S(1)}, u32[]{:S(2)}, u32[]{:S(2)}) async-start(bf16[32,32,1024]{2,1,0:T(8,128)(2,1)} %bitcast.15), calls=%async_computation.1 | async-start | bytes 4194304 | tf_op jit(solution)/shard_map/all_to_all | solution.py:237
  78.7 0.6 collective-permute-start.6
  79.2 23.9 %collective-permute-done.6.rb_ref = bf16[2,256,1024]{2,1,0:T(8,128)(2,1)S(1)} collective-permute-done((bf16[2,256,1024]{2,1,0:T(8,128)(2,1)}, bf16[2,256,1024]{2,1,0:T(8,128)(2,1)S(1)}, u32[]{:S(2)}, u32[]{:S(2)}) %collective-permute-start.6) | collective-permute-done | bytes 1048608 | tf_op jit(solution)/shard_map/ppermute | solution.py:242
  103.1 1.6 %fusion.1 = bf16[256,1024]{1,0:T(8,128)(2,1)S(1)} fusion(bf16[2,256,1024]{2,1,0:T(8,128)(2,1)S(1)} %collective-permute-done.6.rb_ref, bf16[2,256,1024]{2,1,0:T(8,128)(2,1)} %get-tuple-element.33.kb_ref), kind=kLoop, calls=%fused_computation.3 | loop fusion | flops 1048576 | bytes 1572864 | tf_op jit(solution)/shard_map/convert_element_type | solution.py:244
  104.7 0.1 collective-permute-start.7
  104.8 0.2 fusion
  105.0 0.6 collective-permute-start.5
  105.6 10.0 %collective-permute-done.7.zb_ref = bf16[256,1024]{1,0:T(8,128)(2,1)S(1)} collective-permute-done((bf16[256,1024]{1,0:T(8,128)(2,1)S(1)}, bf16[256,1024]{1,0:T(8,128)(2,1)S(1)}, u32[]{:S(2)}, u32[]{:S(2)}) %collective-permute-start.7) | collective-permute-done | bytes 524320 | tf_op jit(solution)/shard_map/ppermute | solution.py:244
  115.6 0.8 copy-done.5
  116.4 0.7 collective-permute-done.5.za_ref
  117.1 10.3 %all-to-all-done.1 = bf16[32,32,1024]{2,1,0:T(8,128)(2,1)S(1)} async-done(((bf16[32,32,1024]{2,1,0:T(8,128)(2,1)}), bf16[32,32,1024]{2,1,0:T(8,128)(2,1)S(1)}, u32[]{:S(2)}, u32[]{:S(2)}) %all-to-all-start.1) | async-done | bytes 2097184 | tf_op jit(solution)/shard_map/all_to_all | solution.py:237
  127.4 1.3 copy-done
  128.8 5.8 %final.1 = bf16[512,1024]{1,0:T(8,128)(2,1)} custom-call(bf16[512,1024]{1,0:T(8,128)(2,1)} %unpack_matrix.1.sel_ref, bf16[1024,1024]{1,0:T(8,128)(2,1)} %bitcast.14, bf16[512,1024]{1,0:T(8,128)(2,1)} %res_ref.1, bf16[2,256,1024]{2,1,0:T(8,128)(2,1)} %get-tuple-element.31.ka_ref, bf16[2,256,1024]{2,1,0:T(8,128)(2,1)} %copy-done.3, ...), custom_call_target="tpu_custom_call" | custom-call | flops 1073741824 | bytes 6291456 | tf_op jit(solution)/shard_map/final/pallas_call | solution.py:249
  (26 shorter events, 0.2 us)
Async XLA Ops:
  2.9 17.8 %copy-start.9 = (s32[256]{0:T(256)S(1)}, s32[256]{0:T(256)}, u32[]{:S(2)}) copy-start(s32[256]{0:T(256)} %slot_ref.3) | copy-start | bytes 3076
  2.9 18.0 %copy-start.8 = (s32[32,32]{1,0:T(8,128)S(1)}, s32[32,32]{1,0:T(8,128)}, u32[]{:S(2)}) copy-start(s32[32,32]{1,0:T(8,128)} %id_ref.3) | copy-start | bytes 12292
  9.2 19.9 %collective-permute-start = (bf16[4,512,1024]{2,1,0:T(8,128)(2,1)}, bf16[4,512,1024]{2,1,0:T(8,128)(2,1)}, u32[]{:S(2)}, u32[]{:S(2)}) collective-permute-start(bf16[4,512,1024]{2,1,0:T(8,128)(2,1)} %pair_dot.1), channel_id=1, source_target_pairs={{0,32},{32,0},{64,96},{96,64},{128,160},{160,128},{192,224},{224,1... | collective-permute-start | bytes 12582920 | tf_op jit(solution)/shard_map/ppermute | solution.py:170
  9.2 40.7 %all-to-all-start = ((bf16[32,32,512]{2,1,0:T(8,128)(2,1)}), bf16[32,32,512]{2,1,0:T(8,128)(2,1)S(1)}, u32[]{:S(2)}, u32[]{:S(2)}) async-start(bf16[32,32,512]{2,1,0:T(8,128)(2,1)} %bitcast.1), calls=%async_computation | async-start | bytes 2097152 | tf_op jit(solution)/shard_map/all_to_all | solution.py:146
  49.9 1.0 copy-start.4
  53.6 1.6 %collective-permute-start.1 = (bf16[64,1024]{1,0:T(8,128)(2,1)}, bf16[64,1024]{1,0:T(8,128)(2,1)S(1)}, u32[]{:S(2)}, u32[]{:S(2)}) collective-permute-start(bf16[64,1024]{1,0:T(8,128)(2,1)} %down.1), channel_id=1, source_target_pairs={{0,32},{32,0},{64,96},{96,64},{128,160},{160,128},{192,224},{224,1... | collective-permute-start | bytes 393224 | tf_op jit(solution)/shard_map/ppermute | solution.py:217
  56.1 5.6 %collective-permute-start.2 = (bf16[64,1024]{1,0:T(8,128)(2,1)S(1)}, bf16[64,1024]{1,0:T(8,128)(2,1)S(1)}, u32[]{:S(2)}, u32[]{:S(2)}) collective-permute-start(bf16[64,1024]{1,0:T(8,128)(2,1)S(1)} %add_convert_fusion.3), channel_id=1, source_target_pairs={{0,64},{32,96},{64,0},{96,32},{128,192},{160,224},{192,128},{224,1... | collective-permute-start | bytes 393224 | tf_op jit(solution)/shard_map/ppermute | solution.py:217
  61.8 6.3 %copy-start.7 = (bf16[64,1024]{1,0:T(8,128)(2,1)}, bf16[64,1024]{1,0:T(8,128)(2,1)S(1)}, u32[]{:S(2)}) copy-start(bf16[64,1024]{1,0:T(8,128)(2,1)S(1)} %add_convert_fusion.2.l_ref) | copy-start | bytes 393220
  61.8 6.3 %collective-permute-start.3 = (bf16[64,1024]{1,0:T(8,128)(2,1)S(1)}, bf16[64,1024]{1,0:T(8,128)(2,1)S(1)}, u32[]{:S(2)}, u32[]{:S(2)}) collective-permute-start(bf16[64,1024]{1,0:T(8,128)(2,1)S(1)} %add_convert_fusion.2.l_ref), channel_id=1, source_target_pairs={{0,192},{32,224},{64,128},{96,160},{128,64},{160,96},{192,0},{224,... | collective-permute-start | bytes 393224 | tf_op jit(solution)/shard_map/ppermute | solution.py:219
  68.1 0.7 copy-start.10
  68.7 36.1 %copy-start.1 = (bf16[2,256,1024]{2,1,0:T(8,128)(2,1)S(1)}, bf16[2,256,1024]{2,1,0:T(8,128)(2,1)}, u32[]{:S(2)}) copy-start(bf16[2,256,1024]{2,1,0:T(8,128)(2,1)} %get-tuple-element.31.ka_ref) | copy-start | bytes 3145732
  73.5 54.0 %all-to-all-start.1 = ((bf16[32,32,1024]{2,1,0:T(8,128)(2,1)}), bf16[32,32,1024]{2,1,0:T(8,128)(2,1)S(1)}, u32[]{:S(2)}, u32[]{:S(2)}) async-start(bf16[32,32,1024]{2,1,0:T(8,128)(2,1)} %bitcast.15), calls=%async_computation.1 | async-start | bytes 4194304 | tf_op jit(solution)/shard_map/all_to_all | solution.py:237
  78.7 24.4 %collective-permute-start.6 = (bf16[2,256,1024]{2,1,0:T(8,128)(2,1)}, bf16[2,256,1024]{2,1,0:T(8,128)(2,1)S(1)}, u32[]{:S(2)}, u32[]{:S(2)}) collective-permute-start(bf16[2,256,1024]{2,1,0:T(8,128)(2,1)} %get-tuple-element.34), channel_id=1, source_target_pairs={{0,192},{32,224},{64,128},{96,160},{128,64},{160,96},{192,0},{224,... | collective-permute-start | bytes 3145736 | tf_op jit(solution)/shard_map/ppermute | solution.py:242
  79.2 25.6 %collective-permute-start.4 = (bf16[2,256,1024]{2,1,0:T(8,128)(2,1)}, bf16[2,256,1024]{2,1,0:T(8,128)(2,1)S(1)}, u32[]{:S(2)}, u32[]{:S(2)}) collective-permute-start(bf16[2,256,1024]{2,1,0:T(8,128)(2,1)} %get-tuple-element.32), channel_id=1, source_target_pairs={{0,64},{32,96},{64,0},{96,32},{128,192},{160,224},{192,128},{224,1... | collective-permute-start | bytes 3145736 | tf_op jit(solution)/shard_map/ppermute | solution.py:241
  103.1 12.5 %copy-start.2 = (bf16[2,256,1024]{2,1,0:T(8,128)(2,1)}, bf16[2,256,1024]{2,1,0:T(8,128)(2,1)S(1)}, u32[]{:S(2)}) copy-start(bf16[2,256,1024]{2,1,0:T(8,128)(2,1)S(1)} %collective-permute-done.6.rb_ref) | copy-start | bytes 3145732
  104.7 10.9 %collective-permute-start.7 = (bf16[256,1024]{1,0:T(8,128)(2,1)S(1)}, bf16[256,1024]{1,0:T(8,128)(2,1)S(1)}, u32[]{:S(2)}, u32[]{:S(2)}) collective-permute-start(bf16[256,1024]{1,0:T(8,128)(2,1)S(1)} %fusion.1), channel_id=1, source_target_pairs={{0,64},{32,96},{64,0},{96,32},{128,192},{160,224},{192,128},{224,1... | collective-permute-start | bytes 1572872 | tf_op jit(solution)/shard_map/ppermute | solution.py:244
  104.8 10.8 %copy-start.3 = (bf16[2,256,1024]{2,1,0:T(8,128)(2,1)}, bf16[2,256,1024]{2,1,0:T(8,128)(2,1)S(1)}, u32[]{:S(2)}) copy-start(bf16[2,256,1024]{2,1,0:T(8,128)(2,1)S(1)} %collective-permute-done.4.ra_ref) | copy-start | bytes 3145732
  105.0 12.1 %collective-permute-start.5 = (bf16[256,1024]{1,0:T(8,128)(2,1)S(1)}, bf16[256,1024]{1,0:T(8,128)(2,1)S(1)}, u32[]{:S(2)}, u32[]{:S(2)}) collective-permute-start(bf16[256,1024]{1,0:T(8,128)(2,1)S(1)} %fusion), channel_id=1, source_target_pairs={{0,192},{32,224},{64,128},{96,160},{128,64},{160,96},{192,0},{224,... | collective-permute-start | bytes 1572872 | tf_op jit(solution)/shard_map/ppermute | solution.py:243
  115.6 0.8 copy-start.5
  117.1 10.3 %copy-start.6 = (bf16[256,1024]{1,0:T(8,128)(2,1)}, bf16[256,1024]{1,0:T(8,128)(2,1)S(1)}, u32[]{:S(2)}) copy-start(bf16[256,1024]{1,0:T(8,128)(2,1)S(1)} %collective-permute-done.5.za_ref) | copy-start | bytes 1572868
  127.4 1.3 copy-start

commit v2 on v1

--- a/solution.py
+++ b/solution.py
@@ -12,6 +12,9 @@
 F32 = jnp.float32
 VM = pl.BlockSpec(memory_space=pltpu.VMEM)
 SM = pl.BlockSpec(memory_space=pltpu.SMEM)
+
+
+SMALL = pltpu.CompilerParams(vmem_limit_bytes=24 * 2**20)
 
 
 def cost(flops, nbytes):
@@ -57,23 +60,48 @@
         start = start + count
 
 
-def down_kernel(idx_ref, x_ref, d_ref, out_ref, *, pool):
-    rank = out_ref.shape[0]
-    every = lax.dot_general(d_ref[...], x_ref[...], (((1,), (1,)), ((), ())), preferred_element_type=F32)
-    idx = idx_ref[...]
-    acc = jnp.zeros(out_ref.shape, F32)
-    for a in range(pool):
-        acc = acc + jnp.where(idx == a, every[a * rank:(a + 1) * rank], 0.0)
-    out_ref[...] = acc.astype(BF)
-
-
-def up_kernel(idx_ref, l_ref, r_ref, u_ref, out_ref, *, pool):
-    low = (l_ref[...].astype(F32) + r_ref[...].astype(F32)).astype(BF).astype(F32)
-    idx = idx_ref[...]
-    spread = jnp.concatenate([jnp.where(idx == a, low, 0.0).astype(BF) for a in range(pool)], 0)
-    out_ref[...] = lax.dot_general(
-        spread, u_ref[...], (((0,), (0,)), ((), ())), preferred_element_type=F32
-    ).astype(BF)
+def down_kernel(code_ref, x_ref, d_ref, out_ref, *, pool):
+    rank = out_ref.shape[1] // 2
+    half = out_ref.shape[0]
+    every = lax.dot_general(x_ref[...], d_ref[...], (((1,), (1,)), ((), ())), preferred_element_type=F32)
+    code = code_ref[...]
+    acc = jnp.zeros(code.shape, F32)
+    for b in range(pool // 2):
+        acc = acc + jnp.where(code == 2 * b, every[:, 2 * b * rank:2 * (b + 1) * rank], 0.0)
+    acc = acc + pltpu.roll(acc, rank, 1)
+    first = lax.broadcasted_iota(jnp.int32, out_ref.shape, 1) < rank
+    out_ref[...] = jnp.where(first, acc[:half], acc[half:]).astype(BF)
+
+
+def add_kernel(*refs):
+    n = len(refs) // 3
+    for i in range(n):
+        refs[2 * n + i][...] = (refs[i][...].astype(F32) + refs[n + i][...].astype(F32)).astype(BF)
+
+
+def add_split_kernel(l_ref, r_ref, a_ref, b_ref):
+    both = (l_ref[...].astype(F32) + r_ref[...].astype(F32)).astype(BF)
+    half = a_ref.shape[0]
+    a_ref[...] = both[:half]
+    b_ref[...] = both[half:]
+
+
+def up_kernel(code_ref, a_ref, ra_ref, b_ref, rb_ref, u_ref, out_ref, *, pool):
+    i = pl.program_id(0)
+    rows, lanes = a_ref.shape
+    rank = lanes // 2
+    even = lax.rem(i, 2) == 0
+    a = a_ref[...].astype(F32) + ra_ref[...].astype(F32)
+    b = b_ref[...].astype(F32) + rb_ref[...].astype(F32)
+    low = jnp.where(even, a, b).astype(BF).astype(F32)
+    first = lax.broadcasted_iota(jnp.int32, low.shape, 1) < rank
+    mine = jnp.logical_xor(first, i >= 2)
+    low = jnp.where(mine, low, pltpu.roll(low, rank, 1))
+    code = code_ref[pl.ds(pl.multiple_of(i * rows, rows), rows), :]
+    spread = jnp.concatenate(
+        [jnp.where(code == 2 * k, low, 0.0).astype(BF) for k in range(pool // 2)], 1
+    )
+    out_ref[...] = jnp.dot(spread, u_ref[...], preferred_element_type=F32).astype(BF)
 
 
 def pair_dot_kernel(t_ref, x_ref, w_ref, out_ref):
@@ -107,13 +135,27 @@
         sb_ref[1] = low
 
 
-def final_kernel(sel_ref, ret_ref, res_ref, ka_ref, ra_ref, za_ref, kb_ref, rb_ref, zb_ref, out_ref):
+def before_kernel(res_ref, ka_ref, ra_ref, za_ref, kb_ref, rb_ref, zb_ref, out_ref):
     half = res_ref.shape[0] // 2
-    delta = jnp.dot(sel_ref[...], ret_ref[...], preferred_element_type=F32)
     base_a = ka_ref[0].astype(F32) + ra_ref[0].astype(F32) + za_ref[...].astype(F32)
     base_b = kb_ref[0].astype(F32) + rb_ref[0].astype(F32) + zb_ref[...].astype(F32)
-    out_ref[:half] = (res_ref[:half].astype(F32) + base_a + delta[:half]).astype(BF)
-    out_ref[half:] = (res_ref[half:].astype(F32) + base_b + delta[half:]).astype(BF)
+    out_ref[:half] = res_ref[:half].astype(F32) + base_a
+    out_ref[half:] = res_ref[half:].astype(F32) + base_b
+
+
+def final_kernel(sel_ref, ret_ref, pre_ref, out_ref):
+    wide = out_ref.shape[1]
+    at = pl.ds(pl.multiple_of(pl.program_id(0) * wide, wide), wide)
+    delta = jnp.dot(sel_ref[...], ret_ref[:, at], preferred_element_type=F32)
+    out_ref[...] = (pre_ref[...] + delta).astype(BF)
+
+
+def copy_kernel(x_ref, out_ref):
+    out_ref[...] = x_ref[...]
+
+
+def near(v):
+    return pltpu.with_memory_space_constraint(v, pltpu.VMEM)
 
 
 def one_block(x, residual, weight, down, up, pool_slot, req_id, req_len):
@@ -193,50 +235,75 @@
     id_of = jnp.sum(jnp.where(pool_slot[None, :] == held[:, None], ids[None, :], 0), 1)
     uses = req_id[:, :, None] == id_of[None, None, :]
     idx = jnp.sum(jnp.where(uses, jnp.arange(pool, dtype=jnp.int32), 0), (1, 2))
-    idx = jnp.broadcast_to(idx[:, None], (groups, most)).reshape(1, slots)
+    lane = jnp.arange(2 * rank, dtype=jnp.int32)
+    code = jnp.broadcast_to(idx[:, None, None], (groups, most, 2 * rank)) - jnp.where(lane < rank, 0, 1)
+    code = code.reshape(slots, 2 * rank)
+
+    up_maps = pl.pallas_call(
+        copy_kernel,
+        out_shape=pltpu.VMEM((pool * rank, cols), BF),
+        in_specs=[VM],
+        out_specs=VM,
+        cost_estimate=cost(0, 4 * pool * rank * cols),
+        name="fetch_up",
+        compiler_params=SMALL,
+    )(up.reshape(pool * rank, cols))
+
+    arrived, code, up_maps, ka, sa, kb, sb = lax.optimization_barrier(
+        (arrived, code, up_maps, ka, sa, kb, sb)
+    )
+    code = near(code)
+    pair = pltpu.VMEM((slots // 4, 2 * rank), BF)
+    low = pl.pallas_call(
+        functools.partial(down_kernel, pool=pool),
+        out_shape=pltpu.VMEM((slots // 2, 2 * rank), BF),
+        in_specs=[VM, VM, VM],
+        out_specs=VM,
+        cost_estimate=cost(2 * slots * pool * rank * features, 2 * slots * features),
+        name="down",
+        compiler_params=SMALL,
+    )(
+        code,
+        near(arrived.reshape(slots, features)),
+        near(jnp.swapaxes(down, 1, 2).reshape(pool * rank, features)),
+    )
+    other = lax.ppermute(low, "tensor", xor(1))
+    la, lb = pl.pallas_call(
+        add_split_kernel, out_shape=[pair] * 2, in_specs=[VM] * 2, out_specs=[VM] * 2, name="add_core", compiler_params=SMALL
+    )(near(low), near(other))
+    oa = lax.ppermute(la, "tensor", xor(2))
+    ob = lax.ppermute(lb, "tensor", xor(6))
+    la, lb = pl.pallas_call(
+        add_kernel, out_shape=[pair] * 2, in_specs=[VM] * 4, out_specs=[VM] * 2, name="add_x", compiler_params=SMALL
+    )(near(la), near(lb), near(oa), near(ob))
+    oa = lax.ppermute(la, "tensor", xor(6))
+    ob = lax.ppermute(lb, "tensor", xor(2))
+
+    step = slots // 4
+    raised = pl.pallas_call(
+        functools.partial(up_kernel, pool=pool),
+        out_shape=pltpu.HBM((slots, cols), BF),
+        grid=(4,),
+        in_specs=[VM] * 6,
+        out_specs=pl.BlockSpec((step, cols), lambda i: (i, 0)),
+        cost_estimate=cost(2 * slots * pool * rank * cols, 2 * slots * cols),
+        name="up",
+        compiler_params=SMALL,
+    )(code, near(la), near(oa), near(lb), near(ob), near(up_maps))
+    raised, sa, sb, me1 = lax.optimization_barrier((raised, sa, sb, me1))
+    returned = lax.all_to_all(
+        raised.reshape(groups, most, cols), "req", split_axis=0, concat_axis=0, tiled=True
+    )
 
     sel = pl.pallas_call(
         functools.partial(unpack_matrix_kernel, pool=pool, most=most),
-        out_shape=sds((tokens, slots), BF),
+        out_shape=pltpu.VMEM((tokens, slots), BF),
         in_specs=[SM, SM, SM, SM],
         out_specs=VM,
         cost_estimate=cost(8 * slots * tokens, 2 * slots * tokens),
         name="unpack_matrix",
+    compiler_params=SMALL,
     )(me1, req_len, req_id, pool_slot)
-
-    arrived, idx, sel, ka, sa, kb, sb = lax.optimization_barrier((arrived, idx, sel, ka, sa, kb, sb))
-    low = pl.pallas_call(
-        functools.partial(down_kernel, pool=pool),
-        out_shape=sds((rank, slots), BF),
-        in_specs=[VM, VM, VM],
-        out_specs=VM,
-        cost_estimate=cost(2 * slots * pool * rank * features, 2 * slots * features),
-        name="down",
-    )(idx, arrived.reshape(slots, features), jnp.swapaxes(down, 1, 2).reshape(pool * rank, features))
-    for m in (1, 2):
-        other = lax.ppermute(low, "tensor", xor(m))
-        low = (low.astype(F32) + other.astype(F32)).astype(BF)
-    other = lax.ppermute(low, "tensor", xor(6))
-
-    step = slots // 4
-    raised = pl.pallas_call(
-        functools.partial(up_kernel, pool=pool),
-        out_shape=sds((slots, cols), BF),
-        grid=(4,),
-        in_specs=[
-            pl.BlockSpec((1, step), lambda i: (0, i)),
-            pl.BlockSpec((rank, step), lambda i: (0, i)),
-            pl.BlockSpec((rank, step), lambda i: (0, i)),
-            pl.BlockSpec((pool * rank, cols), lambda i: (0, 0)),
-        ],
-        out_specs=pl.BlockSpec((step, cols), lambda i: (i, 0)),
-        cost_estimate=cost(2 * slots * pool * rank * cols, 2 * slots * cols),
-        name="up",
-    )(idx, low, other, up.reshape(pool * rank, cols))
-    raised, sa, sb = lax.optimization_barrier((raised, sa, sb))
-    returned = lax.all_to_all(
-        raised.reshape(groups, most, cols), "req", split_axis=0, concat_axis=0, tiled=True
-    )
 
     ra = lax.ppermute(sa, "tensor", xor(2))
     rb = lax.ppermute(sb, "tensor", xor(6))
@@ -246,20 +313,27 @@
     wide = cols // 4
     lead = pl.BlockSpec((1, half, wide), lambda i: (0, 0, i))
     flat = pl.BlockSpec((half, wide), lambda i: (0, i))
+    tall = pl.BlockSpec((tokens, wide), lambda i: (0, i))
+    pre = pl.pallas_call(
+        before_kernel,
+        out_shape=pltpu.HBM((tokens, cols), F32),
+        grid=(4,),
+        in_specs=[tall, lead, lead, flat, lead, lead, flat],
+        out_specs=tall,
+        cost_estimate=cost(4 * tokens * cols, 12 * tokens * cols),
+        name="before",
+    )(residual, ka, ra, za, kb, rb, zb)
+    returned, pre, sel = lax.optimization_barrier((returned, pre, sel))
     return pl.pallas_call(
         final_kernel,
         out_shape=sds((tokens, cols), BF),
         grid=(4,),
-        in_specs=[
-            pl.BlockSpec((tokens, slots), lambda i: (0, 0)),
-            pl.BlockSpec((slots, wide), lambda i: (0, i)),
-            pl.BlockSpec((tokens, wide), lambda i: (0, i)),
-            lead, lead, flat, lead, lead, flat,
-        ],
-        out_specs=pl.BlockSpec((tokens, wide), lambda i: (0, i)),
+        in_specs=[VM, VM, tall],
+        out_specs=tall,
         cost_estimate=cost(2 * tokens * slots * cols, 2 * cols * (slots + 4 * tokens)),
         name="final",
-    )(sel, returned.reshape(slots, cols), residual, ka, ra, za, kb, rb, zb)
+        compiler_params=pltpu.CompilerParams(vmem_limit_bytes=60 * 2**20),
+    )(near(sel), near(returned.reshape(slots, cols)), pre)
 
 
 def solution(mesh):

time: 135 us -> 132 us (0.978); the launches traced: 135 us -> 130 us
  waiting for transfers between devices: 69.7 us -> 59.7 us
  starting transfers between devices: 19.4 us -> 24.4 us
  Pallas kernels: 37.1 us -> 35.7 us
    ppermute x1, waiting for transfers between devices: 10 us -> 0.06 us  [one_block(): lax.ppermute((kb[1].astype(F32) + rb[1].astype(F32)).astype(BF), 'tensor'...]
    all_to_all x1, waiting for transfers between devices: 12.8 us -> 19.8 us  [one_block(): lax.all_to_all(outgoing.reshape(groups, most, features), 'req', split_axi...]
    all_to_all x1, waiting for transfers between devices: 10.3 us -> 4.87 us  [one_block(): lax.all_to_all(raised.reshape(groups, most, cols), 'req', split_axis=0, c...]
    ppermute x1, waiting for transfers between devices: 0.73 us -> 3.25 us  [one_block(): lax.ppermute((ka[1].astype(F32) + ra[1].astype(F32)).astype(BF), 'tensor'...]
    ppermute x1, waiting for transfers between devices: 23.9 us -> 21.7 us  [one_block(): rb = lax.ppermute(sb, 'tensor', xor(6))]
    ppermute x3 -> x5, waiting for transfers between devices: 12 us -> 10 us  [the longest x1 4.34 us: one_block(): oa = lax.ppermute(la, 'tensor', xor(6))]
    ppermute x3 -> x5, starting transfers between devices: 1.47 us -> 3.37 us  [the longest x1 1.22 us: one_block(): oa = lax.ppermute(la, 'tensor', xor(6))]
    ppermute x1, starting transfers between devices: 0.56 us -> 2.11 us  [one_block(): rb = lax.ppermute(sb, 'tensor', xor(6))]
  transfers between devices with their start and end apart: 10 -> 12, of which waited for: 8 -> 9; matrix products, arithmetic and copies ran while one was open for 3% -> 3% of each run, Pallas kernels for 11% -> 14%
where the time goes in v2:
time: 132 us; the launch traced here: 130 us
  waiting for transfers between devices  59.7 us (45%)
  Pallas kernels  35.7 us (27%)
  starting transfers between devices  24.4 us (18%)
  local copies, waits for them, and re-layouts  5.28 us (4%)
  other arithmetic  4.31 us (3%)
    ppermute x1, waiting for transfers between devices, one_block(): rb = lax.ppermute(sb, 'tensor', xor(6))  21.7 us
    all_to_all x1, waiting for transfers between devices, one_block(): lax.all_to_all(outgoing.reshape(groups, most, features), 'req', split_axi...  19.8 us
    all_to_all x1, starting transfers between devices, one_block(): lax.all_to_all(outgoing.reshape(groups, most, features), 'req', split_axi...  11.5 us
    pallas_call x1, Pallas kernels, one_block(): pl.pallas_call(own_dot_kernel, out_shape=[piece] * 4, grid_spec=pltpu.Pre...  7.98 us
    pallas_call x1, Pallas kernels, one_block(): pl.pallas_call(pair_dot_kernel, out_shape=sds((k, tokens, cols), BF), gri...  6.37 us
    pallas_call x1, Pallas kernels, one_block(): pl.pallas_call(functools.partial(unpack_matrix_kernel, pool=pool, most=mo...  5.53 us
    all_to_all x1, starting transfers between devices, one_block(): lax.all_to_all(raised.reshape(groups, most, cols), 'req', split_axis=0, c...  5.29 us
    unnamed x24, local copies, waits for them, and re-layouts  5.14 us
  transfers between devices with their start and end apart: 12, of which 9 were waited for; matrix products, arithmetic and copies ran while one was open for 3% of the time, Pallas kernels for 14%

profile of v2, /device:TPU:6, one launch (start us, length us, event | category | flops | bytes accessed | tf_op | source)
XLA Modules:
  0.0 129.6 jit_solution(17102646788666265050)
XLA Ops:
  0.0 2.9 %pack.1 = bf16[1024,512]{1,0:T(8,128)(2,1)} custom-call(s32[1]{0:T(128)} %bitcast.me_ref, s32[1,32]{1,0:T(1,128)} %len_ref.3, s32[32,32]{1,0:T(8,128)} %id_ref.3, s32[256]{0:T(256)} %slot_ref.3, bf16[512,512]{1,0:T(8,128)(2,1)} %x_ref.3), custom_call_target="tpu_custom_call" | custom-call | flops 536870912 | bytes 1572864 | tf_op jit(solution)/shard_map/pack/pallas_call | solution.py:179
  2.9 6.4 %pair_dot.1 = bf16[4,512,1024]{2,1,0:T(8,128)(2,1)} custom-call(s32[1]{0:T(128)} %bitcast.3.t_ref, bf16[512,512]{1,0:T(8,128)(2,1)} %x_ref.3, bf16[512,8192]{1,0:T(8,128)(2,1)} %w_ref.3), custom_call_target="tpu_custom_call" | custom-call | flops 2147483648 | bytes 8388608 | tf_op jit(solution)/shard_map/pair_dot/pallas_call | solution.py:197
  9.3 11.5 %all-to-all-start = ((bf16[32,32,512]{2,1,0:T(8,128)(2,1)}), bf16[32,32,512]{2,1,0:T(8,128)(2,1)S(1)}, u32[]{:S(2)}, u32[]{:S(2)}) async-start(bf16[32,32,512]{2,1,0:T(8,128)(2,1)} %bitcast.1), calls=%async_computation | async-start | bytes 2097152 | tf_op jit(solution)/shard_map/all_to_all | solution.py:188
  20.8 0.2 select_reduce_fusion.1
  21.0 0.7 select_reduce_fusion
  22.0 0.2 broadcast_subtract_fusion.code_ref
  22.2 8.0 %own_dot.1 = (bf16[2,256,1024]{2,1,0:T(8,128)(2,1)}, bf16[2,256,1024]{2,1,0:T(8,128)(2,1)}, bf16[2,256,1024]{2,1,0:T(8,128)(2,1)}, bf16[2,256,1024]{2,1,0:T(8,128)(2,1)}) custom-call(s32[1]{0:T(128)} %bitcast.3.t_ref, bf16[512,512]{1,0:T(8,128)(2,1)} %x_ref.3, bf16[512,8192]{1,0:T(8,128)(2,1)} %w_ref.3, bf16[4,512,1024]{2,1,0:T(8,128)(2,1)} %collective-permute-done.p_ref), custom_call_target="tpu_custom_call" | custom-call | flops 2147483648 | bytes 12582912 | tf_op jit(solution)/shard_map/own_dot/pallas_call | solution.py:216
  30.2 19.8 %all-to-all-done = bf16[32,32,512]{2,1,0:T(8,128)(2,1)S(1)} async-done(((bf16[32,32,512]{2,1,0:T(8,128)(2,1)}), bf16[32,32,512]{2,1,0:T(8,128)(2,1)S(1)}, u32[]{:S(2)}, u32[]{:S(2)}) %all-to-all-start) | async-done | bytes 1048608 | tf_op jit(solution)/shard_map/all_to_all | solution.py:188
  50.0 0.8 down.1.l_ref
  50.9 1.3 %collective-permute-done.1.r_ref = bf16[512,128]{1,0:T(8,128)(2,1)S(1)} collective-permute-done((bf16[512,128]{1,0:T(8,128)(2,1)S(1)}, bf16[512,128]{1,0:T(8,128)(2,1)S(1)}, u32[]{:S(2)}, u32[]{:S(2)}) %collective-permute-start.1) | collective-permute-done | bytes 131104 | tf_op jit(solution)/shard_map/ppermute | solution.py:270
  52.3 0.9 collective-permute-start.2
  53.2 1.1 collective-permute-start.3
  54.3 2.3 %collective-permute-done.2.refs_2_ = bf16[256,128]{1,0:T(8,128)(2,1)S(1)} collective-permute-done((bf16[256,128]{1,0:T(8,128)(2,1)S(1)}, bf16[256,128]{1,0:T(8,128)(2,1)S(1)}, u32[]{:S(2)}, u32[]{:S(2)}) %collective-permute-start.2) | collective-permute-done | bytes 65568 | tf_op jit(solution)/shard_map/ppermute | solution.py:274
  56.6 2.0 %collective-permute-done.3.refs_3_ = bf16[256,128]{1,0:T(8,128)(2,1)S(1)} collective-permute-done((bf16[256,128]{1,0:T(8,128)(2,1)S(1)}, bf16[256,128]{1,0:T(8,128)(2,1)S(1)}, u32[]{:S(2)}, u32[]{:S(2)}) %collective-permute-start.3) | collective-permute-done | bytes 65568 | tf_op jit(solution)/shard_map/ppermute | solution.py:275
  58.7 1.2 collective-permute-start.4
  59.9 4.3 %collective-permute-done.4.ra_ref = bf16[256,128]{1,0:T(8,128)(2,1)S(1)} collective-permute-done((bf16[256,128]{1,0:T(8,128)(2,1)S(1)}, bf16[256,128]{1,0:T(8,128)(2,1)S(1)}, u32[]{:S(2)}, u32[]{:S(2)}) %collective-permute-start.4) | collective-permute-done | bytes 65568 | tf_op jit(solution)/shard_map/ppermute | solution.py:279
  64.3 3.1 %up.1 = bf16[1024,1024]{1,0:T(8,128)(2,1)} custom-call(s32[1024,128]{1,0:T(8,128)S(1)} %broadcast_subtract_fusion.code_ref, bf16[256,128]{1,0:T(8,128)(2,1)S(1)} %get-tuple-element.37.a_ref, bf16[256,128]{1,0:T(8,128)(2,1)S(1)} %collective-permute-done.4.ra_ref, bf16[256,128]{1,0:T(8,128)(2,1)S(1)} %get-tuple-element.38.b_ref, ...), custom_call_target="tpu_custom_call" | custom-call | flops 1073741824 | bytes 2097152 | tf_op jit(solution)/shard_map/up/pallas_call | solution.py:283
  67.4 5.3 %all-to-all-start.1 = ((bf16[32,32,1024]{2,1,0:T(8,128)(2,1)}), bf16[32,32,1024]{2,1,0:T(8,128)(2,1)S(1)}, u32[]{:S(2)}, u32[]{:S(2)}) async-start(bf16[32,32,1024]{2,1,0:T(8,128)(2,1)} %bitcast.18), calls=%async_computation.1 | async-start | bytes 4194304 | tf_op jit(solution)/shard_map/all_to_all | solution.py:294
  72.7 2.1 %collective-permute-start.8 = (bf16[2,256,1024]{2,1,0:T(8,128)(2,1)}, bf16[2,256,1024]{2,1,0:T(8,128)(2,1)S(1)}, u32[]{:S(2)}, u32[]{:S(2)}) collective-permute-start(bf16[2,256,1024]{2,1,0:T(8,128)(2,1)} %get-tuple-element.46), channel_id=1, source_target_pairs={{0,192},{32,224},{64,128},{96,160},{128,64},{160,96},{192,0},{224,... | collective-permute-start | bytes 3145736 | tf_op jit(solution)/shard_map/ppermute | solution.py:309
  74.8 21.7 %collective-permute-done.8.rb_ref = bf16[2,256,1024]{2,1,0:T(8,128)(2,1)S(1)} collective-permute-done((bf16[2,256,1024]{2,1,0:T(8,128)(2,1)}, bf16[2,256,1024]{2,1,0:T(8,128)(2,1)S(1)}, u32[]{:S(2)}, u32[]{:S(2)}) %collective-permute-start.8) | collective-permute-done | bytes 1048608 | tf_op jit(solution)/shard_map/ppermute | solution.py:309
  96.5 1.6 %fusion.1 = bf16[256,1024]{1,0:T(8,128)(2,1)S(1)} fusion(bf16[2,256,1024]{2,1,0:T(8,128)(2,1)S(1)} %collective-permute-done.8.rb_ref, bf16[2,256,1024]{2,1,0:T(8,128)(2,1)} %get-tuple-element.45.kb_ref), kind=kLoop, calls=%fused_computation.3 | loop fusion | flops 1048576 | bytes 1572864 | tf_op jit(solution)/shard_map/convert_element_type | solution.py:311
  98.2 1.6 %fusion = bf16[256,1024]{1,0:T(8,128)(2,1)S(1)} fusion(bf16[2,256,1024]{2,1,0:T(8,128)(2,1)S(1)} %collective-permute-done.6.ra_ref, bf16[2,256,1024]{2,1,0:T(8,128)(2,1)} %get-tuple-element.43.ka_ref), kind=kLoop, calls=%fused_computation.2 | loop fusion | flops 1048576 | bytes 1572864 | tf_op jit(solution)/shard_map/convert_element_type | solution.py:310
  99.9 2.0 %collective-permute-start.7 = (bf16[256,1024]{1,0:T(8,128)(2,1)S(1)}, bf16[256,1024]{1,0:T(8,128)(2,1)}, u32[]{:S(2)}, u32[]{:S(2)}) collective-permute-start(bf16[256,1024]{1,0:T(8,128)(2,1)S(1)} %fusion), channel_id=1, source_target_pairs={{0,192},{32,224},{64,128},{96,160},{128,64},{160,96},{192,0},{224,... | collective-permute-start | bytes 1572872 | tf_op jit(solution)/shard_map/ppermute | solution.py:310
  101.9 5.5 %unpack_matrix.1.sel_ref = bf16[512,1024]{1,0:T(8,128)(2,1)S(1)} custom-call(s32[1]{0:T(128)} %bitcast.me_ref, s32[1,32]{1,0:T(1,128)S(1)} %copy-done.8, s32[32,32]{1,0:T(8,128)S(1)} %copy-done.6, s32[256]{0:T(256)S(1)} %copy-done.7), custom_call_target="tpu_custom_call" | custom-call | flops 4194304 | bytes 1048576 | tf_op jit(solution)/shard_map/unpack_matrix/pallas_call | solution.py:298
  107.5 1.0 copy-done.2
  108.5 3.3 %collective-permute-done.7.za_ref = bf16[256,1024]{1,0:T(8,128)(2,1)} collective-permute-done((bf16[256,1024]{1,0:T(8,128)(2,1)S(1)}, bf16[256,1024]{1,0:T(8,128)(2,1)}, u32[]{:S(2)}, u32[]{:S(2)}) %collective-permute-start.7) | collective-permute-done | bytes 524320 | tf_op jit(solution)/shard_map/ppermute | solution.py:310
  111.7 4.5 %before.1.pre_ref = f32[512,1024]{1,0:T(8,128)} custom-call(bf16[512,1024]{1,0:T(8,128)(2,1)} %res_ref.1, bf16[2,256,1024]{2,1,0:T(8,128)(2,1)} %get-tuple-element.43.ka_ref, bf16[2,256,1024]{2,1,0:T(8,128)(2,1)} %copy-done.10, bf16[256,1024]{1,0:T(8,128)(2,1)} %collective-permute-done.7.za_ref, bf16[2,256,1024]{2,1,0:T(8,128)(2,1)} %get-tuple-element.45.kb_ref, ...), custom_call_target="tpu_custom_call" | custom-call | flops 2097152 | bytes 6291456 | tf_op jit(solution)/shard_map/before/pallas_call | solution.py:317
  116.2 4.9 %all-to-all-done.1 = bf16[32,32,1024]{2,1,0:T(8,128)(2,1)S(1)} async-done(((bf16[32,32,1024]{2,1,0:T(8,128)(2,1)}), bf16[32,32,1024]{2,1,0:T(8,128)(2,1)S(1)}, u32[]{:S(2)}, u32[]{:S(2)}) %all-to-all-start.1) | async-done | bytes 2097184 | tf_op jit(solution)/shard_map/all_to_all | solution.py:294
  121.1 1.3 %copy-done = bf16[32,32,1024]{2,1,0:T(8,128)(2,1)} copy-done((bf16[32,32,1024]{2,1,0:T(8,128)(2,1)}, bf16[32,32,1024]{2,1,0:T(8,128)(2,1)S(1)}, u32[]{:S(2)}) %copy-start) | copy-done | bytes 2097176
  122.4 1.6 %copy-done.1 = bf16[32,32,1024]{2,1,0:T(8,128)(2,1)S(1)} copy-done((bf16[32,32,1024]{2,1,0:T(8,128)(2,1)S(1)}, bf16[32,32,1024]{2,1,0:T(8,128)(2,1)}, u32[]{:S(2)}) %copy-start.1) | copy-done | bytes 2097176
  124.0 1.2 copy-done.3
  125.2 4.4 %final.1 = bf16[512,1024]{1,0:T(8,128)(2,1)} custom-call(bf16[512,1024]{1,0:T(8,128)(2,1)S(1)} %copy-done.3, bf16[1024,1024]{1,0:T(8,128)(2,1)S(1)} %bitcast.14, f32[512,1024]{1,0:T(8,128)} %before.1.pre_ref), custom_call_target="tpu_custom_call" | custom-call | flops 1073741824 | bytes 6291456 | tf_op jit(solution)/shard_map/final/pallas_call | solution.py:327
  (36 shorter events, 0.6 us)
Async XLA Ops:
  2.9 17.9 %copy-start.7 = (s32[256]{0:T(256)S(1)}, s32[256]{0:T(256)}, u32[]{:S(2)}) copy-start(s32[256]{0:T(256)} %slot_ref.3) | copy-start | bytes 3076
  2.9 18.1 %copy-start.6 = (s32[32,32]{1,0:T(8,128)S(1)}, s32[32,32]{1,0:T(8,128)}, u32[]{:S(2)}) copy-start(s32[32,32]{1,0:T(8,128)} %id_ref.3) | copy-start | bytes 12292
  2.9 19.0 %copy-start.4 = (bf16[8,64,1024]{2,1,0:T(8,128)(2,1)S(1)}, bf16[8,64,1024]{2,1,0:T(8,128)(2,1)}, u32[]{:S(2)}) copy-start(bf16[8,64,1024]{2,1,0:T(8,128)(2,1)} %param.12) | copy-start | bytes 3145732
  9.3 12.9 %collective-permute-start = (bf16[4,512,1024]{2,1,0:T(8,128)(2,1)}, bf16[4,512,1024]{2,1,0:T(8,128)(2,1)}, u32[]{:S(2)}, u32[]{:S(2)}) collective-permute-start(bf16[4,512,1024]{2,1,0:T(8,128)(2,1)} %pair_dot.1), channel_id=1, source_target_pairs={{0,32},{32,0},{64,96},{96,64},{128,160},{160,128},{192,224},{224,1... | collective-permute-start | bytes 12582920 | tf_op jit(solution)/shard_map/ppermute | solution.py:212
  9.3 40.7 %all-to-all-start = ((bf16[32,32,512]{2,1,0:T(8,128)(2,1)}), bf16[32,32,512]{2,1,0:T(8,128)(2,1)S(1)}, u32[]{:S(2)}, u32[]{:S(2)}) async-start(bf16[32,32,512]{2,1,0:T(8,128)(2,1)} %bitcast.1), calls=%async_computation | async-start | bytes 2097152 | tf_op jit(solution)/shard_map/all_to_all | solution.py:188
  22.2 27.8 %copy-start.5 = (bf16[8,512,64]{1,2,0:T(8,128)(2,1)S(1)}, bf16[8,512,64]{1,2,0:T(8,128)(2,1)}, u32[]{:S(2)}) copy-start(bf16[8,512,64]{1,2,0:T(8,128)(2,1)} %param.11) | copy-start | bytes 1572868
  50.8 1.4 %collective-permute-start.1 = (bf16[512,128]{1,0:T(8,128)(2,1)S(1)}, bf16[512,128]{1,0:T(8,128)(2,1)S(1)}, u32[]{:S(2)}, u32[]{:S(2)}) collective-permute-start(bf16[512,128]{1,0:T(8,128)(2,1)S(1)} %down.1.l_ref), channel_id=1, source_target_pairs={{0,32},{32,0},{64,96},{96,64},{128,160},{160,128},{192,224},{224,1... | collective-permute-start | bytes 393224 | tf_op jit(solution)/shard_map/ppermute | solution.py:270
  52.3 4.4 %collective-permute-start.2 = (bf16[256,128]{1,0:T(8,128)(2,1)S(1)}, bf16[256,128]{1,0:T(8,128)(2,1)S(1)}, u32[]{:S(2)}, u32[]{:S(2)}) collective-permute-start(bf16[256,128]{1,0:T(8,128)(2,1)S(1)} %get-tuple-element.35.refs_0_), channel_id=1, source_target_pairs={{0,64},{32,96},{64,0},{96,32},{128,192},{160,224},{192,128},{224,1... | collective-permute-start | bytes 196616 | tf_op jit(solution)/shard_map/ppermute | solution.py:274
  53.2 5.5 %collective-permute-start.3 = (bf16[256,128]{1,0:T(8,128)(2,1)S(1)}, bf16[256,128]{1,0:T(8,128)(2,1)S(1)}, u32[]{:S(2)}, u32[]{:S(2)}) collective-permute-start(bf16[256,128]{1,0:T(8,128)(2,1)S(1)} %get-tuple-element.36.refs_1_), channel_id=1, source_target_pairs={{0,192},{32,224},{64,128},{96,160},{128,64},{160,96},{192,0},{224,... | collective-permute-start | bytes 196616 | tf_op jit(solution)/shard_map/ppermute | solution.py:275
  58.7 5.6 %collective-permute-start.4 = (bf16[256,128]{1,0:T(8,128)(2,1)S(1)}, bf16[256,128]{1,0:T(8,128)(2,1)S(1)}, u32[]{:S(2)}, u32[]{:S(2)}) collective-permute-start(bf16[256,128]{1,0:T(8,128)(2,1)S(1)} %get-tuple-element.37.a_ref), channel_id=1, source_target_pairs={{0,192},{32,224},{64,128},{96,160},{128,64},{160,96},{192,0},{224,... | collective-permute-start | bytes 196616 | tf_op jit(solution)/shard_map/ppermute | solution.py:279
  59.9 4.3 %collective-permute-start.5 = (bf16[256,128]{1,0:T(8,128)(2,1)S(1)}, bf16[256,128]{1,0:T(8,128)(2,1)S(1)}, u32[]{:S(2)}, u32[]{:S(2)}) collective-permute-start(bf16[256,128]{1,0:T(8,128)(2,1)S(1)} %get-tuple-element.38.b_ref), channel_id=1, source_target_pairs={{0,64},{32,96},{64,0},{96,32},{128,192},{160,224},{192,128},{224,1... | collective-permute-start | bytes 196616 | tf_op jit(solution)/shard_map/ppermute | solution.py:280
  67.4 34.5 %copy-start.8 = (s32[1,32]{1,0:T(1,128)S(1)}, s32[1,32]{1,0:T(1,128)}, u32[]{:S(2)}) copy-start(s32[1,32]{1,0:T(1,128)} %len_ref.3) | copy-start | bytes 388
  67.4 53.7 %all-to-all-start.1 = ((bf16[32,32,1024]{2,1,0:T(8,128)(2,1)}), bf16[32,32,1024]{2,1,0:T(8,128)(2,1)S(1)}, u32[]{:S(2)}, u32[]{:S(2)}) async-start(bf16[32,32,1024]{2,1,0:T(8,128)(2,1)} %bitcast.18), calls=%async_computation.1 | async-start | bytes 4194304 | tf_op jit(solution)/shard_map/all_to_all | solution.py:294
  72.7 23.9 %collective-permute-start.8 = (bf16[2,256,1024]{2,1,0:T(8,128)(2,1)}, bf16[2,256,1024]{2,1,0:T(8,128)(2,1)S(1)}, u32[]{:S(2)}, u32[]{:S(2)}) collective-permute-start(bf16[2,256,1024]{2,1,0:T(8,128)(2,1)} %get-tuple-element.46), channel_id=1, source_target_pairs={{0,192},{32,224},{64,128},{96,160},{128,64},{160,96},{192,0},{224,... | collective-permute-start | bytes 3145736 | tf_op jit(solution)/shard_map/ppermute | solution.py:309
  74.8 23.4 %collective-permute-start.6 = (bf16[2,256,1024]{2,1,0:T(8,128)(2,1)}, bf16[2,256,1024]{2,1,0:T(8,128)(2,1)S(1)}, u32[]{:S(2)}, u32[]{:S(2)}) collective-permute-start(bf16[2,256,1024]{2,1,0:T(8,128)(2,1)} %get-tuple-element.44), channel_id=1, source_target_pairs={{0,64},{32,96},{64,0},{96,32},{128,192},{160,224},{192,128},{224,1... | collective-permute-start | bytes 3145736 | tf_op jit(solution)/shard_map/ppermute | solution.py:308
  96.5 3.3 %copy-start.9 = (bf16[2,256,1024]{2,1,0:T(8,128)(2,1)}, bf16[2,256,1024]{2,1,0:T(8,128)(2,1)S(1)}, u32[]{:S(2)}) copy-start(bf16[2,256,1024]{2,1,0:T(8,128)(2,1)S(1)} %collective-permute-done.8.rb_ref) | copy-start | bytes 3145732
  98.1 10.3 %collective-permute-start.9 = (bf16[256,1024]{1,0:T(8,128)(2,1)S(1)}, bf16[256,1024]{1,0:T(8,128)(2,1)S(1)}, u32[]{:S(2)}, u32[]{:S(2)}) collective-permute-start(bf16[256,1024]{1,0:T(8,128)(2,1)S(1)} %fusion.1), channel_id=1, source_target_pairs={{0,64},{32,96},{64,0},{96,32},{128,192},{160,224},{192,128},{224,1... | collective-permute-start | bytes 1572872 | tf_op jit(solution)/shard_map/ppermute | solution.py:311
  98.2 1.6 %copy-start.10 = (bf16[2,256,1024]{2,1,0:T(8,128)(2,1)}, bf16[2,256,1024]{2,1,0:T(8,128)(2,1)S(1)}, u32[]{:S(2)}) copy-start(bf16[2,256,1024]{2,1,0:T(8,128)(2,1)S(1)} %collective-permute-done.6.ra_ref) | copy-start | bytes 3145732
  99.9 11.8 %collective-permute-start.7 = (bf16[256,1024]{1,0:T(8,128)(2,1)S(1)}, bf16[256,1024]{1,0:T(8,128)(2,1)}, u32[]{:S(2)}, u32[]{:S(2)}) collective-permute-start(bf16[256,1024]{1,0:T(8,128)(2,1)S(1)} %fusion), channel_id=1, source_target_pairs={{0,192},{32,224},{64,128},{96,160},{128,64},{160,96},{192,0},{224,... | collective-permute-start | bytes 1572872 | tf_op jit(solution)/shard_map/ppermute | solution.py:310
  107.4 1.0 copy-start.2
  108.5 3.3 %copy-start.11 = (bf16[256,1024]{1,0:T(8,128)(2,1)}, bf16[256,1024]{1,0:T(8,128)(2,1)S(1)}, u32[]{:S(2)}) copy-start(bf16[256,1024]{1,0:T(8,128)(2,1)S(1)} %collective-permute-done.9.zb_ref) | copy-start | bytes 1572868
  121.1 1.3 %copy-start = (bf16[32,32,1024]{2,1,0:T(8,128)(2,1)}, bf16[32,32,1024]{2,1,0:T(8,128)(2,1)S(1)}, u32[]{:S(2)}) copy-start(bf16[32,32,1024]{2,1,0:T(8,128)(2,1)S(1)} %all-to-all-done.1) | copy-start | bytes 6291460
  122.4 1.6 %copy-start.1 = (bf16[32,32,1024]{2,1,0:T(8,128)(2,1)S(1)}, bf16[32,32,1024]{2,1,0:T(8,128)(2,1)}, u32[]{:S(2)}) copy-start(bf16[32,32,1024]{2,1,0:T(8,128)(2,1)} %copy-done) | copy-start | bytes 6291460
  124.0 1.2 copy-start.3

commit v3 on v2

--- a/solution.py
+++ b/solution.py
@@ -60,43 +60,43 @@
         start = start + count
 
 
-def down_kernel(code_ref, x_ref, d_ref, out_ref, *, pool):
-    rank = out_ref.shape[1] // 2
-    half = out_ref.shape[0]
+def down_kernel(core_ref, code_ref, x_ref, d_ref, keep_ref, send_ref, *, pool):
+    half, lanes = keep_ref.shape
+    rank = lanes // 2
     every = lax.dot_general(x_ref[...], d_ref[...], (((1,), (1,)), ((), ())), preferred_element_type=F32)
     code = code_ref[...]
     acc = jnp.zeros(code.shape, F32)
     for b in range(pool // 2):
         acc = acc + jnp.where(code == 2 * b, every[:, 2 * b * rank:2 * (b + 1) * rank], 0.0)
     acc = acc + pltpu.roll(acc, rank, 1)
-    first = lax.broadcasted_iota(jnp.int32, out_ref.shape, 1) < rank
-    out_ref[...] = jnp.where(first, acc[:half], acc[half:]).astype(BF)
-
-
-def add_kernel(*refs):
-    n = len(refs) // 3
-    for i in range(n):
-        refs[2 * n + i][...] = (refs[i][...].astype(F32) + refs[n + i][...].astype(F32)).astype(BF)
-
-
-def add_split_kernel(l_ref, r_ref, a_ref, b_ref):
-    both = (l_ref[...].astype(F32) + r_ref[...].astype(F32)).astype(BF)
-    half = a_ref.shape[0]
-    a_ref[...] = both[:half]
-    b_ref[...] = both[half:]
-
-
-def up_kernel(code_ref, a_ref, ra_ref, b_ref, rb_ref, u_ref, out_ref, *, pool):
+    first = lax.broadcasted_iota(jnp.int32, (half, lanes), 1) < rank
+    top = jnp.where(first, acc[:half], acc[2 * half:3 * half]).astype(BF)
+    low = jnp.where(first, acc[half:2 * half], acc[3 * half:]).astype(BF)
+    core = core_ref[0]
+
+    @pl.when(core == 0)
+    def _():
+        keep_ref[...] = top
+        send_ref[...] = low
+
+    @pl.when(core != 0)
+    def _():
+        keep_ref[...] = low
+        send_ref[...] = top
+
+
+def add_kernel(l_ref, r_ref, out_ref):
+    out_ref[...] = (l_ref[...].astype(F32) + r_ref[...].astype(F32)).astype(BF)
+
+
+def up_kernel(core_ref, code_ref, mine_ref, other_ref, u_ref, out_ref, *, pool):
     i = pl.program_id(0)
-    rows, lanes = a_ref.shape
+    rows, lanes = mine_ref.shape
     rank = lanes // 2
-    even = lax.rem(i, 2) == 0
-    a = a_ref[...].astype(F32) + ra_ref[...].astype(F32)
-    b = b_ref[...].astype(F32) + rb_ref[...].astype(F32)
-    low = jnp.where(even, a, b).astype(BF).astype(F32)
+    own = lax.rem(i, 2) == core_ref[0]
+    low = jnp.where(own, mine_ref[...].astype(F32), other_ref[...].astype(F32))
     first = lax.broadcasted_iota(jnp.int32, low.shape, 1) < rank
-    mine = jnp.logical_xor(first, i >= 2)
-    low = jnp.where(mine, low, pltpu.roll(low, rank, 1))
+    low = jnp.where(jnp.logical_xor(first, i >= 2), low, pltpu.roll(low, rank, 1))
     code = code_ref[pl.ds(pl.multiple_of(i * rows, rows), rows), :]
     spread = jnp.concatenate(
         [jnp.where(code == 2 * k, low, 0.0).astype(BF) for k in range(pool // 2)], 1
@@ -185,7 +185,9 @@
         cost_estimate=cost(2 * slots * tokens * features, 2 * (slots + tokens) * features),
         name="pack",
     )(me1, req_len, req_id, pool_slot, x)
-    arrived = lax.all_to_all(outgoing.reshape(groups, most, features), "req", split_axis=0, concat_axis=0, tiled=True)
+    arrived = lax.all_to_all(
+        outgoing.reshape(groups, most, features), "req", split_axis=0, concat_axis=0, tiled=True
+    )
 
     x, _ = lax.optimization_barrier((x, outgoing))
 
@@ -253,43 +255,45 @@
         (arrived, code, up_maps, ka, sa, kb, sb)
     )
     code = near(code)
-    pair = pltpu.VMEM((slots // 4, 2 * rank), BF)
-    low = pl.pallas_call(
+    core = t1 & 1
+    piece = pltpu.VMEM((slots // 4, 2 * rank), BF)
+    low, send = pl.pallas_call(
         functools.partial(down_kernel, pool=pool),
-        out_shape=pltpu.VMEM((slots // 2, 2 * rank), BF),
-        in_specs=[VM, VM, VM],
-        out_specs=VM,
+        out_shape=[piece] * 2,
+        in_specs=[SM, VM, VM, VM],
+        out_specs=[VM] * 2,
         cost_estimate=cost(2 * slots * pool * rank * features, 2 * slots * features),
         name="down",
         compiler_params=SMALL,
     )(
+        core,
         code,
         near(arrived.reshape(slots, features)),
         near(jnp.swapaxes(down, 1, 2).reshape(pool * rank, features)),
     )
+    for m, out in ((1, send), (2, None), (6, None)):
+        other = lax.ppermute(low if out is None else out, "tensor", xor(m))
+        low = pl.pallas_call(
+            add_kernel,
+            out_shape=piece,
+            in_specs=[VM] * 2,
+            out_specs=VM,
+            name="add_low",
+            compiler_params=SMALL,
+        )(near(low), near(other))
     other = lax.ppermute(low, "tensor", xor(1))
-    la, lb = pl.pallas_call(
-        add_split_kernel, out_shape=[pair] * 2, in_specs=[VM] * 2, out_specs=[VM] * 2, name="add_core", compiler_params=SMALL
-    )(near(low), near(other))
-    oa = lax.ppermute(la, "tensor", xor(2))
-    ob = lax.ppermute(lb, "tensor", xor(6))
-    la, lb = pl.pallas_call(
-        add_kernel, out_shape=[pair] * 2, in_specs=[VM] * 4, out_specs=[VM] * 2, name="add_x", compiler_params=SMALL
-    )(near(la), near(lb), near(oa), near(ob))
-    oa = lax.ppermute(la, "tensor", xor(6))
-    ob = lax.ppermute(lb, "tensor", xor(2))
 
     step = slots // 4
     raised = pl.pallas_call(
         functools.partial(up_kernel, pool=pool),
         out_shape=pltpu.HBM((slots, cols), BF),
         grid=(4,),
-        in_specs=[VM] * 6,
+        in_specs=[SM] + [VM] * 4,
         out_specs=pl.BlockSpec((step, cols), lambda i: (i, 0)),
         cost_estimate=cost(2 * slots * pool * rank * cols, 2 * slots * cols),
         name="up",
         compiler_params=SMALL,
-    )(code, near(la), near(oa), near(lb), near(ob), near(up_maps))
+    )(core, code, near(low), near(other), near(up_maps))
     raised, sa, sb, me1 = lax.optimization_barrier((raised, sa, sb, me1))
     returned = lax.all_to_all(
         raised.reshape(groups, most, cols), "req", split_axis=0, concat_axis=0, tiled=True
@@ -332,7 +336,7 @@
         out_specs=tall,
         cost_estimate=cost(2 * tokens * slots * cols, 2 * cols * (slots + 4 * tokens)),
         name="final",
-        compiler_params=pltpu.CompilerParams(vmem_limit_bytes=60 * 2**20),
+        compiler_params=pltpu.CompilerParams(vmem_limit_bytes=59 * 2**20),
     )(near(sel), near(returned.reshape(slots, cols)), pre)
 
 
@@ -347,4 +351,6 @@
         P(),
         P("req", None),
     )
-    return jax.shard_map(one_block, mesh=mesh, in_specs=in_specs, out_specs=P("req", "tensor"), check_vma=False)
+    return jax.shard_map(
+        one_block, mesh=mesh, in_specs=in_specs, out_specs=P("req", "tensor"), check_vma=False
+    )

time: 132 us -> 127 us (0.962); the launches traced: 130 us -> 127 us
  waiting for transfers between devices: 59.7 us -> 66.4 us
  local copies, waits for them, and re-layouts: 5.28 us -> 0.18 us
  starting transfers between devices: 24.4 us -> 19.9 us
    unnamed x24 -> x14, local copies, waits for them, and re-layouts: 5.14 us -> 0.03 us
    ppermute x1, waiting for transfers between devices: 0.06 us -> 5 us  [one_block(): lax.ppermute((kb[1].astype(F32) + rb[1].astype(F32)).astype(BF), 'tensor'...]
    ppermute x1, waiting for transfers between devices: 21.7 us -> 25.9 us  [one_block(): rb = lax.ppermute(sb, 'tensor', xor(6))]
    all_to_all x1, waiting for transfers between devices: 4.87 us -> 1.65 us  [one_block(): lax.all_to_all(raised.reshape(groups, most, cols), 'req', split_axis=0, c...]
    ppermute x4 -> x3, starting transfers between devices: 3.28 us -> 1.58 us  [one_block(): other = lax.ppermute(low if out is None else out, 'tensor', xor(m))]
    ppermute x1, starting transfers between devices: 2.11 us -> 0.56 us  [one_block(): rb = lax.ppermute(sb, 'tensor', xor(6))]
    ppermute x4 -> x3, waiting for transfers between devices: 8.68 us -> 9.67 us  [one_block(): other = lax.ppermute(low if out is None else out, 'tensor', xor(m))]
  transfers between devices with their start and end apart: 12 -> 11, of which waited for: 9 -> 9; matrix products, arithmetic and copies ran while one was open for 3% -> 4% of each run, Pallas kernels for 14% -> 14%
where the time goes in v3:
time: 127 us
  waiting for transfers between devices  66.4 us (52%)
  Pallas kernels  35.7 us (28%)
  starting transfers between devices  19.9 us (16%)
  other arithmetic  4.32 us (3%)
    ppermute x1, waiting for transfers between devices, one_block(): rb = lax.ppermute(sb, 'tensor', xor(6))  25.9 us
    all_to_all x1, waiting for transfers between devices, one_block(): lax.all_to_all(outgoing.reshape(groups, most, features), 'req', split_axi...  19.8 us
    all_to_all x1, starting transfers between devices, one_block(): lax.all_to_all(outgoing.reshape(groups, most, features), 'req', split_axi...  11.5 us
    ppermute x3, waiting for transfers between devices, one_block(): other = lax.ppermute(low if out is None else out, 'tensor', xor(m))  9.67 us
    pallas_call x1, Pallas kernels, one_block(): pl.pallas_call(own_dot_kernel, out_shape=[piece] * 4, grid_spec=pltpu.Pre...  8 us
    pallas_call x1, Pallas kernels, one_block(): pl.pallas_call(pair_dot_kernel, out_shape=sds((k, tokens, cols), BF), gri...  6.36 us
    pallas_call x1, Pallas kernels, one_block(): pl.pallas_call(functools.partial(unpack_matrix_kernel, pool=pool, most=mo...  5.52 us
    all_to_all x1, starting transfers between devices, one_block(): lax.all_to_all(raised.reshape(groups, most, cols), 'req', split_axis=0, c...  5.31 us
  transfers between devices with their start and end apart: 11, of which 9 were waited for; matrix products, arithmetic and copies ran while one was open for 4% of the time, Pallas kernels for 14%

profile of v3, /device:TPU:6, one launch (start us, length us, event | category | flops | bytes accessed | tf_op | source)
XLA Modules:
  0.0 126.7 jit_solution(7629836813095642471)
XLA Ops:
  0.0 2.9 %pack.1 = bf16[1024,512]{1,0:T(8,128)(2,1)} custom-call(s32[1]{0:T(128)} %bitcast.1.me_ref, s32[1,32]{1,0:T(1,128)} %len_ref.3, s32[32,32]{1,0:T(8,128)} %id_ref.3, s32[256]{0:T(256)} %slot_ref.3, bf16[512,512]{1,0:T(8,128)(2,1)} %x_ref.3), custom_call_target="tpu_custom_call" | custom-call | flops 536870912 | bytes 1572864 | tf_op jit(solution)/shard_map/pack/pallas_call | solution.py:179
  2.9 6.4 %pair_dot.1 = bf16[4,512,1024]{2,1,0:T(8,128)(2,1)} custom-call(s32[1]{0:T(128)} %bitcast.t_ref, bf16[512,512]{1,0:T(8,128)(2,1)} %x_ref.3, bf16[512,8192]{1,0:T(8,128)(2,1)} %w_ref.3), custom_call_target="tpu_custom_call" | custom-call | flops 2147483648 | bytes 8388608 | tf_op jit(solution)/shard_map/pair_dot/pallas_call | solution.py:199
  9.3 11.5 %all-to-all-start = ((bf16[32,32,512]{2,1,0:T(8,128)(2,1)}), bf16[32,32,512]{2,1,0:T(8,128)(2,1)S(1)}, u32[]{:S(2)}, u32[]{:S(2)}) async-start(bf16[32,32,512]{2,1,0:T(8,128)(2,1)} %bitcast.2), calls=%async_computation | async-start | bytes 2097152 | tf_op jit(solution)/shard_map/all_to_all | solution.py:188
  20.8 0.2 select_reduce_fusion.1
  21.0 0.7 select_reduce_fusion
  21.9 0.1 fetch_up.1.u_ref
  22.0 0.2 broadcast_subtract_fusion.code_ref
  22.2 8.0 %own_dot.1 = (bf16[2,256,1024]{2,1,0:T(8,128)(2,1)}, bf16[2,256,1024]{2,1,0:T(8,128)(2,1)}, bf16[2,256,1024]{2,1,0:T(8,128)(2,1)}, bf16[2,256,1024]{2,1,0:T(8,128)(2,1)}) custom-call(s32[1]{0:T(128)} %bitcast.t_ref, bf16[512,512]{1,0:T(8,128)(2,1)} %x_ref.3, bf16[512,8192]{1,0:T(8,128)(2,1)} %w_ref.3, bf16[4,512,1024]{2,1,0:T(8,128)(2,1)} %collective-permute-done.p_ref), custom_call_target="tpu_custom_call" | custom-call | flops 2147483648 | bytes 12582912 | tf_op jit(solution)/shard_map/own_dot/pallas_call | solution.py:218
  30.2 19.8 %all-to-all-done = bf16[32,32,512]{2,1,0:T(8,128)(2,1)S(1)} async-done(((bf16[32,32,512]{2,1,0:T(8,128)(2,1)}), bf16[32,32,512]{2,1,0:T(8,128)(2,1)S(1)}, u32[]{:S(2)}, u32[]{:S(2)}) %all-to-all-start) | async-done | bytes 1048608 | tf_op jit(solution)/shard_map/all_to_all | solution.py:188
  50.0 0.8 down.1
  50.8 0.1 collective-permute-start.1
  50.9 1.2 collective-permute-done.1.r_ref
  52.2 0.9 collective-permute-start.2
  53.1 3.4 %collective-permute-done.2.r_ref = bf16[256,128]{1,0:T(8,128)(2,1)S(1)} collective-permute-done((bf16[256,128]{1,0:T(8,128)(2,1)S(1)}, bf16[256,128]{1,0:T(8,128)(2,1)S(1)}, u32[]{:S(2)}, u32[]{:S(2)}) %collective-permute-start.2) | collective-permute-done | bytes 65568 | tf_op jit(solution)/shard_map/ppermute | solution.py:275
  56.5 0.6 collective-permute-start.3
  57.1 5.0 %collective-permute-done.3.r_ref = bf16[256,128]{1,0:T(8,128)(2,1)S(1)} collective-permute-done((bf16[256,128]{1,0:T(8,128)(2,1)S(1)}, bf16[256,128]{1,0:T(8,128)(2,1)S(1)}, u32[]{:S(2)}, u32[]{:S(2)}) %collective-permute-start.3) | collective-permute-done | bytes 65568 | tf_op jit(solution)/shard_map/ppermute | solution.py:275
  62.1 0.1 collective-permute-start.4
  62.2 1.2 collective-permute-done.4.other_ref
  63.5 3.1 %up.1 = bf16[1024,1024]{1,0:T(8,128)(2,1)} custom-call(s32[1]{0:T(128)S(6)} %and.5.core_ref, s32[1024,128]{1,0:T(8,128)S(1)} %broadcast_subtract_fusion.code_ref, bf16[256,128]{1,0:T(8,128)(2,1)S(1)} %add_low.5.mine_ref, bf16[256,128]{1,0:T(8,128)(2,1)S(1)} %collective-permute-done.4.other_ref, bf16[512,1024]{1,0:T(8,128)(2,1)S(1)} %fetch_up.1.u_ref), custom_call_target="tpu_custom_call" | custom-call | flops 1073741824 | bytes 2097152 | tf_op jit(solution)/shard_map/up/pallas_call | solution.py:287
  66.6 5.3 %all-to-all-start.1 = ((bf16[32,32,1024]{2,1,0:T(8,128)(2,1)}), bf16[32,32,1024]{2,1,0:T(8,128)(2,1)S(1)}, u32[]{:S(2)}, u32[]{:S(2)}) async-start(bf16[32,32,1024]{2,1,0:T(8,128)(2,1)} %bitcast.18), calls=%async_computation.1 | async-start | bytes 4194304 | tf_op jit(solution)/shard_map/all_to_all | solution.py:298
  71.9 0.6 collective-permute-start.7
  72.4 25.9 %collective-permute-done.7.rb_ref = bf16[2,256,1024]{2,1,0:T(8,128)(2,1)S(1)} collective-permute-done((bf16[2,256,1024]{2,1,0:T(8,128)(2,1)}, bf16[2,256,1024]{2,1,0:T(8,128)(2,1)S(1)}, u32[]{:S(2)}, u32[]{:S(2)}) %collective-permute-start.7) | collective-permute-done | bytes 1048608 | tf_op jit(solution)/shard_map/ppermute | solution.py:313
  98.3 1.6 %fusion.1 = bf16[256,1024]{1,0:T(8,128)(2,1)S(1)} fusion(bf16[2,256,1024]{2,1,0:T(8,128)(2,1)S(1)} %collective-permute-done.7.rb_ref, bf16[2,256,1024]{2,1,0:T(8,128)(2,1)} %get-tuple-element.41.kb_ref), kind=kLoop, calls=%fused_computation.3 | loop fusion | flops 1048576 | bytes 1572864 | tf_op jit(solution)/shard_map/convert_element_type | solution.py:315
  99.9 0.1 collective-permute-start.8
  100.1 1.6 %fusion = bf16[256,1024]{1,0:T(8,128)(2,1)S(1)} fusion(bf16[2,256,1024]{2,1,0:T(8,128)(2,1)S(1)} %collective-permute-done.5.ra_ref, bf16[2,256,1024]{2,1,0:T(8,128)(2,1)} %get-tuple-element.39.ka_ref), kind=kLoop, calls=%fused_computation.2 | loop fusion | flops 1048576 | bytes 1572864 | tf_op jit(solution)/shard_map/convert_element_type | solution.py:314
  101.7 0.7 collective-permute-start.6
  102.4 5.5 %unpack_matrix.1.sel_ref = bf16[512,1024]{1,0:T(8,128)(2,1)S(1)} custom-call(s32[1]{0:T(128)} %bitcast.1.me_ref, s32[1,32]{1,0:T(1,128)S(1)} %copy-done.4, s32[32,32]{1,0:T(8,128)S(1)} %copy-done.2, s32[256]{0:T(256)S(1)} %copy-done.3), custom_call_target="tpu_custom_call" | custom-call | flops 4194304 | bytes 1048576 | tf_op jit(solution)/shard_map/unpack_matrix/pallas_call | solution.py:302
  108.0 5.0 %collective-permute-done.8.zb_ref = bf16[256,1024]{1,0:T(8,128)(2,1)} collective-permute-done((bf16[256,1024]{1,0:T(8,128)(2,1)S(1)}, bf16[256,1024]{1,0:T(8,128)(2,1)}, u32[]{:S(2)}, u32[]{:S(2)}) %collective-permute-start.8) | collective-permute-done | bytes 524320 | tf_op jit(solution)/shard_map/ppermute | solution.py:315
  113.0 3.2 %collective-permute-done.6.za_ref = bf16[256,1024]{1,0:T(8,128)(2,1)} collective-permute-done((bf16[256,1024]{1,0:T(8,128)(2,1)S(1)}, bf16[256,1024]{1,0:T(8,128)(2,1)}, u32[]{:S(2)}, u32[]{:S(2)}) %collective-permute-start.6) | collective-permute-done | bytes 524320 | tf_op jit(solution)/shard_map/ppermute | solution.py:314
  116.1 4.5 %before.1.pre_ref = f32[512,1024]{1,0:T(8,128)} custom-call(bf16[512,1024]{1,0:T(8,128)(2,1)} %res_ref.1, bf16[2,256,1024]{2,1,0:T(8,128)(2,1)} %get-tuple-element.39.ka_ref, bf16[2,256,1024]{2,1,0:T(8,128)(2,1)} %copy-done.6, bf16[256,1024]{1,0:T(8,128)(2,1)} %collective-permute-done.6.za_ref, bf16[2,256,1024]{2,1,0:T(8,128)(2,1)} %get-tuple-element.41.kb_ref, ...), custom_call_target="tpu_custom_call" | custom-call | flops 2097152 | bytes 6291456 | tf_op jit(solution)/shard_map/before/pallas_call | solution.py:321
  120.6 1.6 %all-to-all-done.1 = bf16[32,32,1024]{2,1,0:T(8,128)(2,1)S(1)} async-done(((bf16[32,32,1024]{2,1,0:T(8,128)(2,1)}), bf16[32,32,1024]{2,1,0:T(8,128)(2,1)S(1)}, u32[]{:S(2)}, u32[]{:S(2)}) %all-to-all-start.1) | async-done | bytes 2097184 | tf_op jit(solution)/shard_map/all_to_all | solution.py:298
  122.3 4.4 %final.1 = bf16[512,1024]{1,0:T(8,128)(2,1)} custom-call(bf16[512,1024]{1,0:T(8,128)(2,1)S(1)} %unpack_matrix.1.sel_ref, bf16[1024,1024]{1,0:T(8,128)(2,1)S(1)} %bitcast.14, f32[512,1024]{1,0:T(8,128)} %before.1.pre_ref), custom_call_target="tpu_custom_call" | custom-call | flops 1073741824 | bytes 6291456 | tf_op jit(solution)/shard_map/final/pallas_call | solution.py:331
  (25 shorter events, 0.3 us)
Async XLA Ops:
  2.9 17.9 %copy-start.3 = (s32[256]{0:T(256)S(1)}, s32[256]{0:T(256)}, u32[]{:S(2)}) copy-start(s32[256]{0:T(256)} %slot_ref.3) | copy-start | bytes 3076
  2.9 18.1 %copy-start.2 = (s32[32,32]{1,0:T(8,128)S(1)}, s32[32,32]{1,0:T(8,128)}, u32[]{:S(2)}) copy-start(s32[32,32]{1,0:T(8,128)} %id_ref.3) | copy-start | bytes 12292
  2.9 18.9 %copy-start = (bf16[8,64,1024]{2,1,0:T(8,128)(2,1)S(1)}, bf16[8,64,1024]{2,1,0:T(8,128)(2,1)}, u32[]{:S(2)}) copy-start(bf16[8,64,1024]{2,1,0:T(8,128)(2,1)} %param.12) | copy-start | bytes 3145732
  9.3 12.9 %collective-permute-start = (bf16[4,512,1024]{2,1,0:T(8,128)(2,1)}, bf16[4,512,1024]{2,1,0:T(8,128)(2,1)}, u32[]{:S(2)}, u32[]{:S(2)}) collective-permute-start(bf16[4,512,1024]{2,1,0:T(8,128)(2,1)} %pair_dot.1), channel_id=1, source_target_pairs={{0,32},{32,0},{64,96},{96,64},{128,160},{160,128},{192,224},{224,1... | collective-permute-start | bytes 12582920 | tf_op jit(solution)/shard_map/ppermute | solution.py:214
  9.3 40.7 %all-to-all-start = ((bf16[32,32,512]{2,1,0:T(8,128)(2,1)}), bf16[32,32,512]{2,1,0:T(8,128)(2,1)S(1)}, u32[]{:S(2)}, u32[]{:S(2)}) async-start(bf16[32,32,512]{2,1,0:T(8,128)(2,1)} %bitcast.2), calls=%async_computation | async-start | bytes 2097152 | tf_op jit(solution)/shard_map/all_to_all | solution.py:188
  22.2 27.8 %copy-start.1 = (bf16[8,512,64]{1,2,0:T(8,128)(2,1)S(1)}, bf16[8,512,64]{1,2,0:T(8,128)(2,1)}, u32[]{:S(2)}) copy-start(bf16[8,512,64]{1,2,0:T(8,128)(2,1)} %param.11) | copy-start | bytes 1572868
  50.8 1.3 %collective-permute-start.1 = (bf16[256,128]{1,0:T(8,128)(2,1)S(1)}, bf16[256,128]{1,0:T(8,128)(2,1)S(1)}, u32[]{:S(2)}, u32[]{:S(2)}) collective-permute-start(bf16[256,128]{1,0:T(8,128)(2,1)S(1)} %get-tuple-element.34), channel_id=1, source_target_pairs={{0,32},{32,0},{64,96},{96,64},{128,160},{160,128},{192,224},{224,1... | collective-permute-start | bytes 196616 | tf_op jit(solution)/shard_map/ppermute | solution.py:275
  52.2 4.4 %collective-permute-start.2 = (bf16[256,128]{1,0:T(8,128)(2,1)S(1)}, bf16[256,128]{1,0:T(8,128)(2,1)S(1)}, u32[]{:S(2)}, u32[]{:S(2)}) collective-permute-start(bf16[256,128]{1,0:T(8,128)(2,1)S(1)} %add_low.3.l_ref), channel_id=1, source_target_pairs={{0,64},{32,96},{64,0},{96,32},{128,192},{160,224},{192,128},{224,1... | collective-permute-start | bytes 196616 | tf_op jit(solution)/shard_map/ppermute | solution.py:275
  56.5 5.6 %collective-permute-start.3 = (bf16[256,128]{1,0:T(8,128)(2,1)S(1)}, bf16[256,128]{1,0:T(8,128)(2,1)S(1)}, u32[]{:S(2)}, u32[]{:S(2)}) collective-permute-start(bf16[256,128]{1,0:T(8,128)(2,1)S(1)} %add_low.4.l_ref), channel_id=1, source_target_pairs={{0,192},{32,224},{64,128},{96,160},{128,64},{160,96},{192,0},{224,... | collective-permute-start | bytes 196616 | tf_op jit(solution)/shard_map/ppermute | solution.py:275
  62.1 1.3 %collective-permute-start.4 = (bf16[256,128]{1,0:T(8,128)(2,1)S(1)}, bf16[256,128]{1,0:T(8,128)(2,1)S(1)}, u32[]{:S(2)}, u32[]{:S(2)}) collective-permute-start(bf16[256,128]{1,0:T(8,128)(2,1)S(1)} %add_low.5.mine_ref), channel_id=1, source_target_pairs={{0,32},{32,0},{64,96},{96,64},{128,160},{160,128},{192,224},{224,1... | collective-permute-start | bytes 196616 | tf_op jit(solution)/shard_map/ppermute | solution.py:284
  66.6 35.9 %copy-start.4 = (s32[1,32]{1,0:T(1,128)S(1)}, s32[1,32]{1,0:T(1,128)}, u32[]{:S(2)}) copy-start(s32[1,32]{1,0:T(1,128)} %len_ref.3) | copy-start | bytes 388
  66.6 55.7 %all-to-all-start.1 = ((bf16[32,32,1024]{2,1,0:T(8,128)(2,1)}), bf16[32,32,1024]{2,1,0:T(8,128)(2,1)S(1)}, u32[]{:S(2)}, u32[]{:S(2)}) async-start(bf16[32,32,1024]{2,1,0:T(8,128)(2,1)} %bitcast.18), calls=%async_computation.1 | async-start | bytes 4194304 | tf_op jit(solution)/shard_map/all_to_all | solution.py:298
  71.9 26.5 %collective-permute-start.7 = (bf16[2,256,1024]{2,1,0:T(8,128)(2,1)}, bf16[2,256,1024]{2,1,0:T(8,128)(2,1)S(1)}, u32[]{:S(2)}, u32[]{:S(2)}) collective-permute-start(bf16[2,256,1024]{2,1,0:T(8,128)(2,1)} %get-tuple-element.42), channel_id=1, source_target_pairs={{0,192},{32,224},{64,128},{96,160},{128,64},{160,96},{192,0},{224,... | collective-permute-start | bytes 3145736 | tf_op jit(solution)/shard_map/ppermute | solution.py:313
  72.4 27.6 %collective-permute-start.5 = (bf16[2,256,1024]{2,1,0:T(8,128)(2,1)}, bf16[2,256,1024]{2,1,0:T(8,128)(2,1)S(1)}, u32[]{:S(2)}, u32[]{:S(2)}) collective-permute-start(bf16[2,256,1024]{2,1,0:T(8,128)(2,1)} %get-tuple-element.40), channel_id=1, source_target_pairs={{0,64},{32,96},{64,0},{96,32},{128,192},{160,224},{192,128},{224,1... | collective-permute-start | bytes 3145736 | tf_op jit(solution)/shard_map/ppermute | solution.py:312
  98.3 3.3 %copy-start.5 = (bf16[2,256,1024]{2,1,0:T(8,128)(2,1)}, bf16[2,256,1024]{2,1,0:T(8,128)(2,1)S(1)}, u32[]{:S(2)}) copy-start(bf16[2,256,1024]{2,1,0:T(8,128)(2,1)S(1)} %collective-permute-done.7.rb_ref) | copy-start | bytes 3145732
  99.9 13.0 %collective-permute-start.8 = (bf16[256,1024]{1,0:T(8,128)(2,1)S(1)}, bf16[256,1024]{1,0:T(8,128)(2,1)}, u32[]{:S(2)}, u32[]{:S(2)}) collective-permute-start(bf16[256,1024]{1,0:T(8,128)(2,1)S(1)} %fusion.1), channel_id=1, source_target_pairs={{0,64},{32,96},{64,0},{96,32},{128,192},{160,224},{192,128},{224,1... | collective-permute-start | bytes 1572872 | tf_op jit(solution)/shard_map/ppermute | solution.py:315
  100.0 1.6 %copy-start.6 = (bf16[2,256,1024]{2,1,0:T(8,128)(2,1)}, bf16[2,256,1024]{2,1,0:T(8,128)(2,1)S(1)}, u32[]{:S(2)}) copy-start(bf16[2,256,1024]{2,1,0:T(8,128)(2,1)S(1)} %collective-permute-done.5.ra_ref) | copy-start | bytes 3145732
  101.7 14.4 %collective-permute-start.6 = (bf16[256,1024]{1,0:T(8,128)(2,1)S(1)}, bf16[256,1024]{1,0:T(8,128)(2,1)}, u32[]{:S(2)}, u32[]{:S(2)}) collective-permute-start(bf16[256,1024]{1,0:T(8,128)(2,1)S(1)} %fusion), channel_id=1, source_target_pairs={{0,192},{32,224},{64,128},{96,160},{128,64},{160,96},{192,0},{224,... | collective-permute-start | bytes 1572872 | tf_op jit(solution)/shard_map/ppermute | solution.py:314

commit v4 on v3

--- a/solution.py
+++ b/solution.py
@@ -30,11 +30,9 @@
     start = jnp.int32(0)
     for r in range(requests):
         owner = lax.div(slot_ref[id_ref[me, r]], jnp.int32(pool))
-        count = len_ref[0, r]
-        hit = (ahead == start) & (rows < count)
         at = pl.multiple_of(owner * most, most)
-        sel_ref[pl.ds(at, most), :] = jnp.where(hit, 1.0, 0.0).astype(BF)
-        start = start + count
+        sel_ref[pl.ds(at, most), :] = jnp.where(ahead == start, 1.0, 0.0).astype(BF)
+        start = start + len_ref[0, r]
     out_ref[...] = jnp.dot(sel_ref[...], x_ref[...], preferred_element_type=F32).astype(BF)
 
 
@@ -85,10 +83,6 @@
         send_ref[...] = top
 
 
-def add_kernel(l_ref, r_ref, out_ref):
-    out_ref[...] = (l_ref[...].astype(F32) + r_ref[...].astype(F32)).astype(BF)
-
-
 def up_kernel(core_ref, code_ref, mine_ref, other_ref, u_ref, out_ref, *, pool):
     i = pl.program_id(0)
     rows, lanes = mine_ref.shape
@@ -108,46 +102,42 @@
     out_ref[0] = jnp.dot(x_ref[...], w_ref[...], preferred_element_type=F32).astype(BF)
 
 
-def own_dot_kernel(t_ref, x_ref, w_ref, p_ref, ka_ref, sa_ref, kb_ref, sb_ref):
+def own_dot_kernel(t_ref, x_ref, w_ref, p_ref, a0_ref, b0_ref, a1_ref, b1_ref):
     half = x_ref.shape[0] // 2
     both = (jnp.dot(x_ref[...], w_ref[...], preferred_element_type=F32) + p_ref[0].astype(F32)).astype(BF)
-    top, low = both[:half], both[half:]
     j = pl.program_id(0)
 
     @pl.when(j == 0)
     def _():
-        ka_ref[0] = top
-        kb_ref[0] = low
+        a0_ref[...] = both[:half]
+        b0_ref[...] = both[half:]
 
     @pl.when(j == 1)
     def _():
-        sa_ref[0] = top
-        kb_ref[1] = low
-
-    @pl.when(j == 2)
-    def _():
-        ka_ref[1] = top
-        sb_ref[0] = low
-
-    @pl.when(j == 3)
-    def _():
-        sa_ref[1] = top
-        sb_ref[1] = low
-
-
-def before_kernel(res_ref, ka_ref, ra_ref, za_ref, kb_ref, rb_ref, zb_ref, out_ref):
+        a1_ref[...] = both[:half]
+        b1_ref[...] = both[half:]
+
+
+def before_kernel(res_ref, ka_ref, ra_ref, kb_ref, rb_ref, out_ref):
     half = res_ref.shape[0] // 2
-    base_a = ka_ref[0].astype(F32) + ra_ref[0].astype(F32) + za_ref[...].astype(F32)
-    base_b = kb_ref[0].astype(F32) + rb_ref[0].astype(F32) + zb_ref[...].astype(F32)
-    out_ref[:half] = res_ref[:half].astype(F32) + base_a
-    out_ref[half:] = res_ref[half:].astype(F32) + base_b
-
-
-def final_kernel(sel_ref, ret_ref, pre_ref, out_ref):
+    out_ref[:half] = res_ref[:half].astype(F32) + (ka_ref[...].astype(F32) + ra_ref[...].astype(F32))
+    out_ref[half:] = res_ref[half:].astype(F32) + (kb_ref[...].astype(F32) + rb_ref[...].astype(F32))
+
+
+def final_kernel(sel_ref, ret_ref, pre_ref, za_ref, zb_ref, out_ref):
     wide = out_ref.shape[1]
+    half = za_ref.shape[0]
     at = pl.ds(pl.multiple_of(pl.program_id(0) * wide, wide), wide)
-    delta = jnp.dot(sel_ref[...], ret_ref[:, at], preferred_element_type=F32)
-    out_ref[...] = (pre_ref[...] + delta).astype(BF)
+    delta = jnp.dot(sel_ref[...], ret_ref[:, at], preferred_element_type=F32) + pre_ref[...]
+    out_ref[:half] = (delta[:half] + za_ref[...].astype(F32)).astype(BF)
+    out_ref[half:] = (delta[half:] + zb_ref[...].astype(F32)).astype(BF)
+
+
+def sum_kernel(*refs):
+    acc = refs[0][...].astype(F32)
+    for r in refs[1:-1]:
+        acc = acc + r[...].astype(F32)
+    refs[-1][...] = acc.astype(BF)
 
 
 def copy_kernel(x_ref, out_ref):
@@ -185,52 +175,62 @@
         cost_estimate=cost(2 * slots * tokens * features, 2 * (slots + tokens) * features),
         name="pack",
     )(me1, req_len, req_id, pool_slot, x)
-    arrived = lax.all_to_all(
-        outgoing.reshape(groups, most, features), "req", split_axis=0, concat_axis=0, tiled=True
-    )
+    arrived = lax.all_to_all(outgoing.reshape(groups, most, features), "req", split_axis=0, concat_axis=0, tiled=True)
+
+    def parts(offsets, x):
+        def order(j):
+            return jnp.where(j == 0, offsets[0], offsets[1])
+
+        n = len(offsets)
+        flops = 2 * tokens * features * cols * n
+        whole = pl.BlockSpec((tokens, features), lambda j, t_ref: (0, 0))
+        out = pl.pallas_call(
+            pair_dot_kernel,
+            out_shape=sds((n, tokens, cols), BF),
+            grid_spec=pltpu.PrefetchScalarGridSpec(
+                num_scalar_prefetch=1,
+                grid=(n,),
+                in_specs=[whole, pl.BlockSpec((features, cols), lambda j, t_ref: (0, t_ref[0] ^ 1 ^ (2 * order(j))))],
+                out_specs=pl.BlockSpec((1, tokens, cols), lambda j, t_ref: (j, 0, 0)),
+            ),
+            cost_estimate=cost(flops, 2 * n * cols * (tokens + features)),
+            name="pair_dot",
+        )(t1, x, weight)
+
+        def own(x, came):
+            piece = sds((half, cols), BF)
+            keep = pl.BlockSpec((half, cols), lambda j, t_ref: (0, 0))
+            return pl.pallas_call(
+                own_dot_kernel,
+                out_shape=[piece] * 4,
+                grid_spec=pltpu.PrefetchScalarGridSpec(
+                    num_scalar_prefetch=1,
+                    grid=(n,),
+                    in_specs=[
+                        whole,
+                        pl.BlockSpec((features, cols), lambda j, t_ref: (0, t_ref[0] ^ (2 * order(j)))),
+                        pl.BlockSpec((1, tokens, cols), lambda j, t_ref: (j, 0, 0)),
+                    ],
+                    out_specs=[keep] * 4,
+                ),
+                cost_estimate=cost(flops, 2 * n * cols * (2 * tokens + features)),
+                name="own_dot",
+            )(t1, x, weight, came)
+
+        return out, own
 
     x, _ = lax.optimization_barrier((x, outgoing))
-
-    def blocks(j):
-        return j ^ (j >> 1)
-
-    k = n_t // 2
-    wide = 2 * tokens * features * cols * k
-    to_pair = pl.pallas_call(
-        pair_dot_kernel,
-        out_shape=sds((k, tokens, cols), BF),
-        grid_spec=pltpu.PrefetchScalarGridSpec(
-            num_scalar_prefetch=1,
-            grid=(k,),
-            in_specs=[
-                pl.BlockSpec((tokens, features), lambda j, t_ref: (0, 0)),
-                pl.BlockSpec((features, cols), lambda j, t_ref: (0, t_ref[0] ^ 1 ^ (2 * blocks(j)))),
-            ],
-            out_specs=pl.BlockSpec((1, tokens, cols), lambda j, t_ref: (j, 0, 0)),
-        ),
-        cost_estimate=cost(wide, 2 * k * cols * (tokens + features)),
-        name="pair_dot",
-    )(t1, x, weight)
-    from_pair = lax.ppermute(to_pair, "tensor", xor(1))
-
-    piece = sds((2, half, cols), BF)
-    keep = pl.BlockSpec((2, half, cols), lambda j, t_ref: (0, 0, 0))
-    ka, sa, kb, sb = pl.pallas_call(
-        own_dot_kernel,
-        out_shape=[piece] * 4,
-        grid_spec=pltpu.PrefetchScalarGridSpec(
-            num_scalar_prefetch=1,
-            grid=(k,),
-            in_specs=[
-                pl.BlockSpec((tokens, features), lambda j, t_ref: (0, 0)),
-                pl.BlockSpec((features, cols), lambda j, t_ref: (0, t_ref[0] ^ (2 * blocks(j)))),
-                pl.BlockSpec((1, tokens, cols), lambda j, t_ref: (j, 0, 0)),
-            ],
-            out_specs=[keep] * 4,
-        ),
-        cost_estimate=cost(wide, 2 * k * cols * (2 * tokens + features)),
-        name="own_dot",
-    )(t1, x, weight, from_pair)
+    to_1, own_1 = parts((2, 1), x)
+    from_1 = lax.ppermute(to_1, "tensor", xor(1))
+    x, _ = lax.optimization_barrier((x, to_1))
+    to_2, own_2 = parts((3, 0), x)
+    from_2 = lax.ppermute(to_2, "tensor", xor(1))
+    x, _ = lax.optimization_barrier((x, to_2))
+    s2a, s2b, s1a, k1b = own_1(x, from_1)
+    r2a = lax.ppermute(s2a, "tensor", xor(2))
+    r2b = lax.ppermute(s2b, "tensor", xor(6))
+    x, _ = lax.optimization_barrier((x, s2a))
+    k3a, s3b, k0a, k0b = own_2(x, from_2)
 
     ids = jnp.arange(pool_slot.shape[0], dtype=jnp.int32)
     held = me * pool + jnp.arange(pool, dtype=jnp.int32)
@@ -251,9 +251,7 @@
         compiler_params=SMALL,
     )(up.reshape(pool * rank, cols))
 
-    arrived, code, up_maps, ka, sa, kb, sb = lax.optimization_barrier(
-        (arrived, code, up_maps, ka, sa, kb, sb)
-    )
+    arrived, code, up_maps, k0a, s3b = lax.optimization_barrier((arrived, code, up_maps, k0a, s3b))
     code = near(code)
     core = t1 & 1
     piece = pltpu.VMEM((slots // 4, 2 * rank), BF)
@@ -271,16 +269,19 @@
         near(arrived.reshape(slots, features)),
         near(jnp.swapaxes(down, 1, 2).reshape(pool * rank, features)),
     )
-    for m, out in ((1, send), (2, None), (6, None)):
-        other = lax.ppermute(low if out is None else out, "tensor", xor(m))
-        low = pl.pallas_call(
-            add_kernel,
+
+    def total(*terms):
+        return pl.pallas_call(
+            sum_kernel,
             out_shape=piece,
-            in_specs=[VM] * 2,
+            in_specs=[VM] * len(terms),
             out_specs=VM,
-            name="add_low",
+            name="sum_low",
             compiler_params=SMALL,
-        )(near(low), near(other))
+        )(*[near(v) for v in terms])
+
+    low = total(low, lax.ppermute(send, "tensor", xor(1)))
+    low = total(low, *[lax.ppermute(low, "tensor", xor(m)) for m in (4, 2, 6)])
     other = lax.ppermute(low, "tensor", xor(1))
 
     step = slots // 4
@@ -294,7 +295,7 @@
         name="up",
         compiler_params=SMALL,
     )(core, code, near(low), near(other), near(up_maps))
-    raised, sa, sb, me1 = lax.optimization_barrier((raised, sa, sb, me1))
+    raised, s1a, s3b, k3a, k1b, me1 = lax.optimization_barrier((raised, s1a, s3b, k3a, k1b, me1))
     returned = lax.all_to_all(
         raised.reshape(groups, most, cols), "req", split_axis=0, concat_axis=0, tiled=True
     )
@@ -309,35 +310,34 @@
     compiler_params=SMALL,
     )(me1, req_len, req_id, pool_slot)
 
-    ra = lax.ppermute(sa, "tensor", xor(2))
-    rb = lax.ppermute(sb, "tensor", xor(6))
-    za = lax.ppermute((ka[1].astype(F32) + ra[1].astype(F32)).astype(BF), "tensor", xor(6))
-    zb = lax.ppermute((kb[1].astype(F32) + rb[1].astype(F32)).astype(BF), "tensor", xor(2))
+    za = lax.ppermute((k3a.astype(F32) + r2a.astype(F32)).astype(BF), "tensor", xor(6))
+    zb = lax.ppermute((k1b.astype(F32) + r2b.astype(F32)).astype(BF), "tensor", xor(2))
+    r1a = lax.ppermute(s1a, "tensor", xor(2))
+    r3b = lax.ppermute(s3b, "tensor", xor(6))
 
     wide = cols // 4
-    lead = pl.BlockSpec((1, half, wide), lambda i: (0, 0, i))
     flat = pl.BlockSpec((half, wide), lambda i: (0, i))
     tall = pl.BlockSpec((tokens, wide), lambda i: (0, i))
     pre = pl.pallas_call(
         before_kernel,
         out_shape=pltpu.HBM((tokens, cols), F32),
         grid=(4,),
-        in_specs=[tall, lead, lead, flat, lead, lead, flat],
+        in_specs=[tall, flat, flat, flat, flat],
         out_specs=tall,
         cost_estimate=cost(4 * tokens * cols, 12 * tokens * cols),
         name="before",
-    )(residual, ka, ra, za, kb, rb, zb)
-    returned, pre, sel = lax.optimization_barrier((returned, pre, sel))
+    )(residual, k0a, r1a, k0b, r3b)
+    returned, pre, sel, za, zb = lax.optimization_barrier((returned, pre, sel, za, zb))
     return pl.pallas_call(
         final_kernel,
         out_shape=sds((tokens, cols), BF),
         grid=(4,),
-        in_specs=[VM, VM, tall],
+        in_specs=[VM, VM, tall, flat, flat],
         out_specs=tall,
         cost_estimate=cost(2 * tokens * slots * cols, 2 * cols * (slots + 4 * tokens)),
         name="final",
         compiler_params=pltpu.CompilerParams(vmem_limit_bytes=59 * 2**20),
-    )(near(sel), near(returned.reshape(slots, cols)), pre)
+    )(near(sel), near(returned.reshape(slots, cols)), pre, za, zb)
 
 
 def solution(mesh):
@@ -351,6 +351,4 @@
         P(),
         P("req", None),
     )
-    return jax.shard_map(
-        one_block, mesh=mesh, in_specs=in_specs, out_specs=P("req", "tensor"), check_vma=False
-    )
+    return jax.shard_map(one_block, mesh=mesh, in_specs=in_specs, out_specs=P("req", "tensor"), check_vma=False)

time: 127 us -> 128 us (level); the launches traced: 127 us -> 126 us
  waiting for transfers between devices: 66.4 us -> 54.5 us
  starting transfers between devices: 19.9 us -> 29.3 us
  Pallas kernels: 35.7 us -> 38.5 us
    ppermute x8 -> x12, waiting for transfers between devices: 43.7 us -> 23.6 us  [the longest x1 11 us: one_block(): r2b = lax.ppermute(s2b, 'tensor', xor(6))]
    all_to_all x1, waiting for transfers between devices: 1.65 us -> 11.7 us  [one_block(): lax.all_to_all(raised.reshape(groups, most, cols), 'req', split_axis=0, c...]
    ppermute x8 -> x12, starting transfers between devices: 2.99 us -> 12.5 us  [the longest x3 4.18 us: one_block(): low = total(low, *[lax.ppermute(low, 'tensor', xor(m)) for m in (4, 2, 6)])]
    pallas_call x5 -> x6, Pallas kernels: 14.4 us -> 17.2 us  [the longest x2 9.45 us: own(): pl.pallas_call(own_dot_kernel, out_shape=[piece] * 4, grid_spec=pltpu.Pre...]
    all_to_all x1, waiting for transfers between devices: 19.8 us -> 18.1 us  [one_block(): lax.all_to_all(outgoing.reshape(groups, most, features), 'req', split_axi...]
  transfers between devices with their start and end apart: 11 -> 15, of which waited for: 9 -> 10; matrix products, arithmetic and copies ran while one was open for 4% -> 3% of each run, Pallas kernels for 14% -> 18%
where the time goes in v4:
time: 128 us; the launch traced here: 126 us
  waiting for transfers between devices  54.5 us (43%)
  Pallas kernels  38.5 us (30%)
  starting transfers between devices  29.3 us (23%)
  other arithmetic  3.14 us (2%)
    all_to_all x1, waiting for transfers between devices, one_block(): lax.all_to_all(outgoing.reshape(groups, most, features), 'req', split_axi...  18.1 us
    all_to_all x1, waiting for transfers between devices, one_block(): lax.all_to_all(raised.reshape(groups, most, cols), 'req', split_axis=0, c...  11.7 us
    all_to_all x1, starting transfers between devices, one_block(): lax.all_to_all(outgoing.reshape(groups, most, features), 'req', split_axi...  11.5 us
    ppermute x1, waiting for transfers between devices, one_block(): r2b = lax.ppermute(s2b, 'tensor', xor(6))  11 us
    pallas_call x2, Pallas kernels, own(): pl.pallas_call(own_dot_kernel, out_shape=[piece] * 4, grid_spec=pltpu.Pre...  9.45 us
    pallas_call x2, Pallas kernels, parts(): pl.pallas_call(pair_dot_kernel, out_shape=sds((n, tokens, cols), BF), gri...  7.67 us
    ppermute x1, waiting for transfers between devices, one_block(): lax.ppermute((k1b.astype(F32) + r2b.astype(F32)).astype(BF), 'tensor', xo...  5.58 us
    pallas_call x1, Pallas kernels, one_block(): pl.pallas_call(functools.partial(unpack_matrix_kernel, pool=pool, most=mo...  5.52 us
  transfers between devices with their start and end apart: 15, of which 10 were waited for; matrix products, arithmetic and copies ran while one was open for 3% of the time, Pallas kernels for 18%

profile of v4, /device:TPU:6, one launch (start us, length us, event | category | flops | bytes accessed | tf_op | source)
XLA Modules:
  0.0 125.7 jit_solution(970777035179401721)
XLA Ops:
  0.0 2.9 %pack.1 = bf16[1024,512]{1,0:T(8,128)(2,1)} custom-call(s32[1]{0:T(128)} %bitcast.1.me_ref, s32[1,32]{1,0:T(1,128)} %len_ref.3, s32[32,32]{1,0:T(8,128)} %id_ref.3, s32[256]{0:T(256)} %slot_ref.3, bf16[512,512]{1,0:T(8,128)(2,1)} %x_ref.5), custom_call_target="tpu_custom_call" | custom-call | flops 536870912 | bytes 1572864 | tf_op jit(solution)/shard_map/pack/pallas_call | solution.py:169
  2.9 3.9 %pair_dot.2 = bf16[2,512,1024]{2,1,0:T(8,128)(2,1)} custom-call(s32[1]{0:T(128)} %bitcast.t_ref, bf16[512,512]{1,0:T(8,128)(2,1)} %x_ref.5, bf16[512,8192]{1,0:T(8,128)(2,1)} %w_ref.7), custom_call_target="tpu_custom_call" | custom-call | flops 1073741824 | bytes 4194304 | tf_op jit(solution)/shard_map/pair_dot/pallas_call | solution.py:187
  6.8 3.8 %pair_dot.3 = bf16[2,512,1024]{2,1,0:T(8,128)(2,1)} custom-call(s32[1]{0:T(128)} %bitcast.t_ref, bf16[512,512]{1,0:T(8,128)(2,1)} %x_ref.5, bf16[512,8192]{1,0:T(8,128)(2,1)} %w_ref.7), custom_call_target="tpu_custom_call" | custom-call | flops 1073741824 | bytes 4194304 | tf_op jit(solution)/shard_map/pair_dot/pallas_call | solution.py:187
  10.6 0.6 collective-permute-start.1
  11.1 11.5 %all-to-all-start = ((bf16[32,32,512]{2,1,0:T(8,128)(2,1)}), bf16[32,32,512]{2,1,0:T(8,128)(2,1)S(1)}, u32[]{:S(2)}, u32[]{:S(2)}) async-start(bf16[32,32,512]{2,1,0:T(8,128)(2,1)} %bitcast.2), calls=%async_computation | async-start | bytes 2097152 | tf_op jit(solution)/shard_map/all_to_all | solution.py:178
  22.9 0.7 select_reduce_fusion
  23.8 0.2 broadcast_subtract_fusion.code_ref
  24.0 4.7 %own_dot.2 = (bf16[256,1024]{1,0:T(8,128)(2,1)}, bf16[256,1024]{1,0:T(8,128)(2,1)}, bf16[256,1024]{1,0:T(8,128)(2,1)}, bf16[256,1024]{1,0:T(8,128)(2,1)}) custom-call(s32[1]{0:T(128)} %bitcast.t_ref, bf16[512,512]{1,0:T(8,128)(2,1)} %x_ref.5, bf16[512,8192]{1,0:T(8,128)(2,1)} %w_ref.7, bf16[2,512,1024]{2,1,0:T(8,128)(2,1)} %collective-permute-done.p_ref), custom_call_target="tpu_custom_call" | custom-call | flops 1073741824 | bytes 6291456 | tf_op jit(solution)/shard_map/own_dot/pallas_call | solution.py:203
  28.8 4.7 %own_dot.3 = (bf16[256,1024]{1,0:T(8,128)(2,1)}, bf16[256,1024]{1,0:T(8,128)(2,1)}, bf16[256,1024]{1,0:T(8,128)(2,1)}, bf16[256,1024]{1,0:T(8,128)(2,1)}) custom-call(s32[1]{0:T(128)} %bitcast.t_ref, bf16[512,512]{1,0:T(8,128)(2,1)} %x_ref.5, bf16[512,8192]{1,0:T(8,128)(2,1)} %w_ref.7, bf16[2,512,1024]{2,1,0:T(8,128)(2,1)} %collective-permute-done.1.p_ref), custom_call_target="tpu_custom_call" | custom-call | flops 1073741824 | bytes 6291456 | tf_op jit(solution)/shard_map/own_dot/pallas_call | solution.py:203
  33.5 18.1 %all-to-all-done = bf16[32,32,512]{2,1,0:T(8,128)(2,1)S(1)} async-done(((bf16[32,32,512]{2,1,0:T(8,128)(2,1)}), bf16[32,32,512]{2,1,0:T(8,128)(2,1)S(1)}, u32[]{:S(2)}, u32[]{:S(2)}) %all-to-all-start) | async-done | bytes 1048608 | tf_op jit(solution)/shard_map/all_to_all | solution.py:178
  51.6 0.8 down.1
  52.5 1.2 collective-permute-done.2.refs_1_
  53.8 1.5 %collective-permute-start.3 = (bf16[256,128]{1,0:T(8,128)(2,1)S(1)}, bf16[256,128]{1,0:T(8,128)(2,1)S(1)}, u32[]{:S(2)}, u32[]{:S(2)}) collective-permute-start(bf16[256,128]{1,0:T(8,128)(2,1)S(1)} %sum_low.2.refs_0_), channel_id=1, source_target_pairs={{0,128},{32,160},{64,192},{96,224},{128,0},{160,32},{192,64},{224,... | collective-permute-start | bytes 196616 | tf_op jit(solution)/shard_map/ppermute | solution.py:284
  55.2 2.7 %collective-permute-start.5 = (bf16[256,128]{1,0:T(8,128)(2,1)S(1)}, bf16[256,128]{1,0:T(8,128)(2,1)S(1)}, u32[]{:S(2)}, u32[]{:S(2)}) collective-permute-start(bf16[256,128]{1,0:T(8,128)(2,1)S(1)} %sum_low.2.refs_0_), channel_id=1, source_target_pairs={{0,192},{32,224},{64,128},{96,160},{128,64},{160,96},{192,0},{224,... | collective-permute-start | bytes 196616 | tf_op jit(solution)/shard_map/ppermute | solution.py:284
  57.9 2.0 %collective-permute-done.3.refs_1_ = bf16[256,128]{1,0:T(8,128)(2,1)S(1)} collective-permute-done((bf16[256,128]{1,0:T(8,128)(2,1)S(1)}, bf16[256,128]{1,0:T(8,128)(2,1)S(1)}, u32[]{:S(2)}, u32[]{:S(2)}) %collective-permute-start.3) | collective-permute-done | bytes 65568 | tf_op jit(solution)/shard_map/ppermute | solution.py:284
  60.0 1.0 collective-permute-done.5.refs_3_
  61.2 1.2 collective-permute-done.6.other_ref
  62.4 3.1 %up.1 = bf16[1024,1024]{1,0:T(8,128)(2,1)} custom-call(s32[1]{0:T(128)S(6)} %and.5.core_ref, s32[1024,128]{1,0:T(8,128)S(1)} %broadcast_subtract_fusion.code_ref, bf16[256,128]{1,0:T(8,128)(2,1)S(1)} %sum_low.3.mine_ref, bf16[256,128]{1,0:T(8,128)(2,1)S(1)} %collective-permute-done.6.other_ref, bf16[512,1024]{1,0:T(8,128)(2,1)S(1)} %fetch_up.1.u_ref), custom_call_target="tpu_custom_call" | custom-call | flops 1073741824 | bytes 2097152 | tf_op jit(solution)/shard_map/up/pallas_call | solution.py:288
  65.5 5.3 %all-to-all-start.1 = ((bf16[32,32,1024]{2,1,0:T(8,128)(2,1)}), bf16[32,32,1024]{2,1,0:T(8,128)(2,1)S(1)}, u32[]{:S(2)}, u32[]{:S(2)}) async-start(bf16[32,32,1024]{2,1,0:T(8,128)(2,1)} %bitcast.14), calls=%async_computation.1 | async-start | bytes 4194304 | tf_op jit(solution)/shard_map/all_to_all | solution.py:299
  70.8 2.5 %collective-permute-start.11 = (bf16[256,1024]{1,0:T(8,128)(2,1)}, bf16[256,1024]{1,0:T(8,128)(2,1)S(1)}, u32[]{:S(2)}, u32[]{:S(2)}) collective-permute-start(bf16[256,1024]{1,0:T(8,128)(2,1)} %get-tuple-element.59), channel_id=1, source_target_pairs={{0,192},{32,224},{64,128},{96,160},{128,64},{160,96},{192,0},{224,... | collective-permute-start | bytes 1572872 | tf_op jit(solution)/shard_map/ppermute | solution.py:231
  73.3 2.0 %collective-permute-start.7 = (bf16[256,1024]{1,0:T(8,128)(2,1)}, bf16[256,1024]{1,0:T(8,128)(2,1)}, u32[]{:S(2)}, u32[]{:S(2)}) collective-permute-start(bf16[256,1024]{1,0:T(8,128)(2,1)} %get-tuple-element.53), channel_id=1, source_target_pairs={{0,64},{32,96},{64,0},{96,32},{128,192},{160,224},{192,128},{224,1... | collective-permute-start | bytes 1572872 | tf_op jit(solution)/shard_map/ppermute | solution.py:315
  75.3 0.8 collective-permute-start.8
  76.1 11.0 %collective-permute-done.11 = bf16[256,1024]{1,0:T(8,128)(2,1)S(1)} collective-permute-done((bf16[256,1024]{1,0:T(8,128)(2,1)}, bf16[256,1024]{1,0:T(8,128)(2,1)S(1)}, u32[]{:S(2)}, u32[]{:S(2)}) %collective-permute-start.11) | collective-permute-done | bytes 524320 | tf_op jit(solution)/shard_map/ppermute | solution.py:231
  87.1 1.0 add_convert_fusion
  88.3 1.0 add_convert_fusion.1
  89.3 2.3 %collective-permute-start.10 = (bf16[256,1024]{1,0:T(8,128)(2,1)}, bf16[256,1024]{1,0:T(8,128)(2,1)}, u32[]{:S(2)}, u32[]{:S(2)}) collective-permute-start(bf16[256,1024]{1,0:T(8,128)(2,1)} %add_convert_fusion.1), channel_id=1, source_target_pairs={{0,192},{32,224},{64,128},{96,160},{128,64},{160,96},{192,0},{224,... | collective-permute-start | bytes 1572872 | tf_op jit(solution)/shard_map/ppermute | solution.py:313
  91.5 5.5 %unpack_matrix.1.sel_ref = bf16[512,1024]{1,0:T(8,128)(2,1)S(1)} custom-call(s32[1]{0:T(128)} %bitcast.1.me_ref, s32[1,32]{1,0:T(1,128)S(1)} %copy-done.4, s32[32,32]{1,0:T(8,128)S(1)} %copy-done.2, s32[256]{0:T(256)S(1)} %copy-done.3), custom_call_target="tpu_custom_call" | custom-call | flops 4194304 | bytes 1048576 | tf_op jit(solution)/shard_map/unpack_matrix/pallas_call | solution.py:303
  97.0 2.6 %collective-permute-done.7.ra_ref = bf16[256,1024]{1,0:T(8,128)(2,1)} collective-permute-done((bf16[256,1024]{1,0:T(8,128)(2,1)}, bf16[256,1024]{1,0:T(8,128)(2,1)}, u32[]{:S(2)}, u32[]{:S(2)}) %collective-permute-start.7) | collective-permute-done | bytes 524320 | tf_op jit(solution)/shard_map/ppermute | solution.py:315
  99.6 4.3 %before.1.pre_ref = f32[512,1024]{1,0:T(8,128)} custom-call(bf16[512,1024]{1,0:T(8,128)(2,1)} %res_ref.1, bf16[256,1024]{1,0:T(8,128)(2,1)} %get-tuple-element.52.ka_ref, bf16[256,1024]{1,0:T(8,128)(2,1)} %collective-permute-done.7.ra_ref, bf16[256,1024]{1,0:T(8,128)(2,1)} %get-tuple-element.54.kb_ref, bf16[256,1024]{1,0:T(8,128)(2,1)} %collective-permute-done.8.rb_ref), custom_call_target="tpu_custom_call" | custom-call | flops 2097152 | bytes 6291456 | tf_op jit(solution)/shard_map/before/pallas_call | solution.py:321
  103.9 5.6 %collective-permute-done.12.zb_ref = bf16[256,1024]{1,0:T(8,128)(2,1)} collective-permute-done((bf16[256,1024]{1,0:T(8,128)(2,1)}, bf16[256,1024]{1,0:T(8,128)(2,1)}, u32[]{:S(2)}, u32[]{:S(2)}) %collective-permute-start.12) | collective-permute-done | bytes 524320 | tf_op jit(solution)/shard_map/ppermute | solution.py:314
  109.5 11.7 %all-to-all-done.1 = bf16[32,32,1024]{2,1,0:T(8,128)(2,1)S(1)} async-done(((bf16[32,32,1024]{2,1,0:T(8,128)(2,1)}), bf16[32,32,1024]{2,1,0:T(8,128)(2,1)S(1)}, u32[]{:S(2)}, u32[]{:S(2)}) %all-to-all-start.1) | async-done | bytes 2097184 | tf_op jit(solution)/shard_map/all_to_all | solution.py:299
  121.1 4.6 %final.1 = bf16[512,1024]{1,0:T(8,128)(2,1)} custom-call(bf16[512,1024]{1,0:T(8,128)(2,1)S(1)} %unpack_matrix.1.sel_ref, bf16[1024,1024]{1,0:T(8,128)(2,1)S(1)} %bitcast.10, f32[512,1024]{1,0:T(8,128)} %before.1.pre_ref, bf16[256,1024]{1,0:T(8,128)(2,1)} %collective-permute-done.10.za_ref, bf16[256,1024]{1,0:T(8,128)(2,1)} %collective-permute-done.12.zb_ref), custom_call_target="tpu_custom_call" | custom-call | flops 1073741824 | bytes 6291456 | tf_op jit(solution)/shard_map/final/pallas_call | solution.py:331
  (34 shorter events, 0.8 us)
Async XLA Ops:
  6.7 17.3 %collective-permute-start = (bf16[2,512,1024]{2,1,0:T(8,128)(2,1)}, bf16[2,512,1024]{2,1,0:T(8,128)(2,1)}, u32[]{:S(2)}, u32[]{:S(2)}) collective-permute-start(bf16[2,512,1024]{2,1,0:T(8,128)(2,1)} %pair_dot.2), channel_id=1, source_target_pairs={{0,32},{32,0},{64,96},{96,64},{128,160},{160,128},{192,224},{224,1... | collective-permute-start | bytes 6291464 | tf_op jit(solution)/shard_map/ppermute | solution.py:224
  10.6 12.1 %copy-start.3 = (s32[256]{0:T(256)S(1)}, s32[256]{0:T(256)}, u32[]{:S(2)}) copy-start(s32[256]{0:T(256)} %slot_ref.3) | copy-start | bytes 3076
  10.6 12.3 %copy-start.2 = (s32[32,32]{1,0:T(8,128)S(1)}, s32[32,32]{1,0:T(8,128)}, u32[]{:S(2)}) copy-start(s32[32,32]{1,0:T(8,128)} %id_ref.3) | copy-start | bytes 12292
  10.6 13.2 %copy-start = (bf16[8,64,1024]{2,1,0:T(8,128)(2,1)S(1)}, bf16[8,64,1024]{2,1,0:T(8,128)(2,1)}, u32[]{:S(2)}) copy-start(bf16[8,64,1024]{2,1,0:T(8,128)(2,1)} %param.12) | copy-start | bytes 3145732
  10.6 18.2 %collective-permute-start.1 = (bf16[2,512,1024]{2,1,0:T(8,128)(2,1)}, bf16[2,512,1024]{2,1,0:T(8,128)(2,1)}, u32[]{:S(2)}, u32[]{:S(2)}) collective-permute-start(bf16[2,512,1024]{2,1,0:T(8,128)(2,1)} %pair_dot.3), channel_id=1, source_target_pairs={{0,32},{32,0},{64,96},{96,64},{128,160},{160,128},{192,224},{224,1... | collective-permute-start | bytes 6291464 | tf_op jit(solution)/shard_map/ppermute | solution.py:227
  11.1 40.4 %all-to-all-start = ((bf16[32,32,512]{2,1,0:T(8,128)(2,1)}), bf16[32,32,512]{2,1,0:T(8,128)(2,1)S(1)}, u32[]{:S(2)}, u32[]{:S(2)}) async-start(bf16[32,32,512]{2,1,0:T(8,128)(2,1)} %bitcast.2), calls=%async_computation | async-start | bytes 2097152 | tf_op jit(solution)/shard_map/all_to_all | solution.py:178
  28.8 22.8 %copy-start.1 = (bf16[8,512,64]{1,2,0:T(8,128)(2,1)S(1)}, bf16[8,512,64]{1,2,0:T(8,128)(2,1)}, u32[]{:S(2)}) copy-start(bf16[8,512,64]{1,2,0:T(8,128)(2,1)} %param.11) | copy-start | bytes 1572868
  52.4 1.3 %collective-permute-start.2 = (bf16[256,128]{1,0:T(8,128)(2,1)S(1)}, bf16[256,128]{1,0:T(8,128)(2,1)S(1)}, u32[]{:S(2)}, u32[]{:S(2)}) collective-permute-start(bf16[256,128]{1,0:T(8,128)(2,1)S(1)} %get-tuple-element.45), channel_id=1, source_target_pairs={{0,32},{32,0},{64,96},{96,64},{128,160},{160,128},{192,224},{224,1... | collective-permute-start | bytes 196616 | tf_op jit(solution)/shard_map/ppermute | solution.py:283
  53.8 6.2 %collective-permute-start.3 = (bf16[256,128]{1,0:T(8,128)(2,1)S(1)}, bf16[256,128]{1,0:T(8,128)(2,1)S(1)}, u32[]{:S(2)}, u32[]{:S(2)}) collective-permute-start(bf16[256,128]{1,0:T(8,128)(2,1)S(1)} %sum_low.2.refs_0_), channel_id=1, source_target_pairs={{0,128},{32,160},{64,192},{96,224},{128,0},{160,32},{192,64},{224,... | collective-permute-start | bytes 196616 | tf_op jit(solution)/shard_map/ppermute | solution.py:284
  55.2 4.7 %collective-permute-start.4 = (bf16[256,128]{1,0:T(8,128)(2,1)S(1)}, bf16[256,128]{1,0:T(8,128)(2,1)S(1)}, u32[]{:S(2)}, u32[]{:S(2)}) collective-permute-start(bf16[256,128]{1,0:T(8,128)(2,1)S(1)} %sum_low.2.refs_0_), channel_id=1, source_target_pairs={{0,64},{32,96},{64,0},{96,32},{128,192},{160,224},{192,128},{224,1... | collective-permute-start | bytes 196616 | tf_op jit(solution)/shard_map/ppermute | solution.py:284
  55.2 5.8 %collective-permute-start.5 = (bf16[256,128]{1,0:T(8,128)(2,1)S(1)}, bf16[256,128]{1,0:T(8,128)(2,1)S(1)}, u32[]{:S(2)}, u32[]{:S(2)}) collective-permute-start(bf16[256,128]{1,0:T(8,128)(2,1)S(1)} %sum_low.2.refs_0_), channel_id=1, source_target_pairs={{0,192},{32,224},{64,128},{96,160},{128,64},{160,96},{192,0},{224,... | collective-permute-start | bytes 196616 | tf_op jit(solution)/shard_map/ppermute | solution.py:284
  61.1 1.3 %collective-permute-start.6 = (bf16[256,128]{1,0:T(8,128)(2,1)S(1)}, bf16[256,128]{1,0:T(8,128)(2,1)S(1)}, u32[]{:S(2)}, u32[]{:S(2)}) collective-permute-start(bf16[256,128]{1,0:T(8,128)(2,1)S(1)} %sum_low.3.mine_ref), channel_id=1, source_target_pairs={{0,32},{32,0},{64,96},{96,64},{128,160},{160,128},{192,224},{224,1... | collective-permute-start | bytes 196616 | tf_op jit(solution)/shard_map/ppermute | solution.py:285
  65.5 21.6 %copy-start.6 = (bf16[256,1024]{1,0:T(8,128)(2,1)S(1)}, bf16[256,1024]{1,0:T(8,128)(2,1)}, u32[]{:S(2)}) copy-start(bf16[256,1024]{1,0:T(8,128)(2,1)} %get-tuple-element.58) | copy-start | bytes 1572868
  65.5 22.8 %copy-start.5 = (bf16[256,1024]{1,0:T(8,128)(2,1)S(1)}, bf16[256,1024]{1,0:T(8,128)(2,1)}, u32[]{:S(2)}) copy-start(bf16[256,1024]{1,0:T(8,128)(2,1)} %get-tuple-element.57) | copy-start | bytes 1572868
  65.5 55.6 %all-to-all-start.1 = ((bf16[32,32,1024]{2,1,0:T(8,128)(2,1)}), bf16[32,32,1024]{2,1,0:T(8,128)(2,1)S(1)}, u32[]{:S(2)}, u32[]{:S(2)}) async-start(bf16[32,32,1024]{2,1,0:T(8,128)(2,1)} %bitcast.14), calls=%async_computation.1 | async-start | bytes 4194304 | tf_op jit(solution)/shard_map/all_to_all | solution.py:299
  70.8 20.8 %copy-start.4 = (s32[1,32]{1,0:T(1,128)S(1)}, s32[1,32]{1,0:T(1,128)}, u32[]{:S(2)}) copy-start(s32[1,32]{1,0:T(1,128)} %len_ref.3) | copy-start | bytes 388
  70.8 16.3 %collective-permute-start.11 = (bf16[256,1024]{1,0:T(8,128)(2,1)}, bf16[256,1024]{1,0:T(8,128)(2,1)S(1)}, u32[]{:S(2)}, u32[]{:S(2)}) collective-permute-start(bf16[256,1024]{1,0:T(8,128)(2,1)} %get-tuple-element.59), channel_id=1, source_target_pairs={{0,192},{32,224},{64,128},{96,160},{128,64},{160,96},{192,0},{224,... | collective-permute-start | bytes 1572872 | tf_op jit(solution)/shard_map/ppermute | solution.py:231
  73.3 15.0 %collective-permute-start.9 = (bf16[256,1024]{1,0:T(8,128)(2,1)}, bf16[256,1024]{1,0:T(8,128)(2,1)S(1)}, u32[]{:S(2)}, u32[]{:S(2)}) collective-permute-start(bf16[256,1024]{1,0:T(8,128)(2,1)} %get-tuple-element.38), channel_id=1, source_target_pairs={{0,64},{32,96},{64,0},{96,32},{128,192},{160,224},{192,128},{224,1... | collective-permute-start | bytes 1572872 | tf_op jit(solution)/shard_map/ppermute | solution.py:230
  73.3 26.3 %collective-permute-start.7 = (bf16[256,1024]{1,0:T(8,128)(2,1)}, bf16[256,1024]{1,0:T(8,128)(2,1)}, u32[]{:S(2)}, u32[]{:S(2)}) collective-permute-start(bf16[256,1024]{1,0:T(8,128)(2,1)} %get-tuple-element.53), channel_id=1, source_target_pairs={{0,64},{32,96},{64,0},{96,32},{128,192},{160,224},{192,128},{224,1... | collective-permute-start | bytes 1572872 | tf_op jit(solution)/shard_map/ppermute | solution.py:315
  75.3 24.3 %collective-permute-start.8 = (bf16[256,1024]{1,0:T(8,128)(2,1)}, bf16[256,1024]{1,0:T(8,128)(2,1)}, u32[]{:S(2)}, u32[]{:S(2)}) collective-permute-start(bf16[256,1024]{1,0:T(8,128)(2,1)} %get-tuple-element.55), channel_id=1, source_target_pairs={{0,192},{32,224},{64,128},{96,160},{128,64},{160,96},{192,0},{224,... | collective-permute-start | bytes 1572872 | tf_op jit(solution)/shard_map/ppermute | solution.py:316
  88.1 21.4 %collective-permute-start.12 = (bf16[256,1024]{1,0:T(8,128)(2,1)}, bf16[256,1024]{1,0:T(8,128)(2,1)}, u32[]{:S(2)}, u32[]{:S(2)}) collective-permute-start(bf16[256,1024]{1,0:T(8,128)(2,1)} %add_convert_fusion), channel_id=1, source_target_pairs={{0,64},{32,96},{64,0},{96,32},{128,192},{160,224},{192,128},{224,1... | collective-permute-start | bytes 1572872 | tf_op jit(solution)/shard_map/ppermute | solution.py:314
  89.3 20.2 %collective-permute-start.10 = (bf16[256,1024]{1,0:T(8,128)(2,1)}, bf16[256,1024]{1,0:T(8,128)(2,1)}, u32[]{:S(2)}, u32[]{:S(2)}) collective-permute-start(bf16[256,1024]{1,0:T(8,128)(2,1)} %add_convert_fusion.1), channel_id=1, source_target_pairs={{0,192},{32,224},{64,128},{96,160},{128,64},{160,96},{192,0},{224,... | collective-permute-start | bytes 1572872 | tf_op jit(solution)/shard_map/ppermute | solution.py:313

commit v5 on v4

--- a/solution.py
+++ b/solution.py
@@ -12,6 +12,9 @@
 F32 = jnp.float32
 VM = pl.BlockSpec(memory_space=pltpu.VMEM)
 SM = pl.BlockSpec(memory_space=pltpu.SMEM)
+HB = pl.BlockSpec(memory_space=pl.ANY)
+DMA = pltpu.SemaphoreType.DMA
+PARTS = 4
 
 
 SMALL = pltpu.CompilerParams(vmem_limit_bytes=24 * 2**20)
@@ -21,7 +24,9 @@
     return pl.CostEstimate(flops=int(flops), transcendentals=0, bytes_accessed=int(nbytes))
 
 
-def pack_kernel(me_ref, len_ref, id_ref, slot_ref, x_ref, out_ref, sel_ref, *, pool, most):
+def pack_kernel(me_ref, len_ref, id_ref, slot_ref, x_ref, out_ref, x_buf, sel_ref, o_buf, x_sem, o_sem, *, pool, most):
+    fetch = pltpu.make_async_copy(x_ref, x_buf, x_sem)
+    fetch.start()
     requests = len_ref.shape[1]
     tokens = x_ref.shape[0]
     rows = lax.broadcasted_iota(jnp.int32, (most, tokens), 0)
@@ -33,7 +38,16 @@
         at = pl.multiple_of(owner * most, most)
         sel_ref[pl.ds(at, most), :] = jnp.where(ahead == start, 1.0, 0.0).astype(BF)
         start = start + len_ref[0, r]
-    out_ref[...] = jnp.dot(sel_ref[...], x_ref[...], preferred_element_type=F32).astype(BF)
+    fetch.wait()
+    n = out_ref.shape[0] // PARTS
+    leaving = []
+    for i in range(PARTS):
+        at = pl.ds(i * n, n)
+        o_buf[at, :] = jnp.dot(sel_ref[at, :], x_buf[...], preferred_element_type=F32).astype(BF)
+        leaving.append(pltpu.make_async_copy(o_buf.at[at], out_ref.at[at], o_sem.at[i]))
+        leaving[-1].start()
+    for copy in leaving:
+        copy.wait()
 
 
 def unpack_matrix_kernel(me_ref, len_ref, id_ref, slot_ref, sel_ref, *, pool, most):
@@ -83,19 +97,27 @@
         send_ref[...] = top
 
 
-def up_kernel(core_ref, code_ref, mine_ref, other_ref, u_ref, out_ref, *, pool):
-    i = pl.program_id(0)
-    rows, lanes = mine_ref.shape
+def up_kernel(core_ref, code_ref, low_ref, u_ref, *rest, pool, flip):
+    out_ref, o_buf, o_sem = rest[-3:]
+    rows, lanes = low_ref.shape
     rank = lanes // 2
-    own = lax.rem(i, 2) == core_ref[0]
-    low = jnp.where(own, mine_ref[...].astype(F32), other_ref[...].astype(F32))
-    first = lax.broadcasted_iota(jnp.int32, low.shape, 1) < rank
-    low = jnp.where(jnp.logical_xor(first, i >= 2), low, pltpu.roll(low, rank, 1))
-    code = code_ref[pl.ds(pl.multiple_of(i * rows, rows), rows), :]
-    spread = jnp.concatenate(
-        [jnp.where(code == 2 * k, low, 0.0).astype(BF) for k in range(pool // 2)], 1
-    )
-    out_ref[...] = jnp.dot(spread, u_ref[...], preferred_element_type=F32).astype(BF)
+    which = core_ref[0] ^ flip
+    packed = low_ref[...].astype(F32)
+    turned = pltpu.roll(packed, rank, 1)
+    first = lax.broadcasted_iota(jnp.int32, packed.shape, 1) < rank
+    leaving = []
+    for i in range(2):
+        low = jnp.where(first, packed, turned) if i == 0 else jnp.where(first, turned, packed)
+        at = pl.ds(pl.multiple_of((2 * i + which) * rows, rows), rows)
+        code = code_ref[at, :]
+        spread = jnp.concatenate(
+            [jnp.where(code == 2 * k, low, 0.0).astype(BF) for k in range(pool // 2)], 1
+        )
+        o_buf[i] = jnp.dot(spread, u_ref[...], preferred_element_type=F32).astype(BF)
+        leaving.append(pltpu.make_async_copy(o_buf.at[i], out_ref.at[at], o_sem.at[i]))
+        leaving[-1].start()
+    for copy in leaving:
+        copy.wait()
 
 
 def pair_dot_kernel(t_ref, x_ref, w_ref, out_ref):
@@ -118,19 +140,28 @@
         b1_ref[...] = both[half:]
 
 
-def before_kernel(res_ref, ka_ref, ra_ref, kb_ref, rb_ref, out_ref):
+def before_kernel(res_ref, ka_ref, ra_ref, za_ref, kb_ref, rb_ref, zb_ref, out_ref):
     half = res_ref.shape[0] // 2
-    out_ref[:half] = res_ref[:half].astype(F32) + (ka_ref[...].astype(F32) + ra_ref[...].astype(F32))
-    out_ref[half:] = res_ref[half:].astype(F32) + (kb_ref[...].astype(F32) + rb_ref[...].astype(F32))
-
-
-def final_kernel(sel_ref, ret_ref, pre_ref, za_ref, zb_ref, out_ref):
-    wide = out_ref.shape[1]
-    half = za_ref.shape[0]
-    at = pl.ds(pl.multiple_of(pl.program_id(0) * wide, wide), wide)
-    delta = jnp.dot(sel_ref[...], ret_ref[:, at], preferred_element_type=F32) + pre_ref[...]
-    out_ref[:half] = (delta[:half] + za_ref[...].astype(F32)).astype(BF)
-    out_ref[half:] = (delta[half:] + zb_ref[...].astype(F32)).astype(BF)
+    base_a = ka_ref[...].astype(F32) + ra_ref[...].astype(F32) + za_ref[...].astype(F32)
+    base_b = kb_ref[...].astype(F32) + rb_ref[...].astype(F32) + zb_ref[...].astype(F32)
+    out_ref[:half] = res_ref[:half].astype(F32) + base_a
+    out_ref[half:] = res_ref[half:].astype(F32) + base_b
+
+
+def final_kernel(sel_ref, ret_ref, pre_ref, out_ref, p_buf, o_buf, p_sem, o_sem):
+    n = out_ref.shape[1] // PARTS
+    at = [pl.ds(i * n, n) for i in range(PARTS)]
+    coming = [pltpu.make_async_copy(pre_ref.at[:, at[i]], p_buf.at[i], p_sem.at[i]) for i in range(PARTS)]
+    leaving = [pltpu.make_async_copy(o_buf.at[i], out_ref.at[:, at[i]], o_sem.at[i]) for i in range(PARTS)]
+    for copy in coming:
+        copy.start()
+    for i in range(PARTS):
+        delta = jnp.dot(sel_ref[...], ret_ref[:, at[i]], preferred_element_type=F32)
+        coming[i].wait()
+        o_buf[i] = (p_buf[i] + delta).astype(BF)
+        leaving[i].start()
+    for copy in leaving:
+        copy.wait()
 
 
 def sum_kernel(*refs):
@@ -169,9 +200,15 @@
     outgoing = pl.pallas_call(
         functools.partial(pack_kernel, pool=pool, most=most),
         out_shape=sds((slots, features), BF),
-        in_specs=[SM, SM, SM, SM, VM],
-        out_specs=VM,
-        scratch_shapes=[pltpu.VMEM((slots, tokens), BF)],
+        in_specs=[SM, SM, SM, SM, HB],
+        out_specs=HB,
+        scratch_shapes=[
+            pltpu.VMEM((tokens, features), BF),
+            pltpu.VMEM((slots, tokens), BF),
+            pltpu.VMEM((slots, features), BF),
+            DMA,
+            DMA((PARTS,)),
+        ],
         cost_estimate=cost(2 * slots * tokens * features, 2 * (slots + tokens) * features),
         name="pack",
     )(me1, req_len, req_id, pool_slot, x)
@@ -284,17 +321,21 @@
     low = total(low, *[lax.ppermute(low, "tensor", xor(m)) for m in (4, 2, 6)])
     other = lax.ppermute(low, "tensor", xor(1))
 
-    step = slots // 4
-    raised = pl.pallas_call(
-        functools.partial(up_kernel, pool=pool),
-        out_shape=pltpu.HBM((slots, cols), BF),
-        grid=(4,),
-        in_specs=[SM] + [VM] * 4,
-        out_specs=pl.BlockSpec((step, cols), lambda i: (i, 0)),
-        cost_estimate=cost(2 * slots * pool * rank * cols, 2 * slots * cols),
-        name="up",
-        compiler_params=SMALL,
-    )(core, code, near(low), near(other), near(up_maps))
+    def lift(rows_low, flip, filled=()):
+        return pl.pallas_call(
+            functools.partial(up_kernel, pool=pool, flip=flip),
+            out_shape=pltpu.HBM((slots, cols), BF),
+            in_specs=[SM, VM, VM, VM] + [HB] * len(filled),
+            out_specs=HB,
+            scratch_shapes=[pltpu.VMEM((2, slots // 4, cols), BF), DMA((2,))],
+            input_output_aliases={4: 0} if filled else {},
+            cost_estimate=cost(slots * pool * rank * cols, slots * cols),
+            name="up",
+            compiler_params=SMALL,
+        )(core, code, near(rows_low), near(up_maps), *filled)
+
+    raised = lift(low, 0)
+    raised = lift(other, 1, (raised,))
     raised, s1a, s3b, k3a, k1b, me1 = lax.optimization_barrier((raised, s1a, s3b, k3a, k1b, me1))
     returned = lax.all_to_all(
         raised.reshape(groups, most, cols), "req", split_axis=0, concat_axis=0, tiled=True
@@ -322,22 +363,27 @@
         before_kernel,
         out_shape=pltpu.HBM((tokens, cols), F32),
         grid=(4,),
-        in_specs=[tall, flat, flat, flat, flat],
+        in_specs=[tall] + [flat] * 6,
         out_specs=tall,
         cost_estimate=cost(4 * tokens * cols, 12 * tokens * cols),
         name="before",
-    )(residual, k0a, r1a, k0b, r3b)
-    returned, pre, sel, za, zb = lax.optimization_barrier((returned, pre, sel, za, zb))
+    )(residual, k0a, r1a, za, k0b, r3b, zb)
+    returned, pre, sel = lax.optimization_barrier((returned, pre, sel))
     return pl.pallas_call(
         final_kernel,
         out_shape=sds((tokens, cols), BF),
-        grid=(4,),
-        in_specs=[VM, VM, tall, flat, flat],
-        out_specs=tall,
+        in_specs=[VM, VM, HB],
+        out_specs=HB,
+        scratch_shapes=[
+            pltpu.VMEM((PARTS, tokens, cols // PARTS), F32),
+            pltpu.VMEM((PARTS, tokens, cols // PARTS), BF),
+            DMA((PARTS,)),
+            DMA((PARTS,)),
+        ],
         cost_estimate=cost(2 * tokens * slots * cols, 2 * cols * (slots + 4 * tokens)),
         name="final",
         compiler_params=pltpu.CompilerParams(vmem_limit_bytes=59 * 2**20),
-    )(near(sel), near(returned.reshape(slots, cols)), pre, za, zb)
+    )(near(sel), near(returned.reshape(slots, cols)), pre)
 
 
 def solution(mesh):

time: 128 us -> 128 us (level)
  other arithmetic: 3.14 us -> 1.5 us
    ppermute x1, waiting for transfers between devices: 11 us -> 0.01 us  [one_block(): r2b = lax.ppermute(s2b, 'tensor', xor(6))]
    ppermute x1, waiting for transfers between devices: 0.01 us -> 10.3 us  [one_block(): lax.ppermute((k3a.astype(F32) + r2a.astype(F32)).astype(BF), 'tensor', xo...]
    ppermute x1, waiting for transfers between devices: 0.14 us -> 10.3 us  [one_block(): r2a = lax.ppermute(s2a, 'tensor', xor(2))]
    ppermute x1, waiting for transfers between devices: 5.58 us -> 0.01 us  [one_block(): lax.ppermute((k1b.astype(F32) + r2b.astype(F32)).astype(BF), 'tensor', xo...]
    all_to_all x1, waiting for transfers between devices: 11.7 us -> 7.8 us  [one_block(): lax.all_to_all(raised.reshape(groups, most, cols), 'req', split_axis=0, c...]
    ppermute x1, starting transfers between devices: 2.02 us -> 0.01 us  [one_block(): r1a = lax.ppermute(s1a, 'tensor', xor(2))]
    ppermute x1, waiting for transfers between devices: 0.01 us -> 1.53 us  [one_block(): r3b = lax.ppermute(s3b, 'tensor', xor(6))]
    all_to_all x1, waiting for transfers between devices: 18.1 us -> 16.8 us  [one_block(): lax.all_to_all(outgoing.reshape(groups, most, features), 'req', split_axi...]
  transfers between devices with their start and end apart: 15 -> 15, of which waited for: 10 -> 9; matrix products, arithmetic and copies ran while one was open for 3% -> 1% of each run, Pallas kernels for 18% -> 20%
where the time goes in v5:
time: 128 us; the launch traced here: 126 us
  waiting for transfers between devices  54 us (42%)
  Pallas kernels  39 us (30%)
  starting transfers between devices  29.6 us (23%)
  other arithmetic  1.5 us (1%)
  local copies, waits for them, and re-layouts  1.41 us (1%)
    all_to_all x1, waiting for transfers between devices, one_block(): lax.all_to_all(outgoing.reshape(groups, most, features), 'req', split_axi...  16.8 us
    all_to_all x1, starting transfers between devices, one_block(): lax.all_to_all(outgoing.reshape(groups, most, features), 'req', split_axi...  11.5 us
    ppermute x1, waiting for transfers between devices, one_block(): r2a = lax.ppermute(s2a, 'tensor', xor(2))  10.3 us
    ppermute x1, waiting for transfers between devices, one_block(): lax.ppermute((k3a.astype(F32) + r2a.astype(F32)).astype(BF), 'tensor', xo...  10.3 us
    pallas_call x2, Pallas kernels, own(): pl.pallas_call(own_dot_kernel, out_shape=[piece] * 4, grid_spec=pltpu.Pre...  9.5 us
    all_to_all x1, waiting for transfers between devices, one_block(): lax.all_to_all(raised.reshape(groups, most, cols), 'req', split_axis=0, c...  7.8 us
    pallas_call x2, Pallas kernels, parts(): pl.pallas_call(pair_dot_kernel, out_shape=sds((n, tokens, cols), BF), gri...  7.69 us
    pallas_call x1, Pallas kernels, one_block(): pl.pallas_call(functools.partial(unpack_matrix_kernel, pool=pool, most=mo...  5.51 us
  transfers between devices with their start and end apart: 15, of which 9 were waited for; matrix products, arithmetic and copies ran while one was open for 1% of the time, Pallas kernels for 20%

profile of v5, /device:TPU:6, one launch (start us, length us, event | category | flops | bytes accessed | tf_op | source)
XLA Modules:
  0.0 125.8 jit_solution(14048145325712366689)
XLA Ops:
  0.0 3.6 %pack.1 = bf16[1024,512]{1,0:T(8,128)(2,1)} custom-call(s32[1]{0:T(128)} %bitcast.1.me_ref, s32[1,32]{1,0:T(1,128)} %len_ref.3, s32[32,32]{1,0:T(8,128)} %id_ref.3, s32[256]{0:T(256)} %slot_ref.3, bf16[512,512]{1,0:T(8,128)(2,1)} %x_ref.5), custom_call_target="tpu_custom_call" | custom-call | flops 536870912 | bytes 1572864 | tf_op jit(solution)/shard_map/pack/pallas_call | solution.py:200
  3.6 3.9 %pair_dot.2 = bf16[2,512,1024]{2,1,0:T(8,128)(2,1)} custom-call(s32[1]{0:T(128)} %bitcast.t_ref, bf16[512,512]{1,0:T(8,128)(2,1)} %x_ref.5, bf16[512,8192]{1,0:T(8,128)(2,1)} %w_ref.7), custom_call_target="tpu_custom_call" | custom-call | flops 1073741824 | bytes 4194304 | tf_op jit(solution)/shard_map/pair_dot/pallas_call | solution.py:224
  7.5 3.8 %pair_dot.3 = bf16[2,512,1024]{2,1,0:T(8,128)(2,1)} custom-call(s32[1]{0:T(128)} %bitcast.t_ref, bf16[512,512]{1,0:T(8,128)(2,1)} %x_ref.5, bf16[512,8192]{1,0:T(8,128)(2,1)} %w_ref.7), custom_call_target="tpu_custom_call" | custom-call | flops 1073741824 | bytes 4194304 | tf_op jit(solution)/shard_map/pair_dot/pallas_call | solution.py:224
  11.3 0.5 collective-permute-start.1
  11.8 11.5 %all-to-all-start = ((bf16[32,32,512]{2,1,0:T(8,128)(2,1)}), bf16[32,32,512]{2,1,0:T(8,128)(2,1)S(1)}, u32[]{:S(2)}, u32[]{:S(2)}) async-start(bf16[32,32,512]{2,1,0:T(8,128)(2,1)} %bitcast.2), calls=%async_computation | async-start | bytes 2097152 | tf_op jit(solution)/shard_map/all_to_all | solution.py:215
  23.5 0.7 select_reduce_fusion
  24.4 1.2 copy-done
  26.0 4.7 %own_dot.2 = (bf16[256,1024]{1,0:T(8,128)(2,1)}, bf16[256,1024]{1,0:T(8,128)(2,1)}, bf16[256,1024]{1,0:T(8,128)(2,1)}, bf16[256,1024]{1,0:T(8,128)(2,1)}) custom-call(s32[1]{0:T(128)} %bitcast.t_ref, bf16[512,512]{1,0:T(8,128)(2,1)} %x_ref.5, bf16[512,8192]{1,0:T(8,128)(2,1)} %w_ref.7, bf16[2,512,1024]{2,1,0:T(8,128)(2,1)} %collective-permute-done.p_ref), custom_call_target="tpu_custom_call" | custom-call | flops 1073741824 | bytes 6291456 | tf_op jit(solution)/shard_map/own_dot/pallas_call | solution.py:240
  30.7 4.8 %own_dot.3 = (bf16[256,1024]{1,0:T(8,128)(2,1)}, bf16[256,1024]{1,0:T(8,128)(2,1)}, bf16[256,1024]{1,0:T(8,128)(2,1)}, bf16[256,1024]{1,0:T(8,128)(2,1)}) custom-call(s32[1]{0:T(128)} %bitcast.t_ref, bf16[512,512]{1,0:T(8,128)(2,1)} %x_ref.5, bf16[512,8192]{1,0:T(8,128)(2,1)} %w_ref.7, bf16[2,512,1024]{2,1,0:T(8,128)(2,1)} %collective-permute-done.1.p_ref), custom_call_target="tpu_custom_call" | custom-call | flops 1073741824 | bytes 6291456 | tf_op jit(solution)/shard_map/own_dot/pallas_call | solution.py:240
  35.5 16.8 %all-to-all-done = bf16[32,32,512]{2,1,0:T(8,128)(2,1)S(1)} async-done(((bf16[32,32,512]{2,1,0:T(8,128)(2,1)}), bf16[32,32,512]{2,1,0:T(8,128)(2,1)S(1)}, u32[]{:S(2)}, u32[]{:S(2)}) %all-to-all-start) | async-done | bytes 1048608 | tf_op jit(solution)/shard_map/all_to_all | solution.py:215
  52.2 0.8 down.1
  53.2 1.2 collective-permute-done.2.refs_1_
  54.4 0.6 collective-permute-start.5
  55.0 0.9 collective-permute-start.4
  55.9 3.3 %collective-permute-start.3 = (bf16[256,128]{1,0:T(8,128)(2,1)S(1)}, bf16[256,128]{1,0:T(8,128)(2,1)S(1)}, u32[]{:S(2)}, u32[]{:S(2)}) collective-permute-start(bf16[256,128]{1,0:T(8,128)(2,1)S(1)} %sum_low.2.refs_0_), channel_id=1, source_target_pairs={{0,128},{32,160},{64,192},{96,224},{128,0},{160,32},{192,64},{224,... | collective-permute-start | bytes 196616 | tf_op jit(solution)/shard_map/ppermute | solution.py:321
  59.2 0.8 collective-permute-done.5.refs_3_
  60.0 2.5 %collective-permute-done.3.refs_1_ = bf16[256,128]{1,0:T(8,128)(2,1)S(1)} collective-permute-done((bf16[256,128]{1,0:T(8,128)(2,1)S(1)}, bf16[256,128]{1,0:T(8,128)(2,1)S(1)}, u32[]{:S(2)}, u32[]{:S(2)}) %collective-permute-start.3) | collective-permute-done | bytes 65568 | tf_op jit(solution)/shard_map/ppermute | solution.py:321
  62.6 1.6 %up.2.rest_0_ = bf16[1024,1024]{1,0:T(8,128)(2,1)} custom-call(s32[1]{0:T(128)S(6)} %and.5.core_ref, s32[1024,128]{1,0:T(8,128)S(1)} %broadcast_subtract_fusion.code_ref, bf16[256,128]{1,0:T(8,128)(2,1)S(1)} %sum_low.3.low_ref, bf16[512,1024]{1,0:T(8,128)(2,1)S(1)} %fetch_up.1.u_ref), custom_call_target="tpu_custom_call" | custom-call | flops 536870912 | bytes 1048576 | tf_op jit(solution)/shard_map/up/pallas_call | solution.py:325
  64.2 1.6 %up.3 = bf16[1024,1024]{1,0:T(8,128)(2,1)} custom-call(s32[1]{0:T(128)S(6)} %and.5.core_ref, s32[1024,128]{1,0:T(8,128)S(1)} %broadcast_subtract_fusion.code_ref, bf16[256,128]{1,0:T(8,128)(2,1)S(1)} %collective-permute-done.6.low_ref, bf16[512,1024]{1,0:T(8,128)(2,1)S(1)} %fetch_up.1.u_ref, ...), custom_call_target="tpu_custom_call", output_to_operand_aliasing={{}: (4, {})} | custom-call | flops 536870912 | bytes 1048576 | tf_op jit(solution)/shard_map/up/pallas_call | solution.py:325
  65.8 5.3 %all-to-all-start.1 = ((bf16[32,32,1024]{2,1,0:T(8,128)(2,1)}), bf16[32,32,1024]{2,1,0:T(8,128)(2,1)S(1)}, u32[]{:S(2)}, u32[]{:S(2)}) async-start(bf16[32,32,1024]{2,1,0:T(8,128)(2,1)} %bitcast.14), calls=%async_computation.1 | async-start | bytes 4194304 | tf_op jit(solution)/shard_map/all_to_all | solution.py:340
  71.5 2.8 %collective-permute-start.11 = (bf16[256,1024]{1,0:T(8,128)(2,1)}, bf16[256,1024]{1,0:T(8,128)(2,1)S(1)}, u32[]{:S(2)}, u32[]{:S(2)}) collective-permute-start(bf16[256,1024]{1,0:T(8,128)(2,1)} %get-tuple-element.56), channel_id=1, source_target_pairs={{0,192},{32,224},{64,128},{96,160},{128,64},{160,96},{192,0},{224,... | collective-permute-start | bytes 1572872 | tf_op jit(solution)/shard_map/ppermute | solution.py:268
  74.3 1.6 %collective-permute-start.10 = (bf16[256,1024]{1,0:T(8,128)(2,1)}, bf16[256,1024]{1,0:T(8,128)(2,1)}, u32[]{:S(2)}, u32[]{:S(2)}) collective-permute-start(bf16[256,1024]{1,0:T(8,128)(2,1)} %get-tuple-element.54), channel_id=1, source_target_pairs={{0,192},{32,224},{64,128},{96,160},{128,64},{160,96},{192,0},{224,... | collective-permute-start | bytes 1572872 | tf_op jit(solution)/shard_map/ppermute | solution.py:357
  75.8 10.3 %collective-permute-done.8 = bf16[256,1024]{1,0:T(8,128)(2,1)S(1)} collective-permute-done((bf16[256,1024]{1,0:T(8,128)(2,1)}, bf16[256,1024]{1,0:T(8,128)(2,1)S(1)}, u32[]{:S(2)}, u32[]{:S(2)}) %collective-permute-start.8) | collective-permute-done | bytes 524320 | tf_op jit(solution)/shard_map/ppermute | solution.py:267
  86.4 1.4 %collective-permute-start.9 = (bf16[256,1024]{1,0:T(8,128)(2,1)S(1)}, bf16[256,1024]{1,0:T(8,128)(2,1)}, u32[]{:S(2)}, u32[]{:S(2)}) collective-permute-start(bf16[256,1024]{1,0:T(8,128)(2,1)S(1)} %add_convert_fusion.1), channel_id=1, source_target_pairs={{0,192},{32,224},{64,128},{96,160},{128,64},{160,96},{192,0},{224,... | collective-permute-start | bytes 1572872 | tf_op jit(solution)/shard_map/ppermute | solution.py:354
  88.0 1.3 %collective-permute-start.12 = (bf16[256,1024]{1,0:T(8,128)(2,1)S(1)}, bf16[256,1024]{1,0:T(8,128)(2,1)}, u32[]{:S(2)}, u32[]{:S(2)}) collective-permute-start(bf16[256,1024]{1,0:T(8,128)(2,1)S(1)} %add_convert_fusion), channel_id=1, source_target_pairs={{0,64},{32,96},{64,0},{96,32},{128,192},{160,224},{192,128},{224,1... | collective-permute-start | bytes 1572872 | tf_op jit(solution)/shard_map/ppermute | solution.py:355
  89.2 5.5 %unpack_matrix.1.sel_ref = bf16[512,1024]{1,0:T(8,128)(2,1)S(1)} custom-call(s32[1]{0:T(128)} %bitcast.1.me_ref, s32[1,32]{1,0:T(1,128)S(1)} %copy-done.4, s32[32,32]{1,0:T(8,128)S(1)} %copy-done.2, s32[256]{0:T(256)S(1)} %copy-done.3), custom_call_target="tpu_custom_call" | custom-call | flops 4194304 | bytes 1048576 | tf_op jit(solution)/shard_map/unpack_matrix/pallas_call | solution.py:344
  94.8 2.8 %collective-permute-done.7.ra_ref = bf16[256,1024]{1,0:T(8,128)(2,1)} collective-permute-done((bf16[256,1024]{1,0:T(8,128)(2,1)}, bf16[256,1024]{1,0:T(8,128)(2,1)}, u32[]{:S(2)}, u32[]{:S(2)}) %collective-permute-start.7) | collective-permute-done | bytes 524320 | tf_op jit(solution)/shard_map/ppermute | solution.py:356
  97.5 1.5 %collective-permute-done.10.rb_ref = bf16[256,1024]{1,0:T(8,128)(2,1)} collective-permute-done((bf16[256,1024]{1,0:T(8,128)(2,1)}, bf16[256,1024]{1,0:T(8,128)(2,1)}, u32[]{:S(2)}, u32[]{:S(2)}) %collective-permute-start.10) | collective-permute-done | bytes 524320 | tf_op jit(solution)/shard_map/ppermute | solution.py:357
  99.0 10.3 %collective-permute-done.9.za_ref = bf16[256,1024]{1,0:T(8,128)(2,1)} collective-permute-done((bf16[256,1024]{1,0:T(8,128)(2,1)S(1)}, bf16[256,1024]{1,0:T(8,128)(2,1)}, u32[]{:S(2)}, u32[]{:S(2)}) %collective-permute-start.9) | collective-permute-done | bytes 524320 | tf_op jit(solution)/shard_map/ppermute | solution.py:354
  109.3 4.5 %before.1.pre_ref = f32[512,1024]{1,0:T(8,128)} custom-call(bf16[512,1024]{1,0:T(8,128)(2,1)} %res_ref.1, bf16[256,1024]{1,0:T(8,128)(2,1)} %get-tuple-element.50.ka_ref, bf16[256,1024]{1,0:T(8,128)(2,1)} %collective-permute-done.7.ra_ref, bf16[256,1024]{1,0:T(8,128)(2,1)} %collective-permute-done.9.za_ref, bf16[256,1024]{1,0:T(8,128)(2,1)} %get-tuple-element.53.kb_ref, ...), custom_call_target="tpu_custom_call" | custom-call | flops 2097152 | bytes 6291456 | tf_op jit(solution)/shard_map/before/pallas_call | solution.py:362
  113.8 7.8 %all-to-all-done.1 = bf16[32,32,1024]{2,1,0:T(8,128)(2,1)S(1)} async-done(((bf16[32,32,1024]{2,1,0:T(8,128)(2,1)}), bf16[32,32,1024]{2,1,0:T(8,128)(2,1)S(1)}, u32[]{:S(2)}, u32[]{:S(2)}) %all-to-all-start.1) | async-done | bytes 2097184 | tf_op jit(solution)/shard_map/all_to_all | solution.py:340
  121.6 4.0 %final.1 = bf16[512,1024]{1,0:T(8,128)(2,1)} custom-call(bf16[512,1024]{1,0:T(8,128)(2,1)S(1)} %unpack_matrix.1.sel_ref, bf16[1024,1024]{1,0:T(8,128)(2,1)S(1)} %bitcast.10, f32[512,1024]{1,0:T(8,128)} %before.1.pre_ref), custom_call_target="tpu_custom_call" | custom-call | flops 1073741824 | bytes 6291456 | tf_op jit(solution)/shard_map/final/pallas_call | solution.py:372
  (35 shorter events, 1.7 us)
Async XLA Ops:
  7.5 18.4 %collective-permute-start = (bf16[2,512,1024]{2,1,0:T(8,128)(2,1)}, bf16[2,512,1024]{2,1,0:T(8,128)(2,1)}, u32[]{:S(2)}, u32[]{:S(2)}) collective-permute-start(bf16[2,512,1024]{2,1,0:T(8,128)(2,1)} %pair_dot.2), channel_id=1, source_target_pairs={{0,32},{32,0},{64,96},{96,64},{128,160},{160,128},{192,224},{224,1... | collective-permute-start | bytes 6291464 | tf_op jit(solution)/shard_map/ppermute | solution.py:261
  11.3 12.0 %copy-start.3 = (s32[256]{0:T(256)S(1)}, s32[256]{0:T(256)}, u32[]{:S(2)}) copy-start(s32[256]{0:T(256)} %slot_ref.3) | copy-start | bytes 3076
  11.3 12.2 %copy-start.2 = (s32[32,32]{1,0:T(8,128)S(1)}, s32[32,32]{1,0:T(8,128)}, u32[]{:S(2)}) copy-start(s32[32,32]{1,0:T(8,128)} %id_ref.3) | copy-start | bytes 12292
  11.3 19.3 %collective-permute-start.1 = (bf16[2,512,1024]{2,1,0:T(8,128)(2,1)}, bf16[2,512,1024]{2,1,0:T(8,128)(2,1)}, u32[]{:S(2)}, u32[]{:S(2)}) collective-permute-start(bf16[2,512,1024]{2,1,0:T(8,128)(2,1)} %pair_dot.3), channel_id=1, source_target_pairs={{0,32},{32,0},{64,96},{96,64},{128,160},{160,128},{192,224},{224,1... | collective-permute-start | bytes 6291464 | tf_op jit(solution)/shard_map/ppermute | solution.py:264
  11.8 40.4 %all-to-all-start = ((bf16[32,32,512]{2,1,0:T(8,128)(2,1)}), bf16[32,32,512]{2,1,0:T(8,128)(2,1)S(1)}, u32[]{:S(2)}, u32[]{:S(2)}) async-start(bf16[32,32,512]{2,1,0:T(8,128)(2,1)} %bitcast.2), calls=%async_computation | async-start | bytes 2097152 | tf_op jit(solution)/shard_map/all_to_all | solution.py:215
  24.4 1.2 copy-start
  30.7 21.6 %copy-start.1 = (bf16[8,512,64]{1,2,0:T(8,128)(2,1)S(1)}, bf16[8,512,64]{1,2,0:T(8,128)(2,1)}, u32[]{:S(2)}) copy-start(bf16[8,512,64]{1,2,0:T(8,128)(2,1)} %param.11) | copy-start | bytes 1572868
  53.1 1.3 %collective-permute-start.2 = (bf16[256,128]{1,0:T(8,128)(2,1)S(1)}, bf16[256,128]{1,0:T(8,128)(2,1)S(1)}, u32[]{:S(2)}, u32[]{:S(2)}) collective-permute-start(bf16[256,128]{1,0:T(8,128)(2,1)S(1)} %get-tuple-element.43), channel_id=1, source_target_pairs={{0,32},{32,0},{64,96},{96,64},{128,160},{160,128},{192,224},{224,1... | collective-permute-start | bytes 196616 | tf_op jit(solution)/shard_map/ppermute | solution.py:320
  54.4 5.6 %collective-permute-start.5 = (bf16[256,128]{1,0:T(8,128)(2,1)S(1)}, bf16[256,128]{1,0:T(8,128)(2,1)S(1)}, u32[]{:S(2)}, u32[]{:S(2)}) collective-permute-start(bf16[256,128]{1,0:T(8,128)(2,1)S(1)} %sum_low.2.refs_0_), channel_id=1, source_target_pairs={{0,192},{32,224},{64,128},{96,160},{128,64},{160,96},{192,0},{224,... | collective-permute-start | bytes 196616 | tf_op jit(solution)/shard_map/ppermute | solution.py:321
  55.0 5.0 %collective-permute-start.4 = (bf16[256,128]{1,0:T(8,128)(2,1)S(1)}, bf16[256,128]{1,0:T(8,128)(2,1)S(1)}, u32[]{:S(2)}, u32[]{:S(2)}) collective-permute-start(bf16[256,128]{1,0:T(8,128)(2,1)S(1)} %sum_low.2.refs_0_), channel_id=1, source_target_pairs={{0,64},{32,96},{64,0},{96,32},{128,192},{160,224},{192,128},{224,1... | collective-permute-start | bytes 196616 | tf_op jit(solution)/shard_map/ppermute | solution.py:321
  55.9 6.6 %collective-permute-start.3 = (bf16[256,128]{1,0:T(8,128)(2,1)S(1)}, bf16[256,128]{1,0:T(8,128)(2,1)S(1)}, u32[]{:S(2)}, u32[]{:S(2)}) collective-permute-start(bf16[256,128]{1,0:T(8,128)(2,1)S(1)} %sum_low.2.refs_0_), channel_id=1, source_target_pairs={{0,128},{32,160},{64,192},{96,224},{128,0},{160,32},{192,64},{224,... | collective-permute-start | bytes 196616 | tf_op jit(solution)/shard_map/ppermute | solution.py:321
  62.5 1.7 %collective-permute-start.6 = (bf16[256,128]{1,0:T(8,128)(2,1)S(1)}, bf16[256,128]{1,0:T(8,128)(2,1)S(1)}, u32[]{:S(2)}, u32[]{:S(2)}) collective-permute-start(bf16[256,128]{1,0:T(8,128)(2,1)S(1)} %sum_low.3.low_ref), channel_id=1, source_target_pairs={{0,32},{32,0},{64,96},{96,64},{128,160},{160,128},{192,224},{224,1... | collective-permute-start | bytes 196616 | tf_op jit(solution)/shard_map/ppermute | solution.py:322
  65.8 20.4 %copy-start.6 = (bf16[256,1024]{1,0:T(8,128)(2,1)S(1)}, bf16[256,1024]{1,0:T(8,128)(2,1)}, u32[]{:S(2)}) copy-start(bf16[256,1024]{1,0:T(8,128)(2,1)} %get-tuple-element.52) | copy-start | bytes 1572868
  65.8 22.0 %copy-start.5 = (bf16[256,1024]{1,0:T(8,128)(2,1)S(1)}, bf16[256,1024]{1,0:T(8,128)(2,1)}, u32[]{:S(2)}) copy-start(bf16[256,1024]{1,0:T(8,128)(2,1)} %get-tuple-element.55) | copy-start | bytes 1572868
  65.8 55.8 %all-to-all-start.1 = ((bf16[32,32,1024]{2,1,0:T(8,128)(2,1)}), bf16[32,32,1024]{2,1,0:T(8,128)(2,1)S(1)}, u32[]{:S(2)}, u32[]{:S(2)}) async-start(bf16[32,32,1024]{2,1,0:T(8,128)(2,1)} %bitcast.14), calls=%async_computation.1 | async-start | bytes 4194304 | tf_op jit(solution)/shard_map/all_to_all | solution.py:340
  71.1 18.2 %copy-start.4 = (s32[1,32]{1,0:T(1,128)S(1)}, s32[1,32]{1,0:T(1,128)}, u32[]{:S(2)}) copy-start(s32[1,32]{1,0:T(1,128)} %len_ref.3) | copy-start | bytes 388
  71.1 15.1 %collective-permute-start.8 = (bf16[256,1024]{1,0:T(8,128)(2,1)}, bf16[256,1024]{1,0:T(8,128)(2,1)S(1)}, u32[]{:S(2)}, u32[]{:S(2)}) collective-permute-start(bf16[256,1024]{1,0:T(8,128)(2,1)} %get-tuple-element.36), channel_id=1, source_target_pairs={{0,64},{32,96},{64,0},{96,32},{128,192},{160,224},{192,128},{224,1... | collective-permute-start | bytes 1572872 | tf_op jit(solution)/shard_map/ppermute | solution.py:267
  71.5 16.3 %collective-permute-start.11 = (bf16[256,1024]{1,0:T(8,128)(2,1)}, bf16[256,1024]{1,0:T(8,128)(2,1)S(1)}, u32[]{:S(2)}, u32[]{:S(2)}) collective-permute-start(bf16[256,1024]{1,0:T(8,128)(2,1)} %get-tuple-element.56), channel_id=1, source_target_pairs={{0,192},{32,224},{64,128},{96,160},{128,64},{160,96},{192,0},{224,... | collective-permute-start | bytes 1572872 | tf_op jit(solution)/shard_map/ppermute | solution.py:268
  74.2 23.3 %collective-permute-start.7 = (bf16[256,1024]{1,0:T(8,128)(2,1)}, bf16[256,1024]{1,0:T(8,128)(2,1)}, u32[]{:S(2)}, u32[]{:S(2)}) collective-permute-start(bf16[256,1024]{1,0:T(8,128)(2,1)} %get-tuple-element.51), channel_id=1, source_target_pairs={{0,64},{32,96},{64,0},{96,32},{128,192},{160,224},{192,128},{224,1... | collective-permute-start | bytes 1572872 | tf_op jit(solution)/shard_map/ppermute | solution.py:356
  74.3 24.8 %collective-permute-start.10 = (bf16[256,1024]{1,0:T(8,128)(2,1)}, bf16[256,1024]{1,0:T(8,128)(2,1)}, u32[]{:S(2)}, u32[]{:S(2)}) collective-permute-start(bf16[256,1024]{1,0:T(8,128)(2,1)} %get-tuple-element.54), channel_id=1, source_target_pairs={{0,192},{32,224},{64,128},{96,160},{128,64},{160,96},{192,0},{224,... | collective-permute-start | bytes 1572872 | tf_op jit(solution)/shard_map/ppermute | solution.py:357
  86.4 22.9 %collective-permute-start.9 = (bf16[256,1024]{1,0:T(8,128)(2,1)S(1)}, bf16[256,1024]{1,0:T(8,128)(2,1)}, u32[]{:S(2)}, u32[]{:S(2)}) collective-permute-start(bf16[256,1024]{1,0:T(8,128)(2,1)S(1)} %add_convert_fusion.1), channel_id=1, source_target_pairs={{0,192},{32,224},{64,128},{96,160},{128,64},{160,96},{192,0},{224,... | collective-permute-start | bytes 1572872 | tf_op jit(solution)/shard_map/ppermute | solution.py:354
  88.0 21.4 %collective-permute-start.12 = (bf16[256,1024]{1,0:T(8,128)(2,1)S(1)}, bf16[256,1024]{1,0:T(8,128)(2,1)}, u32[]{:S(2)}, u32[]{:S(2)}) collective-permute-start(bf16[256,1024]{1,0:T(8,128)(2,1)S(1)} %add_convert_fusion), channel_id=1, source_target_pairs={{0,64},{32,96},{64,0},{96,32},{128,192},{160,224},{192,128},{224,1... | collective-permute-start | bytes 1572872 | tf_op jit(solution)/shard_map/ppermute | solution.py:355

commit v6 on v5

--- a/solution.py
+++ b/solution.py
@@ -24,9 +24,7 @@
     return pl.CostEstimate(flops=int(flops), transcendentals=0, bytes_accessed=int(nbytes))
 
 
-def pack_kernel(me_ref, len_ref, id_ref, slot_ref, x_ref, out_ref, x_buf, sel_ref, o_buf, x_sem, o_sem, *, pool, most):
-    fetch = pltpu.make_async_copy(x_ref, x_buf, x_sem)
-    fetch.start()
+def pack_kernel(me_ref, len_ref, id_ref, slot_ref, x_ref, out_ref, sel_ref, *, pool, most):
     requests = len_ref.shape[1]
     tokens = x_ref.shape[0]
     rows = lax.broadcasted_iota(jnp.int32, (most, tokens), 0)
@@ -38,38 +36,19 @@
         at = pl.multiple_of(owner * most, most)
         sel_ref[pl.ds(at, most), :] = jnp.where(ahead == start, 1.0, 0.0).astype(BF)
         start = start + len_ref[0, r]
-    fetch.wait()
-    n = out_ref.shape[0] // PARTS
-    leaving = []
-    for i in range(PARTS):
-        at = pl.ds(i * n, n)
-        o_buf[at, :] = jnp.dot(sel_ref[at, :], x_buf[...], preferred_element_type=F32).astype(BF)
-        leaving.append(pltpu.make_async_copy(o_buf.at[at], out_ref.at[at], o_sem.at[i]))
-        leaving[-1].start()
-    for copy in leaving:
-        copy.wait()
-
-
-def unpack_matrix_kernel(me_ref, len_ref, id_ref, slot_ref, sel_ref, *, pool, most):
-    requests = len_ref.shape[1]
-    tokens = sel_ref.shape[0]
-    lanes = 128
-    per = lanes // most
-    tok = lax.broadcasted_iota(jnp.int32, (tokens, lanes), 0)
-    lane = lax.broadcasted_iota(jnp.int32, (tokens, lanes), 1)
-    behind = tok - lane
-    sel_ref[...] = jnp.zeros_like(sel_ref)
+    out_ref[...] = jnp.dot(sel_ref[...], x_ref[...], preferred_element_type=F32).astype(BF)
+
+
+def unpack_index_kernel(me_ref, len_ref, id_ref, slot_ref, out_ref, *, pool, most):
+    tok = lax.broadcasted_iota(jnp.int32, out_ref.shape, 0)
     me = me_ref[0]
     start = jnp.int32(0)
-    for r in range(requests):
+    shift = jnp.zeros(out_ref.shape, jnp.int32)
+    for r in range(len_ref.shape[1]):
         owner = lax.div(slot_ref[id_ref[me, r]], jnp.int32(pool))
-        count = len_ref[0, r]
-        block = lax.div(owner, jnp.int32(per))
-        off = (owner - block * per) * most
-        hit = (behind == start - off) & (tok >= start) & (tok < start + count)
-        at = pl.ds(pl.multiple_of(block * lanes, lanes), lanes)
-        sel_ref[:, at] = sel_ref[:, at] + jnp.where(hit, 1.0, 0.0).astype(BF)
-        start = start + count
+        shift = jnp.where(tok >= start, owner * most - start, shift)
+        start = start + len_ref[0, r]
+    out_ref[...] = tok + shift
 
 
 def down_kernel(core_ref, code_ref, x_ref, d_ref, keep_ref, send_ref, *, pool):
@@ -126,8 +105,9 @@
 
 def own_dot_kernel(t_ref, x_ref, w_ref, p_ref, a0_ref, b0_ref, a1_ref, b1_ref):
     half = x_ref.shape[0] // 2
-    both = (jnp.dot(x_ref[...], w_ref[...], preferred_element_type=F32) + p_ref[0].astype(F32)).astype(BF)
     j = pl.program_id(0)
+    came = p_ref[j if p_ref.shape[0] > 1 else 0].astype(F32)
+    both = (jnp.dot(x_ref[...], w_ref[...], preferred_element_type=F32) + came).astype(BF)
 
     @pl.when(j == 0)
     def _():
@@ -140,28 +120,50 @@
         b1_ref[...] = both[half:]
 
 
-def before_kernel(res_ref, ka_ref, ra_ref, za_ref, kb_ref, rb_ref, zb_ref, out_ref):
-    half = res_ref.shape[0] // 2
+def before_kernel(res_ref, ka_ref, ra_ref, za_ref, kb_ref, rb_ref, zb_ref, left_ref, right_ref):
+    half = ka_ref.shape[0]
+    wide = left_ref.shape[1]
     base_a = ka_ref[...].astype(F32) + ra_ref[...].astype(F32) + za_ref[...].astype(F32)
     base_b = kb_ref[...].astype(F32) + rb_ref[...].astype(F32) + zb_ref[...].astype(F32)
-    out_ref[:half] = res_ref[:half].astype(F32) + base_a
-    out_ref[half:] = res_ref[half:].astype(F32) + base_b
-
-
-def final_kernel(sel_ref, ret_ref, pre_ref, out_ref, p_buf, o_buf, p_sem, o_sem):
+    top = res_ref[:half].astype(F32) + base_a
+    low = res_ref[half:].astype(F32) + base_b
+    left_ref[:half] = top[:, :wide]
+    left_ref[half:] = low[:, :wide]
+    right_ref[:half] = top[:, wide:]
+    right_ref[half:] = low[:, wide:]
+
+
+def final_kernel(row_ref, ret_ref, left_ref, right_ref, out_ref, sel_ref, p_buf, o_buf, p_sem, o_sem):
     n = out_ref.shape[1] // PARTS
+    near_parts = left_ref.shape[1] // n
     at = [pl.ds(i * n, n) for i in range(PARTS)]
-    coming = [pltpu.make_async_copy(pre_ref.at[:, at[i]], p_buf.at[i], p_sem.at[i]) for i in range(PARTS)]
+    coming = [
+        pltpu.make_async_copy(right_ref.at[:, at[i]], p_buf.at[i], p_sem.at[i]) for i in range(PARTS - near_parts)
+    ]
     leaving = [pltpu.make_async_copy(o_buf.at[i], out_ref.at[:, at[i]], o_sem.at[i]) for i in range(PARTS)]
     for copy in coming:
         copy.start()
+    lanes = row_ref.shape[1]
+    row = row_ref[...] - lax.broadcasted_iota(jnp.int32, row_ref.shape, 1)
+    for k in range(sel_ref.shape[1] // lanes):
+        sel_ref[:, k * lanes:(k + 1) * lanes] = jnp.where(row == k * lanes, 1.0, 0.0).astype(BF)
     for i in range(PARTS):
         delta = jnp.dot(sel_ref[...], ret_ref[:, at[i]], preferred_element_type=F32)
-        coming[i].wait()
-        o_buf[i] = (p_buf[i] + delta).astype(BF)
+        if i < near_parts:
+            pre = left_ref[:, at[i]]
+        else:
+            coming[i - near_parts].wait()
+            pre = p_buf[i - near_parts]
+        o_buf[i] = (pre + delta).astype(BF)
         leaving[i].start()
     for copy in leaving:
         copy.wait()
+
+
+def fetch_kernel(x_ref, out_ref, sem):
+    copy = pltpu.make_async_copy(x_ref, out_ref, sem)
+    copy.start()
+    copy.wait()
 
 
 def sum_kernel(*refs):
@@ -171,12 +173,12 @@
     refs[-1][...] = acc.astype(BF)
 
 
-def copy_kernel(x_ref, out_ref):
-    out_ref[...] = x_ref[...]
-
-
 def near(v):
     return pltpu.with_memory_space_constraint(v, pltpu.VMEM)
+
+
+def far(v):
+    return pltpu.with_memory_space_constraint(v, pltpu.HBM)
 
 
 def one_block(x, residual, weight, down, up, pool_slot, req_id, req_len):
@@ -200,15 +202,9 @@
     outgoing = pl.pallas_call(
         functools.partial(pack_kernel, pool=pool, most=most),
         out_shape=sds((slots, features), BF),
-        in_specs=[SM, SM, SM, SM, HB],
-        out_specs=HB,
-        scratch_shapes=[
-            pltpu.VMEM((tokens, features), BF),
-            pltpu.VMEM((slots, tokens), BF),
-            pltpu.VMEM((slots, features), BF),
-            DMA,
-            DMA((PARTS,)),
-        ],
+        in_specs=[SM, SM, SM, SM, VM],
+        out_specs=VM,
+        scratch_shapes=[pltpu.VMEM((slots, tokens), BF)],
         cost_estimate=cost(2 * slots * tokens * features, 2 * (slots + tokens) * features),
         name="pack",
     )(me1, req_len, req_id, pool_slot, x)
@@ -234,7 +230,7 @@
             name="pair_dot",
         )(t1, x, weight)
 
-        def own(x, came):
+        def own(x, came, close):
             piece = sds((half, cols), BF)
             keep = pl.BlockSpec((half, cols), lambda j, t_ref: (0, 0))
             return pl.pallas_call(
@@ -246,13 +242,13 @@
                     in_specs=[
                         whole,
                         pl.BlockSpec((features, cols), lambda j, t_ref: (0, t_ref[0] ^ (2 * order(j)))),
-                        pl.BlockSpec((1, tokens, cols), lambda j, t_ref: (j, 0, 0)),
+                        VM if close else pl.BlockSpec((1, tokens, cols), lambda j, t_ref: (j, 0, 0)),
                     ],
                     out_specs=[keep] * 4,
                 ),
                 cost_estimate=cost(flops, 2 * n * cols * (2 * tokens + features)),
                 name="own_dot",
-            )(t1, x, weight, came)
+            )(t1, x, weight, near(came) if close else came)
 
         return out, own
 
@@ -263,32 +259,32 @@
     to_2, own_2 = parts((3, 0), x)
     from_2 = lax.ppermute(to_2, "tensor", xor(1))
     x, _ = lax.optimization_barrier((x, to_2))
-    s2a, s2b, s1a, k1b = own_1(x, from_1)
+    s2a, s2b, s1a, k1b = own_1(x, from_1, True)
     r2a = lax.ppermute(s2a, "tensor", xor(2))
     r2b = lax.ppermute(s2b, "tensor", xor(6))
-    x, _ = lax.optimization_barrier((x, s2a))
-    k3a, s3b, k0a, k0b = own_2(x, from_2)
+    x, req_id2, pool_slot2, up, _ = lax.optimization_barrier((x, req_id, pool_slot, up, s2a))
 
     ids = jnp.arange(pool_slot.shape[0], dtype=jnp.int32)
     held = me * pool + jnp.arange(pool, dtype=jnp.int32)
-    id_of = jnp.sum(jnp.where(pool_slot[None, :] == held[:, None], ids[None, :], 0), 1)
-    uses = req_id[:, :, None] == id_of[None, None, :]
+    id_of = jnp.sum(jnp.where(pool_slot2[None, :] == held[:, None], ids[None, :], 0), 1)
+    uses = req_id2[:, :, None] == id_of[None, None, :]
     idx = jnp.sum(jnp.where(uses, jnp.arange(pool, dtype=jnp.int32), 0), (1, 2))
     lane = jnp.arange(2 * rank, dtype=jnp.int32)
     code = jnp.broadcast_to(idx[:, None, None], (groups, most, 2 * rank)) - jnp.where(lane < rank, 0, 1)
     code = code.reshape(slots, 2 * rank)
 
     up_maps = pl.pallas_call(
-        copy_kernel,
+        fetch_kernel,
         out_shape=pltpu.VMEM((pool * rank, cols), BF),
-        in_specs=[VM],
+        in_specs=[HB],
         out_specs=VM,
+        scratch_shapes=[DMA],
         cost_estimate=cost(0, 4 * pool * rank * cols),
         name="fetch_up",
         compiler_params=SMALL,
-    )(up.reshape(pool * rank, cols))
-
-    arrived, code, up_maps, k0a, s3b = lax.optimization_barrier((arrived, code, up_maps, k0a, s3b))
+    )(far(up.reshape(pool * rank, cols)))
+
+    arrived, code, up_maps = lax.optimization_barrier((arrived, code, up_maps))
     code = near(code)
     core = t1 & 1
     piece = pltpu.VMEM((slots // 4, 2 * rank), BF)
@@ -318,7 +314,10 @@
         )(*[near(v) for v in terms])
 
     low = total(low, lax.ppermute(send, "tensor", xor(1)))
-    low = total(low, *[lax.ppermute(low, "tensor", xor(m)) for m in (4, 2, 6)])
+    came = []
+    for m in (4, 2, 6):
+        came.append(lax.ppermute(low, "tensor", xor(m)))
+    low = total(low, *came)
     other = lax.ppermute(low, "tensor", xor(1))
 
     def lift(rows_low, flip, filled=()):
@@ -336,54 +335,53 @@
 
     raised = lift(low, 0)
     raised = lift(other, 1, (raised,))
-    raised, s1a, s3b, k3a, k1b, me1 = lax.optimization_barrier((raised, s1a, s3b, k3a, k1b, me1))
+    raised, s1a, k1b, x, me1 = lax.optimization_barrier((raised, s1a, k1b, x, me1))
     returned = lax.all_to_all(
         raised.reshape(groups, most, cols), "req", split_axis=0, concat_axis=0, tiled=True
     )
 
-    sel = pl.pallas_call(
-        functools.partial(unpack_matrix_kernel, pool=pool, most=most),
-        out_shape=pltpu.VMEM((tokens, slots), BF),
+    row = pl.pallas_call(
+        functools.partial(unpack_index_kernel, pool=pool, most=most),
+        out_shape=pltpu.VMEM((tokens, 128), jnp.int32),
         in_specs=[SM, SM, SM, SM],
         out_specs=VM,
-        cost_estimate=cost(8 * slots * tokens, 2 * slots * tokens),
-        name="unpack_matrix",
+        cost_estimate=cost(64 * 128 * tokens, 4 * 128 * tokens),
+        name="unpack_index",
     compiler_params=SMALL,
     )(me1, req_len, req_id, pool_slot)
 
+    k3a, s3b, k0a, k0b = own_2(x, from_2, False)
     za = lax.ppermute((k3a.astype(F32) + r2a.astype(F32)).astype(BF), "tensor", xor(6))
     zb = lax.ppermute((k1b.astype(F32) + r2b.astype(F32)).astype(BF), "tensor", xor(2))
     r1a = lax.ppermute(s1a, "tensor", xor(2))
     r3b = lax.ppermute(s3b, "tensor", xor(6))
 
-    wide = cols // 4
-    flat = pl.BlockSpec((half, wide), lambda i: (0, i))
-    tall = pl.BlockSpec((tokens, wide), lambda i: (0, i))
-    pre = pl.pallas_call(
+    wide = cols // PARTS
+    left, right = pl.pallas_call(
         before_kernel,
-        out_shape=pltpu.HBM((tokens, cols), F32),
-        grid=(4,),
-        in_specs=[tall] + [flat] * 6,
-        out_specs=tall,
+        out_shape=[pltpu.VMEM((tokens, 2 * wide), F32), pltpu.HBM((tokens, cols - 2 * wide), F32)],
+        in_specs=[VM] * 7,
+        out_specs=[VM, VM],
         cost_estimate=cost(4 * tokens * cols, 12 * tokens * cols),
         name="before",
-    )(residual, k0a, r1a, za, k0b, r3b, zb)
-    returned, pre, sel = lax.optimization_barrier((returned, pre, sel))
+    )(residual, *[far(v) for v in (k0a, r1a, za, k0b, r3b, zb)])
+    returned, left, right, row = lax.optimization_barrier((returned, left, right, row))
     return pl.pallas_call(
         final_kernel,
         out_shape=sds((tokens, cols), BF),
-        in_specs=[VM, VM, HB],
+        in_specs=[VM, VM, VM, HB],
         out_specs=HB,
         scratch_shapes=[
-            pltpu.VMEM((PARTS, tokens, cols // PARTS), F32),
-            pltpu.VMEM((PARTS, tokens, cols // PARTS), BF),
-            DMA((PARTS,)),
+            pltpu.VMEM((tokens, slots), BF),
+            pltpu.VMEM((PARTS - 2, tokens, wide), F32),
+            pltpu.VMEM((PARTS, tokens, wide), BF),
+            DMA((PARTS - 2,)),
             DMA((PARTS,)),
         ],
         cost_estimate=cost(2 * tokens * slots * cols, 2 * cols * (slots + 4 * tokens)),
         name="final",
-        compiler_params=pltpu.CompilerParams(vmem_limit_bytes=59 * 2**20),
-    )(near(sel), near(returned.reshape(slots, cols)), pre)
+        compiler_params=pltpu.CompilerParams(vmem_limit_bytes=56 * 2**20),
+    )(near(row), near(returned.reshape(slots, cols)), near(left), right)
 
 
 def solution(mesh):

time: 128 us -> 121 us (0.945)
  Pallas kernels: 39 us -> 32.6 us
  waiting for transfers between devices: 54 us -> 52.7 us
    ppermute x1, waiting for transfers between devices: 10.3 us -> 3.68 us  [one_block(): r2a = lax.ppermute(s2a, 'tensor', xor(2))]
    ppermute x1, waiting for transfers between devices: 1.53 us -> 6.73 us  [one_block(): r3b = lax.ppermute(s3b, 'tensor', xor(6))]
    pallas_call x3, Pallas kernels: 10.1 us -> 6.29 us  [the longest x1 3.38 us: one_block(): pl.pallas_call(before_kernel, out_shape=[pltpu.VMEM((tokens, 2 * wide), F...]
    ppermute x1, waiting for transfers between devices: 2.75 us -> 0.01 us  [one_block(): r1a = lax.ppermute(s1a, 'tensor', xor(2))]
    all_to_all x1, waiting for transfers between devices: 16.8 us -> 18.4 us  [one_block(): lax.all_to_all(outgoing.reshape(groups, most, features), 'req', split_axi...]
    pallas_call x1, Pallas kernels: 4.02 us -> 2.74 us  [one_block(): pl.pallas_call(final_kernel, out_shape=sds((tokens, cols), BF), in_specs=...]
  transfers between devices with their start and end apart: 15 -> 15, of which waited for: 9 -> 9; matrix products, arithmetic and copies ran while one was open for 1% -> 2% of each run, Pallas kernels for 20% -> 17%
where the time goes in v6:
time: 121 us; the launch traced here: 120 us
  waiting for transfers between devices  52.7 us (44%)
  Pallas kernels  32.6 us (27%)
  starting transfers between devices  30.1 us (25%)
  other arithmetic  2.7 us (2%)
    all_to_all x1, waiting for transfers between devices, one_block(): lax.all_to_all(outgoing.reshape(groups, most, features), 'req', split_axi...  18.4 us
    all_to_all x1, starting transfers between devices, one_block(): lax.all_to_all(outgoing.reshape(groups, most, features), 'req', split_axi...  11.5 us
    ppermute x1, waiting for transfers between devices, one_block(): lax.ppermute((k3a.astype(F32) + r2a.astype(F32)).astype(BF), 'tensor', xo...  10.3 us
    pallas_call x2, Pallas kernels, own(): pl.pallas_call(own_dot_kernel, out_shape=[piece] * 4, grid_spec=pltpu.Pre...  9.06 us
    all_to_all x1, waiting for transfers between devices, one_block(): lax.all_to_all(raised.reshape(groups, most, cols), 'req', split_axis=0, c...  7.84 us
    pallas_call x2, Pallas kernels, parts(): pl.pallas_call(pair_dot_kernel, out_shape=sds((n, tokens, cols), BF), gri...  7.59 us
    ppermute x1, waiting for transfers between devices, one_block(): r3b = lax.ppermute(s3b, 'tensor', xor(6))  6.73 us
    all_to_all x1, starting transfers between devices, one_block(): lax.all_to_all(raised.reshape(groups, most, cols), 'req', split_axis=0, c...  5.2 us
  transfers between devices with their start and end apart: 15, of which 9 were waited for; matrix products, arithmetic and copies ran while one was open for 2% of the time, Pallas kernels for 17%

profile of v6, /device:TPU:6, one launch (start us, length us, event | category | flops | bytes accessed | tf_op | source)
XLA Modules:
  0.0 119.6 jit_solution(14201482720777652277)
XLA Ops:
  0.0 2.9 %pack.1 = bf16[1024,512]{1,0:T(8,128)(2,1)} custom-call(s32[1]{0:T(128)} %bitcast.1.me_ref, s32[1,32]{1,0:T(1,128)} %len_ref.3, s32[32,32]{1,0:T(8,128)} %id_ref.3, s32[256]{0:T(256)} %slot_ref.3, bf16[512,512]{1,0:T(8,128)(2,1)} %x_ref.5), custom_call_target="tpu_custom_call" | custom-call | flops 536870912 | bytes 1572864 | tf_op jit(solution)/shard_map/pack/pallas_call | solution.py:202
  2.9 3.8 %pair_dot.2 = bf16[2,512,1024]{2,1,0:T(8,128)(2,1)} custom-call(s32[1]{0:T(128)} %bitcast.t_ref, bf16[512,512]{1,0:T(8,128)(2,1)} %x_ref.5, bf16[512,8192]{1,0:T(8,128)(2,1)} %w_ref.7), custom_call_target="tpu_custom_call" | custom-call | flops 1073741824 | bytes 4194304 | tf_op jit(solution)/shard_map/pair_dot/pallas_call | solution.py:220
  6.7 11.5 %all-to-all-start = ((bf16[32,32,512]{2,1,0:T(8,128)(2,1)}), bf16[32,32,512]{2,1,0:T(8,128)(2,1)S(1)}, u32[]{:S(2)}, u32[]{:S(2)}) async-start(bf16[32,32,512]{2,1,0:T(8,128)(2,1)} %bitcast.15), calls=%async_computation | async-start | bytes 2097152 | tf_op jit(solution)/shard_map/all_to_all | solution.py:211
  18.2 3.8 %pair_dot.3 = bf16[2,512,1024]{2,1,0:T(8,128)(2,1)} custom-call(s32[1]{0:T(128)} %bitcast.t_ref, bf16[512,512]{1,0:T(8,128)(2,1)} %x_ref.5, bf16[512,8192]{1,0:T(8,128)(2,1)} %w_ref.7), custom_call_target="tpu_custom_call" | custom-call | flops 1073741824 | bytes 4194304 | tf_op jit(solution)/shard_map/pair_dot/pallas_call | solution.py:220
  22.0 4.4 %own_dot.2 = (bf16[256,1024]{1,0:T(8,128)(2,1)}, bf16[256,1024]{1,0:T(8,128)(2,1)}, bf16[256,1024]{1,0:T(8,128)(2,1)}, bf16[256,1024]{1,0:T(8,128)(2,1)}) custom-call(s32[1]{0:T(128)} %bitcast.t_ref, bf16[512,512]{1,0:T(8,128)(2,1)} %x_ref.5, bf16[512,8192]{1,0:T(8,128)(2,1)} %w_ref.7, bf16[2,512,1024]{2,1,0:T(8,128)(2,1)S(1)} %collective-permute-done.p_ref), custom_call_target="tpu_custom_call" | custom-call | flops 1073741824 | bytes 6291456 | tf_op jit(solution)/shard_map/own_dot/pallas_call | solution.py:236
  27.5 1.2 %fetch_up.1.u_ref = bf16[512,1024]{1,0:T(8,128)(2,1)S(1)} custom-call(bf16[512,1024]{1,0:T(8,128)(2,1)} %bitcast.14), custom_call_target="tpu_custom_call" | custom-call | bytes 2097152 | tf_op jit(solution)/shard_map/fetch_up/pallas_call | solution.py:276
  28.9 18.4 %all-to-all-done = bf16[32,32,512]{2,1,0:T(8,128)(2,1)S(1)} async-done(((bf16[32,32,512]{2,1,0:T(8,128)(2,1)}), bf16[32,32,512]{2,1,0:T(8,128)(2,1)S(1)}, u32[]{:S(2)}, u32[]{:S(2)}) %all-to-all-start) | async-done | bytes 1048608 | tf_op jit(solution)/shard_map/all_to_all | solution.py:211
  47.4 0.8 down.1
  48.3 1.2 %collective-permute-done.1.refs_1_ = bf16[256,128]{1,0:T(8,128)(2,1)S(1)} collective-permute-done((bf16[256,128]{1,0:T(8,128)(2,1)S(1)}, bf16[256,128]{1,0:T(8,128)(2,1)S(1)}, u32[]{:S(2)}, u32[]{:S(2)}) %collective-permute-start.1) | collective-permute-done | bytes 65568 | tf_op jit(solution)/shard_map/ppermute | solution.py:316
  50.1 0.9 collective-permute-start.3
  51.0 3.3 %collective-permute-start.2 = (bf16[256,128]{1,0:T(8,128)(2,1)S(1)}, bf16[256,128]{1,0:T(8,128)(2,1)S(1)}, u32[]{:S(2)}, u32[]{:S(2)}) collective-permute-start(bf16[256,128]{1,0:T(8,128)(2,1)S(1)} %sum_low.2.refs_0_), channel_id=1, source_target_pairs={{0,128},{32,160},{64,192},{96,224},{128,0},{160,32},{192,64},{224,... | collective-permute-start | bytes 196616 | tf_op jit(solution)/shard_map/ppermute | solution.py:319
  54.3 0.8 collective-permute-done.4.refs_3_
  55.1 2.5 %collective-permute-done.2.refs_1_ = bf16[256,128]{1,0:T(8,128)(2,1)S(1)} collective-permute-done((bf16[256,128]{1,0:T(8,128)(2,1)S(1)}, bf16[256,128]{1,0:T(8,128)(2,1)S(1)}, u32[]{:S(2)}, u32[]{:S(2)}) %collective-permute-start.2) | collective-permute-done | bytes 65568 | tf_op jit(solution)/shard_map/ppermute | solution.py:319
  57.7 1.6 %up.2.rest_0_ = bf16[1024,1024]{1,0:T(8,128)(2,1)} custom-call(s32[1]{0:T(128)S(6)} %and.5.core_ref, s32[1024,128]{1,0:T(8,128)S(1)} %broadcast_subtract_fusion.code_ref, bf16[256,128]{1,0:T(8,128)(2,1)S(1)} %sum_low.3.low_ref, bf16[512,1024]{1,0:T(8,128)(2,1)S(1)} %fetch_up.1.u_ref), custom_call_target="tpu_custom_call" | custom-call | flops 536870912 | bytes 1048576 | tf_op jit(solution)/shard_map/up/pallas_call | solution.py:324
  59.3 1.6 %up.3 = bf16[1024,1024]{1,0:T(8,128)(2,1)} custom-call(s32[1]{0:T(128)S(6)} %and.5.core_ref, s32[1024,128]{1,0:T(8,128)S(1)} %broadcast_subtract_fusion.code_ref, bf16[256,128]{1,0:T(8,128)(2,1)S(1)} %collective-permute-done.5.low_ref, bf16[512,1024]{1,0:T(8,128)(2,1)S(1)} %fetch_up.1.u_ref, ...), custom_call_target="tpu_custom_call", output_to_operand_aliasing={{}: (4, {})} | custom-call | flops 536870912 | bytes 1048576 | tf_op jit(solution)/shard_map/up/pallas_call | solution.py:324
  60.9 5.2 %all-to-all-start.1 = ((bf16[32,32,1024]{2,1,0:T(8,128)(2,1)}), bf16[32,32,1024]{2,1,0:T(8,128)(2,1)S(1)}, u32[]{:S(2)}, u32[]{:S(2)}) async-start(bf16[32,32,1024]{2,1,0:T(8,128)(2,1)} %bitcast.13), calls=%async_computation.1 | async-start | bytes 4194304 | tf_op jit(solution)/shard_map/all_to_all | solution.py:339
  66.8 2.8 %collective-permute-start.11 = (bf16[256,1024]{1,0:T(8,128)(2,1)}, bf16[256,1024]{1,0:T(8,128)(2,1)S(1)}, u32[]{:S(2)}, u32[]{:S(2)}) collective-permute-start(bf16[256,1024]{1,0:T(8,128)(2,1)} %get-tuple-element.59), channel_id=1, source_target_pairs={{0,192},{32,224},{64,128},{96,160},{128,64},{160,96},{192,0},{224,... | collective-permute-start | bytes 1572872 | tf_op jit(solution)/shard_map/ppermute | solution.py:264
  69.5 1.2 %collective-permute-done.6.p_ref = bf16[2,512,1024]{2,1,0:T(8,128)(2,1)} collective-permute-done((bf16[2,512,1024]{2,1,0:T(8,128)(2,1)}, bf16[2,512,1024]{2,1,0:T(8,128)(2,1)}, u32[]{:S(2)}, u32[]{:S(2)}) %collective-permute-start.6) | collective-permute-done | bytes 2097184 | tf_op jit(solution)/shard_map/ppermute | solution.py:260
  70.7 4.7 %own_dot.3 = (bf16[256,1024]{1,0:T(8,128)(2,1)}, bf16[256,1024]{1,0:T(8,128)(2,1)}, bf16[256,1024]{1,0:T(8,128)(2,1)}, bf16[256,1024]{1,0:T(8,128)(2,1)}) custom-call(s32[1]{0:T(128)} %bitcast.t_ref, bf16[512,512]{1,0:T(8,128)(2,1)} %x_ref.5, bf16[512,8192]{1,0:T(8,128)(2,1)} %w_ref.7, bf16[2,512,1024]{2,1,0:T(8,128)(2,1)} %collective-permute-done.6.p_ref), custom_call_target="tpu_custom_call" | custom-call | flops 1073741824 | bytes 6291456 | tf_op jit(solution)/shard_map/own_dot/pallas_call | solution.py:236
  75.4 1.3 %collective-permute-start.10 = (bf16[256,1024]{1,0:T(8,128)(2,1)}, bf16[256,1024]{1,0:T(8,128)(2,1)S(1)}, u32[]{:S(2)}, u32[]{:S(2)}) collective-permute-start(bf16[256,1024]{1,0:T(8,128)(2,1)} %get-tuple-element.57), channel_id=1, source_target_pairs={{0,192},{32,224},{64,128},{96,160},{128,64},{160,96},{192,0},{224,... | collective-permute-start | bytes 1572872 | tf_op jit(solution)/shard_map/ppermute | solution.py:357
  76.7 1.2 %collective-permute-start.7 = (bf16[256,1024]{1,0:T(8,128)(2,1)}, bf16[256,1024]{1,0:T(8,128)(2,1)S(1)}, u32[]{:S(2)}, u32[]{:S(2)}) collective-permute-start(bf16[256,1024]{1,0:T(8,128)(2,1)} %get-tuple-element.54), channel_id=1, source_target_pairs={{0,64},{32,96},{64,0},{96,32},{128,192},{160,224},{192,128},{224,1... | collective-permute-start | bytes 1572872 | tf_op jit(solution)/shard_map/ppermute | solution.py:356
  77.9 3.7 %collective-permute-done.8 = bf16[256,1024]{1,0:T(8,128)(2,1)} collective-permute-done((bf16[256,1024]{1,0:T(8,128)(2,1)}, bf16[256,1024]{1,0:T(8,128)(2,1)}, u32[]{:S(2)}, u32[]{:S(2)}) %collective-permute-start.8) | collective-permute-done | bytes 524320 | tf_op jit(solution)/shard_map/ppermute | solution.py:263
  81.5 1.4 %add_convert_fusion.1 = bf16[256,1024]{1,0:T(8,128)(2,1)S(1)} fusion(bf16[256,1024]{1,0:T(8,128)(2,1)} %collective-permute-done.8, bf16[256,1024]{1,0:T(8,128)(2,1)} %get-tuple-element.55), kind=kLoop, calls=%fused_computation.1 | loop fusion | flops 1048576 | bytes 1572864 | tf_op jit(solution)/shard_map/convert_element_type | solution.py:354
  82.9 1.4 %collective-permute-start.9 = (bf16[256,1024]{1,0:T(8,128)(2,1)S(1)}, bf16[256,1024]{1,0:T(8,128)(2,1)S(1)}, u32[]{:S(2)}, u32[]{:S(2)}) collective-permute-start(bf16[256,1024]{1,0:T(8,128)(2,1)S(1)} %add_convert_fusion.1), channel_id=1, source_target_pairs={{0,192},{32,224},{64,128},{96,160},{128,64},{160,96},{192,0},{224,... | collective-permute-start | bytes 1572872 | tf_op jit(solution)/shard_map/ppermute | solution.py:354
  84.5 1.3 %collective-permute-start.12 = (bf16[256,1024]{1,0:T(8,128)(2,1)S(1)}, bf16[256,1024]{1,0:T(8,128)(2,1)S(1)}, u32[]{:S(2)}, u32[]{:S(2)}) collective-permute-start(bf16[256,1024]{1,0:T(8,128)(2,1)S(1)} %add_convert_fusion), channel_id=1, source_target_pairs={{0,64},{32,96},{64,0},{96,32},{128,192},{160,224},{192,128},{224,1... | collective-permute-start | bytes 1572872 | tf_op jit(solution)/shard_map/ppermute | solution.py:355
  85.8 1.7 %unpack_index.1.row_ref = s32[512,128]{1,0:T(8,128)S(1)} custom-call(s32[1]{0:T(128)} %bitcast.1.me_ref, s32[1,32]{1,0:T(1,128)S(1)} %copy-done.3, s32[32,32]{1,0:T(8,128)S(1)} %copy-done.1, s32[256]{0:T(256)S(1)} %copy-done.2), custom_call_target="tpu_custom_call" | custom-call | flops 4194304 | bytes 262144 | tf_op jit(solution)/shard_map/unpack_index/pallas_call | solution.py:343
  87.5 6.7 %collective-permute-done.10.rb_ref = bf16[256,1024]{1,0:T(8,128)(2,1)S(1)} collective-permute-done((bf16[256,1024]{1,0:T(8,128)(2,1)}, bf16[256,1024]{1,0:T(8,128)(2,1)S(1)}, u32[]{:S(2)}, u32[]{:S(2)}) %collective-permute-start.10) | collective-permute-done | bytes 524320 | tf_op jit(solution)/shard_map/ppermute | solution.py:357
  94.2 10.3 %collective-permute-done.9.za_ref = bf16[256,1024]{1,0:T(8,128)(2,1)S(1)} collective-permute-done((bf16[256,1024]{1,0:T(8,128)(2,1)S(1)}, bf16[256,1024]{1,0:T(8,128)(2,1)S(1)}, u32[]{:S(2)}, u32[]{:S(2)}) %collective-permute-start.9) | collective-permute-done | bytes 524320 | tf_op jit(solution)/shard_map/ppermute | solution.py:354
  104.5 0.8 copy-done.7
  105.5 3.4 %before.1 = (f32[512,512]{1,0:T(8,128)S(1)}, f32[512,512]{1,0:T(8,128)}) custom-call(bf16[512,1024]{1,0:T(8,128)(2,1)} %res_ref.1, bf16[256,1024]{1,0:T(8,128)(2,1)} %get-tuple-element.53.ka_ref, bf16[256,1024]{1,0:T(8,128)(2,1)} %copy-done.6, bf16[256,1024]{1,0:T(8,128)(2,1)} %copy-done.7, bf16[256,1024]{1,0:T(8,128)(2,1)} %get-tuple-element.56.kb_ref, ...), custom_call_target="tpu_custom_call" | custom-call | flops 2097152 | bytes 6291456 | tf_op jit(solution)/shard_map/before/pallas_call | solution.py:360
  108.9 7.8 %all-to-all-done.1 = bf16[32,32,1024]{2,1,0:T(8,128)(2,1)S(1)} async-done(((bf16[32,32,1024]{2,1,0:T(8,128)(2,1)}), bf16[32,32,1024]{2,1,0:T(8,128)(2,1)S(1)}, u32[]{:S(2)}, u32[]{:S(2)}) %all-to-all-start.1) | async-done | bytes 2097184 | tf_op jit(solution)/shard_map/all_to_all | solution.py:339
  116.7 2.7 %final.1 = bf16[512,1024]{1,0:T(8,128)(2,1)} custom-call(s32[512,128]{1,0:T(8,128)S(1)} %unpack_index.1.row_ref, bf16[1024,1024]{1,0:T(8,128)(2,1)S(1)} %bitcast.10, f32[512,512]{1,0:T(8,128)S(1)} %get-tuple-element.65.left_ref, f32[512,512]{1,0:T(8,128)} %get-tuple-element.66.right_ref), custom_call_target="tpu_custom_call" | custom-call | flops 1073741824 | bytes 6291456 | tf_op jit(solution)/shard_map/final/pallas_call | solution.py:369
  (39 shorter events, 3.1 us)
Async XLA Ops:
  6.7 15.3 %collective-permute-start = (bf16[2,512,1024]{2,1,0:T(8,128)(2,1)}, bf16[2,512,1024]{2,1,0:T(8,128)(2,1)S(1)}, u32[]{:S(2)}, u32[]{:S(2)}) collective-permute-start(bf16[2,512,1024]{2,1,0:T(8,128)(2,1)} %pair_dot.2), channel_id=1, source_target_pairs={{0,32},{32,0},{64,96},{96,64},{128,160},{160,128},{192,224},{224,1... | collective-permute-start | bytes 6291464 | tf_op jit(solution)/shard_map/ppermute | solution.py:257
  6.7 40.7 %all-to-all-start = ((bf16[32,32,512]{2,1,0:T(8,128)(2,1)}), bf16[32,32,512]{2,1,0:T(8,128)(2,1)S(1)}, u32[]{:S(2)}, u32[]{:S(2)}) async-start(bf16[32,32,512]{2,1,0:T(8,128)(2,1)} %bitcast.15), calls=%async_computation | async-start | bytes 2097152 | tf_op jit(solution)/shard_map/all_to_all | solution.py:211
  22.0 4.4 %copy-start.2 = (s32[256]{0:T(256)S(1)}, s32[256]{0:T(256)}, u32[]{:S(2)}) copy-start(s32[256]{0:T(256)} %slot_ref.3) | copy-start | bytes 3076
  22.0 4.6 %copy-start.1 = (s32[32,32]{1,0:T(8,128)S(1)}, s32[32,32]{1,0:T(8,128)}, u32[]{:S(2)}) copy-start(s32[32,32]{1,0:T(8,128)} %id_ref.3) | copy-start | bytes 12292
  26.4 20.9 %copy-start = (bf16[8,512,64]{1,2,0:T(8,128)(2,1)S(1)}, bf16[8,512,64]{1,2,0:T(8,128)(2,1)}, u32[]{:S(2)}) copy-start(bf16[8,512,64]{1,2,0:T(8,128)(2,1)} %param.11) | copy-start | bytes 1572868
  48.2 1.3 %collective-permute-start.1 = (bf16[256,128]{1,0:T(8,128)(2,1)S(1)}, bf16[256,128]{1,0:T(8,128)(2,1)S(1)}, u32[]{:S(2)}, u32[]{:S(2)}) collective-permute-start(bf16[256,128]{1,0:T(8,128)(2,1)S(1)} %get-tuple-element.46), channel_id=1, source_target_pairs={{0,32},{32,0},{64,96},{96,64},{128,160},{160,128},{192,224},{224,1... | collective-permute-start | bytes 196616 | tf_op jit(solution)/shard_map/ppermute | solution.py:316
  49.6 5.6 %collective-permute-start.4 = (bf16[256,128]{1,0:T(8,128)(2,1)S(1)}, bf16[256,128]{1,0:T(8,128)(2,1)S(1)}, u32[]{:S(2)}, u32[]{:S(2)}) collective-permute-start(bf16[256,128]{1,0:T(8,128)(2,1)S(1)} %sum_low.2.refs_0_), channel_id=1, source_target_pairs={{0,192},{32,224},{64,128},{96,160},{128,64},{160,96},{192,0},{224,... | collective-permute-start | bytes 196616 | tf_op jit(solution)/shard_map/ppermute | solution.py:319
  50.1 5.0 %collective-permute-start.3 = (bf16[256,128]{1,0:T(8,128)(2,1)S(1)}, bf16[256,128]{1,0:T(8,128)(2,1)S(1)}, u32[]{:S(2)}, u32[]{:S(2)}) collective-permute-start(bf16[256,128]{1,0:T(8,128)(2,1)S(1)} %sum_low.2.refs_0_), channel_id=1, source_target_pairs={{0,64},{32,96},{64,0},{96,32},{128,192},{160,224},{192,128},{224,1... | collective-permute-start | bytes 196616 | tf_op jit(solution)/shard_map/ppermute | solution.py:319
  51.0 6.6 %collective-permute-start.2 = (bf16[256,128]{1,0:T(8,128)(2,1)S(1)}, bf16[256,128]{1,0:T(8,128)(2,1)S(1)}, u32[]{:S(2)}, u32[]{:S(2)}) collective-permute-start(bf16[256,128]{1,0:T(8,128)(2,1)S(1)} %sum_low.2.refs_0_), channel_id=1, source_target_pairs={{0,128},{32,160},{64,192},{96,224},{128,0},{160,32},{192,64},{224,... | collective-permute-start | bytes 196616 | tf_op jit(solution)/shard_map/ppermute | solution.py:319
  57.6 1.7 %collective-permute-start.5 = (bf16[256,128]{1,0:T(8,128)(2,1)S(1)}, bf16[256,128]{1,0:T(8,128)(2,1)S(1)}, u32[]{:S(2)}, u32[]{:S(2)}) collective-permute-start(bf16[256,128]{1,0:T(8,128)(2,1)S(1)} %sum_low.3.low_ref), channel_id=1, source_target_pairs={{0,32},{32,0},{64,96},{96,64},{128,160},{160,128},{192,224},{224,1... | collective-permute-start | bytes 196616 | tf_op jit(solution)/shard_map/ppermute | solution.py:321
  60.9 55.8 %all-to-all-start.1 = ((bf16[32,32,1024]{2,1,0:T(8,128)(2,1)}), bf16[32,32,1024]{2,1,0:T(8,128)(2,1)S(1)}, u32[]{:S(2)}, u32[]{:S(2)}) async-start(bf16[32,32,1024]{2,1,0:T(8,128)(2,1)} %bitcast.13), calls=%async_computation.1 | async-start | bytes 4194304 | tf_op jit(solution)/shard_map/all_to_all | solution.py:339
  66.1 4.6 %collective-permute-start.6 = (bf16[2,512,1024]{2,1,0:T(8,128)(2,1)}, bf16[2,512,1024]{2,1,0:T(8,128)(2,1)}, u32[]{:S(2)}, u32[]{:S(2)}) collective-permute-start(bf16[2,512,1024]{2,1,0:T(8,128)(2,1)} %pair_dot.3), channel_id=1, source_target_pairs={{0,32},{32,0},{64,96},{96,64},{128,160},{160,128},{192,224},{224,1... | collective-permute-start | bytes 6291464 | tf_op jit(solution)/shard_map/ppermute | solution.py:260
  66.4 15.1 %collective-permute-start.8 = (bf16[256,1024]{1,0:T(8,128)(2,1)}, bf16[256,1024]{1,0:T(8,128)(2,1)}, u32[]{:S(2)}, u32[]{:S(2)}) collective-permute-start(bf16[256,1024]{1,0:T(8,128)(2,1)} %get-tuple-element.39), channel_id=1, source_target_pairs={{0,64},{32,96},{64,0},{96,32},{128,192},{160,224},{192,128},{224,1... | collective-permute-start | bytes 1572872 | tf_op jit(solution)/shard_map/ppermute | solution.py:263
  66.8 17.6 %copy-start.4 = (bf16[256,1024]{1,0:T(8,128)(2,1)S(1)}, bf16[256,1024]{1,0:T(8,128)(2,1)}, u32[]{:S(2)}) copy-start(bf16[256,1024]{1,0:T(8,128)(2,1)} %get-tuple-element.58) | copy-start | bytes 1572868
  66.8 17.5 %collective-permute-start.11 = (bf16[256,1024]{1,0:T(8,128)(2,1)}, bf16[256,1024]{1,0:T(8,128)(2,1)S(1)}, u32[]{:S(2)}, u32[]{:S(2)}) collective-permute-start(bf16[256,1024]{1,0:T(8,128)(2,1)} %get-tuple-element.59), channel_id=1, source_target_pairs={{0,192},{32,224},{64,128},{96,160},{128,64},{160,96},{192,0},{224,... | collective-permute-start | bytes 1572872 | tf_op jit(solution)/shard_map/ppermute | solution.py:264
  75.4 10.4 %copy-start.3 = (s32[1,32]{1,0:T(1,128)S(1)}, s32[1,32]{1,0:T(1,128)}, u32[]{:S(2)}) copy-start(s32[1,32]{1,0:T(1,128)} %len_ref.3) | copy-start | bytes 388
  75.4 18.8 %collective-permute-start.10 = (bf16[256,1024]{1,0:T(8,128)(2,1)}, bf16[256,1024]{1,0:T(8,128)(2,1)S(1)}, u32[]{:S(2)}, u32[]{:S(2)}) collective-permute-start(bf16[256,1024]{1,0:T(8,128)(2,1)} %get-tuple-element.57), channel_id=1, source_target_pairs={{0,192},{32,224},{64,128},{96,160},{128,64},{160,96},{192,0},{224,... | collective-permute-start | bytes 1572872 | tf_op jit(solution)/shard_map/ppermute | solution.py:357
  76.7 17.5 %collective-permute-start.7 = (bf16[256,1024]{1,0:T(8,128)(2,1)}, bf16[256,1024]{1,0:T(8,128)(2,1)S(1)}, u32[]{:S(2)}, u32[]{:S(2)}) collective-permute-start(bf16[256,1024]{1,0:T(8,128)(2,1)} %get-tuple-element.54), channel_id=1, source_target_pairs={{0,64},{32,96},{64,0},{96,32},{128,192},{160,224},{192,128},{224,1... | collective-permute-start | bytes 1572872 | tf_op jit(solution)/shard_map/ppermute | solution.py:356
  82.9 21.6 %collective-permute-start.9 = (bf16[256,1024]{1,0:T(8,128)(2,1)S(1)}, bf16[256,1024]{1,0:T(8,128)(2,1)S(1)}, u32[]{:S(2)}, u32[]{:S(2)}) collective-permute-start(bf16[256,1024]{1,0:T(8,128)(2,1)S(1)} %add_convert_fusion.1), channel_id=1, source_target_pairs={{0,192},{32,224},{64,128},{96,160},{128,64},{160,96},{192,0},{224,... | collective-permute-start | bytes 1572872 | tf_op jit(solution)/shard_map/ppermute | solution.py:354
  84.5 20.0 %collective-permute-start.12 = (bf16[256,1024]{1,0:T(8,128)(2,1)S(1)}, bf16[256,1024]{1,0:T(8,128)(2,1)S(1)}, u32[]{:S(2)}, u32[]{:S(2)}) collective-permute-start(bf16[256,1024]{1,0:T(8,128)(2,1)S(1)} %add_convert_fusion), channel_id=1, source_target_pairs={{0,64},{32,96},{64,0},{96,32},{128,192},{160,224},{192,128},{224,1... | collective-permute-start | bytes 1572872 | tf_op jit(solution)/shard_map/ppermute | solution.py:355
  94.2 10.3 %copy-start.5 = (bf16[256,1024]{1,0:T(8,128)(2,1)}, bf16[256,1024]{1,0:T(8,128)(2,1)S(1)}, u32[]{:S(2)}) copy-start(bf16[256,1024]{1,0:T(8,128)(2,1)S(1)} %collective-permute-done.10.rb_ref) | copy-start | bytes 1572868
  94.2 10.3 %copy-start.6 = (bf16[256,1024]{1,0:T(8,128)(2,1)}, bf16[256,1024]{1,0:T(8,128)(2,1)S(1)}, u32[]{:S(2)}) copy-start(bf16[256,1024]{1,0:T(8,128)(2,1)S(1)} %collective-permute-done.7.ra_ref) | copy-start | bytes 1572868
  104.5 0.8 copy-start.7
  104.5 1.0 copy-start.8

commit v7 on v6

--- a/solution.py
+++ b/solution.py
@@ -24,7 +24,7 @@
     return pl.CostEstimate(flops=int(flops), transcendentals=0, bytes_accessed=int(nbytes))
 
 
-def pack_kernel(me_ref, len_ref, id_ref, slot_ref, x_ref, out_ref, sel_ref, *, pool, most):
+def pack_kernel(me_ref, len_ref, id_ref, slot_ref, x_ref, out_ref, sel_ref, o_buf, o_sem, *, pool, most):
     requests = len_ref.shape[1]
     tokens = x_ref.shape[0]
     rows = lax.broadcasted_iota(jnp.int32, (most, tokens), 0)
@@ -36,7 +36,15 @@
         at = pl.multiple_of(owner * most, most)
         sel_ref[pl.ds(at, most), :] = jnp.where(ahead == start, 1.0, 0.0).astype(BF)
         start = start + len_ref[0, r]
-    out_ref[...] = jnp.dot(sel_ref[...], x_ref[...], preferred_element_type=F32).astype(BF)
+    n = o_buf.shape[1]
+    leaving = []
+    for i in range(2):
+        at = pl.ds(i * n, n)
+        o_buf[i] = jnp.dot(sel_ref[at, :], x_ref[...], preferred_element_type=F32).astype(BF)
+        leaving.append(pltpu.make_async_copy(o_buf.at[i], out_ref.at[at], o_sem.at[i]))
+        leaving[-1].start()
+    for copy in leaving:
+        copy.wait()
 
 
 def unpack_index_kernel(me_ref, len_ref, id_ref, slot_ref, out_ref, *, pool, most):
@@ -51,29 +59,20 @@
     out_ref[...] = tok + shift
 
 
-def down_kernel(core_ref, code_ref, x_ref, d_ref, keep_ref, send_ref, *, pool):
-    half, lanes = keep_ref.shape
+def down_kernel(core_ref, code_ref, x_ref, d_ref, out_ref, *, pool, flip):
+    rows, lanes = out_ref.shape
     rank = lanes // 2
-    every = lax.dot_general(x_ref[...], d_ref[...], (((1,), (1,)), ((), ())), preferred_element_type=F32)
-    code = code_ref[...]
+    which = core_ref[0] ^ flip
+    at = [pl.ds(pl.multiple_of((2 * i + which) * rows, rows), rows) for i in range(2)]
+    x = jnp.concatenate([x_ref[at[0], :], x_ref[at[1], :]], 0)
+    code = jnp.concatenate([code_ref[at[0], :], code_ref[at[1], :]], 0)
+    every = lax.dot_general(x, d_ref[...], (((1,), (1,)), ((), ())), preferred_element_type=F32)
     acc = jnp.zeros(code.shape, F32)
     for b in range(pool // 2):
         acc = acc + jnp.where(code == 2 * b, every[:, 2 * b * rank:2 * (b + 1) * rank], 0.0)
     acc = acc + pltpu.roll(acc, rank, 1)
-    first = lax.broadcasted_iota(jnp.int32, (half, lanes), 1) < rank
-    top = jnp.where(first, acc[:half], acc[2 * half:3 * half]).astype(BF)
-    low = jnp.where(first, acc[half:2 * half], acc[3 * half:]).astype(BF)
-    core = core_ref[0]
-
-    @pl.when(core == 0)
-    def _():
-        keep_ref[...] = top
-        send_ref[...] = low
-
-    @pl.when(core != 0)
-    def _():
-        keep_ref[...] = low
-        send_ref[...] = top
+    first = lax.broadcasted_iota(jnp.int32, (rows, lanes), 1) < rank
+    out_ref[...] = jnp.where(first, acc[:rows], acc[rows:]).astype(BF)
 
 
 def up_kernel(core_ref, code_ref, low_ref, u_ref, *rest, pool, flip):
@@ -203,8 +202,8 @@
         functools.partial(pack_kernel, pool=pool, most=most),
         out_shape=sds((slots, features), BF),
         in_specs=[SM, SM, SM, SM, VM],
-        out_specs=VM,
-        scratch_shapes=[pltpu.VMEM((slots, tokens), BF)],
+        out_specs=HB,
+        scratch_shapes=[pltpu.VMEM((slots, tokens), BF), pltpu.VMEM((2, slots // 2, features), BF), DMA((2,))],
         cost_estimate=cost(2 * slots * tokens * features, 2 * (slots + tokens) * features),
         name="pack",
     )(me1, req_len, req_id, pool_slot, x)
@@ -288,20 +287,24 @@
     code = near(code)
     core = t1 & 1
     piece = pltpu.VMEM((slots // 4, 2 * rank), BF)
-    low, send = pl.pallas_call(
-        functools.partial(down_kernel, pool=pool),
-        out_shape=[piece] * 2,
-        in_specs=[SM, VM, VM, VM],
-        out_specs=[VM] * 2,
-        cost_estimate=cost(2 * slots * pool * rank * features, 2 * slots * features),
-        name="down",
-        compiler_params=SMALL,
-    )(
-        core,
-        code,
-        near(arrived.reshape(slots, features)),
-        near(jnp.swapaxes(down, 1, 2).reshape(pool * rank, features)),
-    )
+    rows_here = arrived.reshape(slots, features)
+    down_maps = jnp.swapaxes(down, 1, 2).reshape(pool * rank, features)
+
+    def lower(flip):
+        return pl.pallas_call(
+            functools.partial(down_kernel, pool=pool, flip=flip),
+            out_shape=piece,
+            in_specs=[SM, VM, VM, VM],
+            out_specs=VM,
+            cost_estimate=cost(slots * pool * rank * features, slots * features),
+            name="down",
+            compiler_params=SMALL,
+        )(core, code, near(rows_here), near(down_maps))
+
+    send = lower(1)
+    other = lax.ppermute(send, "tensor", xor(1))
+    rows_here, _ = lax.optimization_barrier((rows_here, send))
+    low = lower(0)
 
     def total(*terms):
         return pl.pallas_call(
@@ -313,7 +316,7 @@
             compiler_params=SMALL,
         )(*[near(v) for v in terms])
 
-    low = total(low, lax.ppermute(send, "tensor", xor(1)))
+    low = total(low, other)
     came = []
     for m in (4, 2, 6):
         came.append(lax.ppermute(low, "tensor", xor(m)))

time: 121 us -> 121 us (level)
  transfers between devices with their start and end apart: 15 -> 15, of which waited for: 9 -> 9; matrix products, arithmetic and copies ran while one was open for 2% -> 2% of each run, Pallas kernels for 17% -> 18%
where the time goes in v7:
time: 121 us; the launch traced here: 119 us
  waiting for transfers between devices  52.1 us (43%)
  Pallas kernels  32.8 us (27%)
  starting transfers between devices  30.1 us (25%)
  other arithmetic  2.7 us (2%)
    all_to_all x1, waiting for transfers between devices, one_block(): lax.all_to_all(outgoing.reshape(groups, most, features), 'req', split_axi...  18.4 us
    all_to_all x1, starting transfers between devices, one_block(): lax.all_to_all(outgoing.reshape(groups, most, features), 'req', split_axi...  11.5 us
    ppermute x1, waiting for transfers between devices, one_block(): lax.ppermute((k3a.astype(F32) + r2a.astype(F32)).astype(BF), 'tensor', xo...  10.3 us
    pallas_call x2, Pallas kernels, own(): pl.pallas_call(own_dot_kernel, out_shape=[piece] * 4, grid_spec=pltpu.Pre...  9.05 us
    all_to_all x1, waiting for transfers between devices, one_block(): lax.all_to_all(raised.reshape(groups, most, cols), 'req', split_axis=0, c...  7.82 us
    pallas_call x2, Pallas kernels, parts(): pl.pallas_call(pair_dot_kernel, out_shape=sds((n, tokens, cols), BF), gri...  7.6 us
    ppermute x1, waiting for transfers between devices, one_block(): r3b = lax.ppermute(s3b, 'tensor', xor(6))  6.73 us
    all_to_all x1, starting transfers between devices, one_block(): lax.all_to_all(raised.reshape(groups, most, cols), 'req', split_axis=0, c...  5.19 us
  transfers between devices with their start and end apart: 15, of which 9 were waited for; matrix products, arithmetic and copies ran while one was open for 2% of the time, Pallas kernels for 18%

profile of v7, /device:TPU:6, one launch (start us, length us, event | category | flops | bytes accessed | tf_op | source)
XLA Modules:
  0.0 119.2 jit_solution(3203428214098962298)
XLA Ops:
  0.0 2.7 %pack.1 = bf16[1024,512]{1,0:T(8,128)(2,1)} custom-call(s32[1]{0:T(128)} %bitcast.1.me_ref, s32[1,32]{1,0:T(1,128)} %len_ref.3, s32[32,32]{1,0:T(8,128)} %id_ref.3, s32[256]{0:T(256)} %slot_ref.3, bf16[512,512]{1,0:T(8,128)(2,1)} %x_ref.5), custom_call_target="tpu_custom_call" | custom-call | flops 536870912 | bytes 1572864 | tf_op jit(solution)/shard_map/pack/pallas_call | solution.py:201
  2.7 3.8 %pair_dot.2 = bf16[2,512,1024]{2,1,0:T(8,128)(2,1)} custom-call(s32[1]{0:T(128)} %bitcast.t_ref, bf16[512,512]{1,0:T(8,128)(2,1)} %x_ref.5, bf16[512,8192]{1,0:T(8,128)(2,1)} %w_ref.7), custom_call_target="tpu_custom_call" | custom-call | flops 1073741824 | bytes 4194304 | tf_op jit(solution)/shard_map/pair_dot/pallas_call | solution.py:219
  6.5 11.5 %all-to-all-start = ((bf16[32,32,512]{2,1,0:T(8,128)(2,1)}), bf16[32,32,512]{2,1,0:T(8,128)(2,1)S(1)}, u32[]{:S(2)}, u32[]{:S(2)}) async-start(bf16[32,32,512]{2,1,0:T(8,128)(2,1)} %bitcast.17), calls=%async_computation | async-start | bytes 2097152 | tf_op jit(solution)/shard_map/all_to_all | solution.py:210
  18.0 3.8 %pair_dot.3 = bf16[2,512,1024]{2,1,0:T(8,128)(2,1)} custom-call(s32[1]{0:T(128)} %bitcast.t_ref, bf16[512,512]{1,0:T(8,128)(2,1)} %x_ref.5, bf16[512,8192]{1,0:T(8,128)(2,1)} %w_ref.7), custom_call_target="tpu_custom_call" | custom-call | flops 1073741824 | bytes 4194304 | tf_op jit(solution)/shard_map/pair_dot/pallas_call | solution.py:219
  21.9 4.4 %own_dot.2 = (bf16[256,1024]{1,0:T(8,128)(2,1)}, bf16[256,1024]{1,0:T(8,128)(2,1)}, bf16[256,1024]{1,0:T(8,128)(2,1)}, bf16[256,1024]{1,0:T(8,128)(2,1)}) custom-call(s32[1]{0:T(128)} %bitcast.t_ref, bf16[512,512]{1,0:T(8,128)(2,1)} %x_ref.5, bf16[512,8192]{1,0:T(8,128)(2,1)} %w_ref.7, bf16[2,512,1024]{2,1,0:T(8,128)(2,1)S(1)} %collective-permute-done.p_ref), custom_call_target="tpu_custom_call" | custom-call | flops 1073741824 | bytes 6291456 | tf_op jit(solution)/shard_map/own_dot/pallas_call | solution.py:235
  26.5 0.7 select_reduce_fusion
  27.3 1.2 %fetch_up.1.u_ref = bf16[512,1024]{1,0:T(8,128)(2,1)S(1)} custom-call(bf16[512,1024]{1,0:T(8,128)(2,1)} %bitcast.16), custom_call_target="tpu_custom_call" | custom-call | bytes 2097152 | tf_op jit(solution)/shard_map/fetch_up/pallas_call | solution.py:275
  28.8 18.4 %all-to-all-done = bf16[32,32,512]{2,1,0:T(8,128)(2,1)S(1)} async-done(((bf16[32,32,512]{2,1,0:T(8,128)(2,1)}), bf16[32,32,512]{2,1,0:T(8,128)(2,1)S(1)}, u32[]{:S(2)}, u32[]{:S(2)}) %all-to-all-start) | async-done | bytes 1048608 | tf_op jit(solution)/shard_map/all_to_all | solution.py:210
  48.4 0.7 collective-permute-done.1.refs_1_
  49.7 0.9 collective-permute-start.3
  50.6 3.3 %collective-permute-start.2 = (bf16[256,128]{1,0:T(8,128)(2,1)S(1)}, bf16[256,128]{1,0:T(8,128)(2,1)S(1)}, u32[]{:S(2)}, u32[]{:S(2)}) collective-permute-start(bf16[256,128]{1,0:T(8,128)(2,1)S(1)} %sum_low.2.refs_0_), channel_id=1, source_target_pairs={{0,128},{32,160},{64,192},{96,224},{128,0},{160,32},{192,64},{224,... | collective-permute-start | bytes 196616 | tf_op jit(solution)/shard_map/ppermute | solution.py:322
  53.9 0.8 collective-permute-done.4.refs_3_
  54.7 2.5 %collective-permute-done.2.refs_1_ = bf16[256,128]{1,0:T(8,128)(2,1)S(1)} collective-permute-done((bf16[256,128]{1,0:T(8,128)(2,1)S(1)}, bf16[256,128]{1,0:T(8,128)(2,1)S(1)}, u32[]{:S(2)}, u32[]{:S(2)}) %collective-permute-start.2) | collective-permute-done | bytes 65568 | tf_op jit(solution)/shard_map/ppermute | solution.py:322
  57.3 1.6 %up.2.rest_0_ = bf16[1024,1024]{1,0:T(8,128)(2,1)} custom-call(s32[1]{0:T(128)S(6)} %and.5.core_ref, s32[1024,128]{1,0:T(8,128)S(1)} %broadcast_subtract_fusion.code_ref, bf16[256,128]{1,0:T(8,128)(2,1)S(1)} %sum_low.3.low_ref, bf16[512,1024]{1,0:T(8,128)(2,1)S(1)} %fetch_up.1.u_ref), custom_call_target="tpu_custom_call" | custom-call | flops 536870912 | bytes 1048576 | tf_op jit(solution)/shard_map/up/pallas_call | solution.py:327
  58.9 1.6 %up.3 = bf16[1024,1024]{1,0:T(8,128)(2,1)} custom-call(s32[1]{0:T(128)S(6)} %and.5.core_ref, s32[1024,128]{1,0:T(8,128)S(1)} %broadcast_subtract_fusion.code_ref, bf16[256,128]{1,0:T(8,128)(2,1)S(1)} %collective-permute-done.5.low_ref, bf16[512,1024]{1,0:T(8,128)(2,1)S(1)} %fetch_up.1.u_ref, ...), custom_call_target="tpu_custom_call", output_to_operand_aliasing={{}: (4, {})} | custom-call | flops 536870912 | bytes 1048576 | tf_op jit(solution)/shard_map/up/pallas_call | solution.py:327
  60.5 5.2 %all-to-all-start.1 = ((bf16[32,32,1024]{2,1,0:T(8,128)(2,1)}), bf16[32,32,1024]{2,1,0:T(8,128)(2,1)S(1)}, u32[]{:S(2)}, u32[]{:S(2)}) async-start(bf16[32,32,1024]{2,1,0:T(8,128)(2,1)} %bitcast.15), calls=%async_computation.1 | async-start | bytes 4194304 | tf_op jit(solution)/shard_map/all_to_all | solution.py:342
  66.3 2.8 %collective-permute-start.11 = (bf16[256,1024]{1,0:T(8,128)(2,1)}, bf16[256,1024]{1,0:T(8,128)(2,1)S(1)}, u32[]{:S(2)}, u32[]{:S(2)}) collective-permute-start(bf16[256,1024]{1,0:T(8,128)(2,1)} %get-tuple-element.57), channel_id=1, source_target_pairs={{0,192},{32,224},{64,128},{96,160},{128,64},{160,96},{192,0},{224,... | collective-permute-start | bytes 1572872 | tf_op jit(solution)/shard_map/ppermute | solution.py:263
  69.1 1.2 %collective-permute-done.6.p_ref = bf16[2,512,1024]{2,1,0:T(8,128)(2,1)} collective-permute-done((bf16[2,512,1024]{2,1,0:T(8,128)(2,1)}, bf16[2,512,1024]{2,1,0:T(8,128)(2,1)}, u32[]{:S(2)}, u32[]{:S(2)}) %collective-permute-start.6) | collective-permute-done | bytes 2097184 | tf_op jit(solution)/shard_map/ppermute | solution.py:259
  70.3 4.7 %own_dot.3 = (bf16[256,1024]{1,0:T(8,128)(2,1)}, bf16[256,1024]{1,0:T(8,128)(2,1)}, bf16[256,1024]{1,0:T(8,128)(2,1)}, bf16[256,1024]{1,0:T(8,128)(2,1)}) custom-call(s32[1]{0:T(128)} %bitcast.t_ref, bf16[512,512]{1,0:T(8,128)(2,1)} %x_ref.5, bf16[512,8192]{1,0:T(8,128)(2,1)} %w_ref.7, bf16[2,512,1024]{2,1,0:T(8,128)(2,1)} %collective-permute-done.6.p_ref), custom_call_target="tpu_custom_call" | custom-call | flops 1073741824 | bytes 6291456 | tf_op jit(solution)/shard_map/own_dot/pallas_call | solution.py:235
  75.0 1.3 %collective-permute-start.10 = (bf16[256,1024]{1,0:T(8,128)(2,1)}, bf16[256,1024]{1,0:T(8,128)(2,1)S(1)}, u32[]{:S(2)}, u32[]{:S(2)}) collective-permute-start(bf16[256,1024]{1,0:T(8,128)(2,1)} %get-tuple-element.55), channel_id=1, source_target_pairs={{0,192},{32,224},{64,128},{96,160},{128,64},{160,96},{192,0},{224,... | collective-permute-start | bytes 1572872 | tf_op jit(solution)/shard_map/ppermute | solution.py:360
  76.3 1.2 %collective-permute-start.7 = (bf16[256,1024]{1,0:T(8,128)(2,1)}, bf16[256,1024]{1,0:T(8,128)(2,1)S(1)}, u32[]{:S(2)}, u32[]{:S(2)}) collective-permute-start(bf16[256,1024]{1,0:T(8,128)(2,1)} %get-tuple-element.52), channel_id=1, source_target_pairs={{0,64},{32,96},{64,0},{96,32},{128,192},{160,224},{192,128},{224,1... | collective-permute-start | bytes 1572872 | tf_op jit(solution)/shard_map/ppermute | solution.py:359
  77.5 3.7 %collective-permute-done.8 = bf16[256,1024]{1,0:T(8,128)(2,1)} collective-permute-done((bf16[256,1024]{1,0:T(8,128)(2,1)}, bf16[256,1024]{1,0:T(8,128)(2,1)}, u32[]{:S(2)}, u32[]{:S(2)}) %collective-permute-start.8) | collective-permute-done | bytes 524320 | tf_op jit(solution)/shard_map/ppermute | solution.py:262
  81.1 1.4 %add_convert_fusion.1 = bf16[256,1024]{1,0:T(8,128)(2,1)S(1)} fusion(bf16[256,1024]{1,0:T(8,128)(2,1)} %collective-permute-done.8, bf16[256,1024]{1,0:T(8,128)(2,1)} %get-tuple-element.53), kind=kLoop, calls=%fused_computation.1 | loop fusion | flops 1048576 | bytes 1572864 | tf_op jit(solution)/shard_map/convert_element_type | solution.py:357
  82.5 1.4 %collective-permute-start.9 = (bf16[256,1024]{1,0:T(8,128)(2,1)S(1)}, bf16[256,1024]{1,0:T(8,128)(2,1)S(1)}, u32[]{:S(2)}, u32[]{:S(2)}) collective-permute-start(bf16[256,1024]{1,0:T(8,128)(2,1)S(1)} %add_convert_fusion.1), channel_id=1, source_target_pairs={{0,192},{32,224},{64,128},{96,160},{128,64},{160,96},{192,0},{224,... | collective-permute-start | bytes 1572872 | tf_op jit(solution)/shard_map/ppermute | solution.py:357
  84.1 1.3 %collective-permute-start.12 = (bf16[256,1024]{1,0:T(8,128)(2,1)S(1)}, bf16[256,1024]{1,0:T(8,128)(2,1)S(1)}, u32[]{:S(2)}, u32[]{:S(2)}) collective-permute-start(bf16[256,1024]{1,0:T(8,128)(2,1)S(1)} %add_convert_fusion), channel_id=1, source_target_pairs={{0,64},{32,96},{64,0},{96,32},{128,192},{160,224},{192,128},{224,1... | collective-permute-start | bytes 1572872 | tf_op jit(solution)/shard_map/ppermute | solution.py:358
  85.4 1.7 %unpack_index.1.row_ref = s32[512,128]{1,0:T(8,128)S(1)} custom-call(s32[1]{0:T(128)} %bitcast.1.me_ref, s32[1,32]{1,0:T(1,128)S(1)} %copy-done.3, s32[32,32]{1,0:T(8,128)S(1)} %copy-done.1, s32[256]{0:T(256)S(1)} %copy-done.2), custom_call_target="tpu_custom_call" | custom-call | flops 4194304 | bytes 262144 | tf_op jit(solution)/shard_map/unpack_index/pallas_call | solution.py:346
  87.1 6.7 %collective-permute-done.10.rb_ref = bf16[256,1024]{1,0:T(8,128)(2,1)S(1)} collective-permute-done((bf16[256,1024]{1,0:T(8,128)(2,1)}, bf16[256,1024]{1,0:T(8,128)(2,1)S(1)}, u32[]{:S(2)}, u32[]{:S(2)}) %collective-permute-start.10) | collective-permute-done | bytes 524320 | tf_op jit(solution)/shard_map/ppermute | solution.py:360
  93.8 10.3 %collective-permute-done.9.za_ref = bf16[256,1024]{1,0:T(8,128)(2,1)S(1)} collective-permute-done((bf16[256,1024]{1,0:T(8,128)(2,1)S(1)}, bf16[256,1024]{1,0:T(8,128)(2,1)S(1)}, u32[]{:S(2)}, u32[]{:S(2)}) %collective-permute-start.9) | collective-permute-done | bytes 524320 | tf_op jit(solution)/shard_map/ppermute | solution.py:357
  104.1 0.8 copy-done.7
  105.1 3.4 %before.1 = (f32[512,512]{1,0:T(8,128)S(1)}, f32[512,512]{1,0:T(8,128)}) custom-call(bf16[512,1024]{1,0:T(8,128)(2,1)} %res_ref.1, bf16[256,1024]{1,0:T(8,128)(2,1)} %get-tuple-element.51.ka_ref, bf16[256,1024]{1,0:T(8,128)(2,1)} %copy-done.6, bf16[256,1024]{1,0:T(8,128)(2,1)} %copy-done.7, bf16[256,1024]{1,0:T(8,128)(2,1)} %get-tuple-element.54.kb_ref, ...), custom_call_target="tpu_custom_call" | custom-call | flops 2097152 | bytes 6291456 | tf_op jit(solution)/shard_map/before/pallas_call | solution.py:363
  108.4 7.8 %all-to-all-done.1 = bf16[32,32,1024]{2,1,0:T(8,128)(2,1)S(1)} async-done(((bf16[32,32,1024]{2,1,0:T(8,128)(2,1)}), bf16[32,32,1024]{2,1,0:T(8,128)(2,1)S(1)}, u32[]{:S(2)}, u32[]{:S(2)}) %all-to-all-start.1) | async-done | bytes 2097184 | tf_op jit(solution)/shard_map/all_to_all | solution.py:342
  116.3 2.8 %final.1 = bf16[512,1024]{1,0:T(8,128)(2,1)} custom-call(s32[512,128]{1,0:T(8,128)S(1)} %unpack_index.1.row_ref, bf16[1024,1024]{1,0:T(8,128)(2,1)S(1)} %bitcast.12, f32[512,512]{1,0:T(8,128)S(1)} %get-tuple-element.63.left_ref, f32[512,512]{1,0:T(8,128)} %get-tuple-element.64.right_ref), custom_call_target="tpu_custom_call" | custom-call | flops 1073741824 | bytes 6291456 | tf_op jit(solution)/shard_map/final/pallas_call | solution.py:372
  (40 shorter events, 3.5 us)
Async XLA Ops:
  6.5 15.3 %collective-permute-start = (bf16[2,512,1024]{2,1,0:T(8,128)(2,1)}, bf16[2,512,1024]{2,1,0:T(8,128)(2,1)S(1)}, u32[]{:S(2)}, u32[]{:S(2)}) collective-permute-start(bf16[2,512,1024]{2,1,0:T(8,128)(2,1)} %pair_dot.2), channel_id=1, source_target_pairs={{0,32},{32,0},{64,96},{96,64},{128,160},{160,128},{192,224},{224,1... | collective-permute-start | bytes 6291464 | tf_op jit(solution)/shard_map/ppermute | solution.py:256
  6.5 40.7 %all-to-all-start = ((bf16[32,32,512]{2,1,0:T(8,128)(2,1)}), bf16[32,32,512]{2,1,0:T(8,128)(2,1)S(1)}, u32[]{:S(2)}, u32[]{:S(2)}) async-start(bf16[32,32,512]{2,1,0:T(8,128)(2,1)} %bitcast.17), calls=%async_computation | async-start | bytes 2097152 | tf_op jit(solution)/shard_map/all_to_all | solution.py:210
  21.8 4.4 %copy-start.2 = (s32[256]{0:T(256)S(1)}, s32[256]{0:T(256)}, u32[]{:S(2)}) copy-start(s32[256]{0:T(256)} %slot_ref.3) | copy-start | bytes 3076
  21.9 4.6 %copy-start.1 = (s32[32,32]{1,0:T(8,128)S(1)}, s32[32,32]{1,0:T(8,128)}, u32[]{:S(2)}) copy-start(s32[32,32]{1,0:T(8,128)} %id_ref.3) | copy-start | bytes 12292
  26.3 21.0 %copy-start = (bf16[8,512,64]{1,2,0:T(8,128)(2,1)S(1)}, bf16[8,512,64]{1,2,0:T(8,128)(2,1)}, u32[]{:S(2)}) copy-start(bf16[8,512,64]{1,2,0:T(8,128)(2,1)} %param.11) | copy-start | bytes 1572868
  47.8 1.3 %collective-permute-start.1 = (bf16[256,128]{1,0:T(8,128)(2,1)S(1)}, bf16[256,128]{1,0:T(8,128)(2,1)S(1)}, u32[]{:S(2)}, u32[]{:S(2)}) collective-permute-start(bf16[256,128]{1,0:T(8,128)(2,1)S(1)} %down.2), channel_id=1, source_target_pairs={{0,32},{32,0},{64,96},{96,64},{128,160},{160,128},{192,224},{224,1... | collective-permute-start | bytes 196616 | tf_op jit(solution)/shard_map/ppermute | solution.py:305
  49.1 5.6 %collective-permute-start.4 = (bf16[256,128]{1,0:T(8,128)(2,1)S(1)}, bf16[256,128]{1,0:T(8,128)(2,1)S(1)}, u32[]{:S(2)}, u32[]{:S(2)}) collective-permute-start(bf16[256,128]{1,0:T(8,128)(2,1)S(1)} %sum_low.2.refs_0_), channel_id=1, source_target_pairs={{0,192},{32,224},{64,128},{96,160},{128,64},{160,96},{192,0},{224,... | collective-permute-start | bytes 196616 | tf_op jit(solution)/shard_map/ppermute | solution.py:322
  49.7 5.0 %collective-permute-start.3 = (bf16[256,128]{1,0:T(8,128)(2,1)S(1)}, bf16[256,128]{1,0:T(8,128)(2,1)S(1)}, u32[]{:S(2)}, u32[]{:S(2)}) collective-permute-start(bf16[256,128]{1,0:T(8,128)(2,1)S(1)} %sum_low.2.refs_0_), channel_id=1, source_target_pairs={{0,64},{32,96},{64,0},{96,32},{128,192},{160,224},{192,128},{224,1... | collective-permute-start | bytes 196616 | tf_op jit(solution)/shard_map/ppermute | solution.py:322
  50.6 6.6 %collective-permute-start.2 = (bf16[256,128]{1,0:T(8,128)(2,1)S(1)}, bf16[256,128]{1,0:T(8,128)(2,1)S(1)}, u32[]{:S(2)}, u32[]{:S(2)}) collective-permute-start(bf16[256,128]{1,0:T(8,128)(2,1)S(1)} %sum_low.2.refs_0_), channel_id=1, source_target_pairs={{0,128},{32,160},{64,192},{96,224},{128,0},{160,32},{192,64},{224,... | collective-permute-start | bytes 196616 | tf_op jit(solution)/shard_map/ppermute | solution.py:322
  57.2 1.7 %collective-permute-start.5 = (bf16[256,128]{1,0:T(8,128)(2,1)S(1)}, bf16[256,128]{1,0:T(8,128)(2,1)S(1)}, u32[]{:S(2)}, u32[]{:S(2)}) collective-permute-start(bf16[256,128]{1,0:T(8,128)(2,1)S(1)} %sum_low.3.low_ref), channel_id=1, source_target_pairs={{0,32},{32,0},{64,96},{96,64},{128,160},{160,128},{192,224},{224,1... | collective-permute-start | bytes 196616 | tf_op jit(solution)/shard_map/ppermute | solution.py:324
  60.5 55.7 %all-to-all-start.1 = ((bf16[32,32,1024]{2,1,0:T(8,128)(2,1)}), bf16[32,32,1024]{2,1,0:T(8,128)(2,1)S(1)}, u32[]{:S(2)}, u32[]{:S(2)}) async-start(bf16[32,32,1024]{2,1,0:T(8,128)(2,1)} %bitcast.15), calls=%async_computation.1 | async-start | bytes 4194304 | tf_op jit(solution)/shard_map/all_to_all | solution.py:342
  65.7 4.6 %collective-permute-start.6 = (bf16[2,512,1024]{2,1,0:T(8,128)(2,1)}, bf16[2,512,1024]{2,1,0:T(8,128)(2,1)}, u32[]{:S(2)}, u32[]{:S(2)}) collective-permute-start(bf16[2,512,1024]{2,1,0:T(8,128)(2,1)} %pair_dot.3), channel_id=1, source_target_pairs={{0,32},{32,0},{64,96},{96,64},{128,160},{160,128},{192,224},{224,1... | collective-permute-start | bytes 6291464 | tf_op jit(solution)/shard_map/ppermute | solution.py:259
  66.0 15.1 %collective-permute-start.8 = (bf16[256,1024]{1,0:T(8,128)(2,1)}, bf16[256,1024]{1,0:T(8,128)(2,1)}, u32[]{:S(2)}, u32[]{:S(2)}) collective-permute-start(bf16[256,1024]{1,0:T(8,128)(2,1)} %get-tuple-element.38), channel_id=1, source_target_pairs={{0,64},{32,96},{64,0},{96,32},{128,192},{160,224},{192,128},{224,1... | collective-permute-start | bytes 1572872 | tf_op jit(solution)/shard_map/ppermute | solution.py:262
  66.3 17.6 %copy-start.4 = (bf16[256,1024]{1,0:T(8,128)(2,1)S(1)}, bf16[256,1024]{1,0:T(8,128)(2,1)}, u32[]{:S(2)}) copy-start(bf16[256,1024]{1,0:T(8,128)(2,1)} %get-tuple-element.56) | copy-start | bytes 1572868
  66.3 17.6 %collective-permute-start.11 = (bf16[256,1024]{1,0:T(8,128)(2,1)}, bf16[256,1024]{1,0:T(8,128)(2,1)S(1)}, u32[]{:S(2)}, u32[]{:S(2)}) collective-permute-start(bf16[256,1024]{1,0:T(8,128)(2,1)} %get-tuple-element.57), channel_id=1, source_target_pairs={{0,192},{32,224},{64,128},{96,160},{128,64},{160,96},{192,0},{224,... | collective-permute-start | bytes 1572872 | tf_op jit(solution)/shard_map/ppermute | solution.py:263
  75.0 10.4 %copy-start.3 = (s32[1,32]{1,0:T(1,128)S(1)}, s32[1,32]{1,0:T(1,128)}, u32[]{:S(2)}) copy-start(s32[1,32]{1,0:T(1,128)} %len_ref.3) | copy-start | bytes 388
  75.0 18.8 %collective-permute-start.10 = (bf16[256,1024]{1,0:T(8,128)(2,1)}, bf16[256,1024]{1,0:T(8,128)(2,1)S(1)}, u32[]{:S(2)}, u32[]{:S(2)}) collective-permute-start(bf16[256,1024]{1,0:T(8,128)(2,1)} %get-tuple-element.55), channel_id=1, source_target_pairs={{0,192},{32,224},{64,128},{96,160},{128,64},{160,96},{192,0},{224,... | collective-permute-start | bytes 1572872 | tf_op jit(solution)/shard_map/ppermute | solution.py:360
  76.3 17.5 %collective-permute-start.7 = (bf16[256,1024]{1,0:T(8,128)(2,1)}, bf16[256,1024]{1,0:T(8,128)(2,1)S(1)}, u32[]{:S(2)}, u32[]{:S(2)}) collective-permute-start(bf16[256,1024]{1,0:T(8,128)(2,1)} %get-tuple-element.52), channel_id=1, source_target_pairs={{0,64},{32,96},{64,0},{96,32},{128,192},{160,224},{192,128},{224,1... | collective-permute-start | bytes 1572872 | tf_op jit(solution)/shard_map/ppermute | solution.py:359
  82.5 21.6 %collective-permute-start.9 = (bf16[256,1024]{1,0:T(8,128)(2,1)S(1)}, bf16[256,1024]{1,0:T(8,128)(2,1)S(1)}, u32[]{:S(2)}, u32[]{:S(2)}) collective-permute-start(bf16[256,1024]{1,0:T(8,128)(2,1)S(1)} %add_convert_fusion.1), channel_id=1, source_target_pairs={{0,192},{32,224},{64,128},{96,160},{128,64},{160,96},{192,0},{224,... | collective-permute-start | bytes 1572872 | tf_op jit(solution)/shard_map/ppermute | solution.py:357
  84.1 20.0 %collective-permute-start.12 = (bf16[256,1024]{1,0:T(8,128)(2,1)S(1)}, bf16[256,1024]{1,0:T(8,128)(2,1)S(1)}, u32[]{:S(2)}, u32[]{:S(2)}) collective-permute-start(bf16[256,1024]{1,0:T(8,128)(2,1)S(1)} %add_convert_fusion), channel_id=1, source_target_pairs={{0,64},{32,96},{64,0},{96,32},{128,192},{160,224},{192,128},{224,1... | collective-permute-start | bytes 1572872 | tf_op jit(solution)/shard_map/ppermute | solution.py:358
  93.8 10.3 %copy-start.5 = (bf16[256,1024]{1,0:T(8,128)(2,1)}, bf16[256,1024]{1,0:T(8,128)(2,1)S(1)}, u32[]{:S(2)}) copy-start(bf16[256,1024]{1,0:T(8,128)(2,1)S(1)} %collective-permute-done.10.rb_ref) | copy-start | bytes 1572868
  93.8 10.3 %copy-start.6 = (bf16[256,1024]{1,0:T(8,128)(2,1)}, bf16[256,1024]{1,0:T(8,128)(2,1)S(1)}, u32[]{:S(2)}) copy-start(bf16[256,1024]{1,0:T(8,128)(2,1)S(1)} %collective-permute-done.7.ra_ref) | copy-start | bytes 1572868
  104.1 0.8 copy-start.7
  104.1 1.0 copy-start.8

commit v8 on v7

--- a/solution.py
+++ b/solution.py
@@ -91,9 +91,14 @@
         spread = jnp.concatenate(
             [jnp.where(code == 2 * k, low, 0.0).astype(BF) for k in range(pool // 2)], 1
         )
-        o_buf[i] = jnp.dot(spread, u_ref[...], preferred_element_type=F32).astype(BF)
-        leaving.append(pltpu.make_async_copy(o_buf.at[i], out_ref.at[at], o_sem.at[i]))
-        leaving[-1].start()
+        n = rows // 2
+        for h in range(2):
+            o_buf[2 * i + h] = jnp.dot(
+                spread[h * n:(h + 1) * n], u_ref[...], preferred_element_type=F32
+            ).astype(BF)
+            to = pl.ds(pl.multiple_of((2 * i + which) * rows + h * n, n), n)
+            leaving.append(pltpu.make_async_copy(o_buf.at[2 * i + h], out_ref.at[to], o_sem.at[2 * i + h]))
+            leaving[-1].start()
     for copy in leaving:
         copy.wait()
 
@@ -329,7 +334,7 @@
             out_shape=pltpu.HBM((slots, cols), BF),
             in_specs=[SM, VM, VM, VM] + [HB] * len(filled),
             out_specs=HB,
-            scratch_shapes=[pltpu.VMEM((2, slots // 4, cols), BF), DMA((2,))],
+            scratch_shapes=[pltpu.VMEM((4, slots // 8, cols), BF), DMA((4,))],
             input_output_aliases={4: 0} if filled else {},
             cost_estimate=cost(slots * pool * rank * cols, slots * cols),
             name="up",

time: 121 us -> 121 us (level)
  no operation moved by 1% of the time
where the time goes in v8:
time: 121 us; the launch traced here: 119 us
  waiting for transfers between devices  52.1 us (43%)
  Pallas kernels  32.6 us (27%)
  starting transfers between devices  30.2 us (25%)
  other arithmetic  2.7 us (2%)
    all_to_all x1, waiting for transfers between devices, one_block(): lax.all_to_all(outgoing.reshape(groups, most, features), 'req', split_axi...  18.4 us
    all_to_all x1, starting transfers between devices, one_block(): lax.all_to_all(outgoing.reshape(groups, most, features), 'req', split_axi...  11.5 us
    ppermute x1, waiting for transfers between devices, one_block(): lax.ppermute((k3a.astype(F32) + r2a.astype(F32)).astype(BF), 'tensor', xo...  10.3 us
    pallas_call x2, Pallas kernels, own(): pl.pallas_call(own_dot_kernel, out_shape=[piece] * 4, grid_spec=pltpu.Pre...  9.05 us
    all_to_all x1, waiting for transfers between devices, one_block(): lax.all_to_all(raised.reshape(groups, most, cols), 'req', split_axis=0, c...  7.84 us
    pallas_call x2, Pallas kernels, parts(): pl.pallas_call(pair_dot_kernel, out_shape=sds((n, tokens, cols), BF), gri...  7.6 us
    ppermute x1, waiting for transfers between devices, one_block(): r3b = lax.ppermute(s3b, 'tensor', xor(6))  6.72 us
    all_to_all x1, starting transfers between devices, one_block(): lax.all_to_all(raised.reshape(groups, most, cols), 'req', split_axis=0, c...  5.19 us
  transfers between devices with their start and end apart: 15, of which 9 were waited for; matrix products, arithmetic and copies ran while one was open for 2% of the time, Pallas kernels for 18%

profile of v8, /device:TPU:6, one launch (start us, length us, event | category | flops | bytes accessed | tf_op | source)
XLA Modules:
  0.0 119.1 jit_solution(10001050557583017369)
XLA Ops:
  0.0 2.7 %pack.1 = bf16[1024,512]{1,0:T(8,128)(2,1)} custom-call(s32[1]{0:T(128)} %bitcast.1.me_ref, s32[1,32]{1,0:T(1,128)} %len_ref.3, s32[32,32]{1,0:T(8,128)} %id_ref.3, s32[256]{0:T(256)} %slot_ref.3, bf16[512,512]{1,0:T(8,128)(2,1)} %x_ref.5), custom_call_target="tpu_custom_call" | custom-call | flops 536870912 | bytes 1572864 | tf_op jit(solution)/shard_map/pack/pallas_call | solution.py:206
  2.7 3.8 %pair_dot.2 = bf16[2,512,1024]{2,1,0:T(8,128)(2,1)} custom-call(s32[1]{0:T(128)} %bitcast.t_ref, bf16[512,512]{1,0:T(8,128)(2,1)} %x_ref.5, bf16[512,8192]{1,0:T(8,128)(2,1)} %w_ref.7), custom_call_target="tpu_custom_call" | custom-call | flops 1073741824 | bytes 4194304 | tf_op jit(solution)/shard_map/pair_dot/pallas_call | solution.py:224
  6.5 11.5 %all-to-all-start = ((bf16[32,32,512]{2,1,0:T(8,128)(2,1)}), bf16[32,32,512]{2,1,0:T(8,128)(2,1)S(1)}, u32[]{:S(2)}, u32[]{:S(2)}) async-start(bf16[32,32,512]{2,1,0:T(8,128)(2,1)} %bitcast.17), calls=%async_computation | async-start | bytes 2097152 | tf_op jit(solution)/shard_map/all_to_all | solution.py:215
  18.0 3.8 %pair_dot.3 = bf16[2,512,1024]{2,1,0:T(8,128)(2,1)} custom-call(s32[1]{0:T(128)} %bitcast.t_ref, bf16[512,512]{1,0:T(8,128)(2,1)} %x_ref.5, bf16[512,8192]{1,0:T(8,128)(2,1)} %w_ref.7), custom_call_target="tpu_custom_call" | custom-call | flops 1073741824 | bytes 4194304 | tf_op jit(solution)/shard_map/pair_dot/pallas_call | solution.py:224
  21.9 4.4 %own_dot.2 = (bf16[256,1024]{1,0:T(8,128)(2,1)}, bf16[256,1024]{1,0:T(8,128)(2,1)}, bf16[256,1024]{1,0:T(8,128)(2,1)}, bf16[256,1024]{1,0:T(8,128)(2,1)}) custom-call(s32[1]{0:T(128)} %bitcast.t_ref, bf16[512,512]{1,0:T(8,128)(2,1)} %x_ref.5, bf16[512,8192]{1,0:T(8,128)(2,1)} %w_ref.7, bf16[2,512,1024]{2,1,0:T(8,128)(2,1)S(1)} %collective-permute-done.p_ref), custom_call_target="tpu_custom_call" | custom-call | flops 1073741824 | bytes 6291456 | tf_op jit(solution)/shard_map/own_dot/pallas_call | solution.py:240
  26.5 0.7 select_reduce_fusion
  27.3 1.2 %fetch_up.1.u_ref = bf16[512,1024]{1,0:T(8,128)(2,1)S(1)} custom-call(bf16[512,1024]{1,0:T(8,128)(2,1)} %bitcast.16), custom_call_target="tpu_custom_call" | custom-call | bytes 2097152 | tf_op jit(solution)/shard_map/fetch_up/pallas_call | solution.py:280
  28.8 18.4 %all-to-all-done = bf16[32,32,512]{2,1,0:T(8,128)(2,1)S(1)} async-done(((bf16[32,32,512]{2,1,0:T(8,128)(2,1)}), bf16[32,32,512]{2,1,0:T(8,128)(2,1)S(1)}, u32[]{:S(2)}, u32[]{:S(2)}) %all-to-all-start) | async-done | bytes 1048608 | tf_op jit(solution)/shard_map/all_to_all | solution.py:215
  48.4 0.7 collective-permute-done.1.refs_1_
  49.7 0.9 collective-permute-start.3
  50.6 3.3 %collective-permute-start.2 = (bf16[256,128]{1,0:T(8,128)(2,1)S(1)}, bf16[256,128]{1,0:T(8,128)(2,1)S(1)}, u32[]{:S(2)}, u32[]{:S(2)}) collective-permute-start(bf16[256,128]{1,0:T(8,128)(2,1)S(1)} %sum_low.2.refs_0_), channel_id=1, source_target_pairs={{0,128},{32,160},{64,192},{96,224},{128,0},{160,32},{192,64},{224,... | collective-permute-start | bytes 196616 | tf_op jit(solution)/shard_map/ppermute | solution.py:327
  53.9 0.8 collective-permute-done.4.refs_3_
  54.7 2.5 %collective-permute-done.2.refs_1_ = bf16[256,128]{1,0:T(8,128)(2,1)S(1)} collective-permute-done((bf16[256,128]{1,0:T(8,128)(2,1)S(1)}, bf16[256,128]{1,0:T(8,128)(2,1)S(1)}, u32[]{:S(2)}, u32[]{:S(2)}) %collective-permute-start.2) | collective-permute-done | bytes 65568 | tf_op jit(solution)/shard_map/ppermute | solution.py:327
  57.3 1.5 %up.2.rest_0_ = bf16[1024,1024]{1,0:T(8,128)(2,1)} custom-call(s32[1]{0:T(128)S(6)} %and.5.core_ref, s32[1024,128]{1,0:T(8,128)S(1)} %broadcast_subtract_fusion.code_ref, bf16[256,128]{1,0:T(8,128)(2,1)S(1)} %sum_low.3.low_ref, bf16[512,1024]{1,0:T(8,128)(2,1)S(1)} %fetch_up.1.u_ref), custom_call_target="tpu_custom_call" | custom-call | flops 536870912 | bytes 1048576 | tf_op jit(solution)/shard_map/up/pallas_call | solution.py:332
  58.8 1.5 %up.3 = bf16[1024,1024]{1,0:T(8,128)(2,1)} custom-call(s32[1]{0:T(128)S(6)} %and.5.core_ref, s32[1024,128]{1,0:T(8,128)S(1)} %broadcast_subtract_fusion.code_ref, bf16[256,128]{1,0:T(8,128)(2,1)S(1)} %collective-permute-done.5.low_ref, bf16[512,1024]{1,0:T(8,128)(2,1)S(1)} %fetch_up.1.u_ref, ...), custom_call_target="tpu_custom_call", output_to_operand_aliasing={{}: (4, {})} | custom-call | flops 536870912 | bytes 1048576 | tf_op jit(solution)/shard_map/up/pallas_call | solution.py:332
  60.3 5.2 %all-to-all-start.1 = ((bf16[32,32,1024]{2,1,0:T(8,128)(2,1)}), bf16[32,32,1024]{2,1,0:T(8,128)(2,1)S(1)}, u32[]{:S(2)}, u32[]{:S(2)}) async-start(bf16[32,32,1024]{2,1,0:T(8,128)(2,1)} %bitcast.15), calls=%async_computation.1 | async-start | bytes 4194304 | tf_op jit(solution)/shard_map/all_to_all | solution.py:347
  66.2 2.8 %collective-permute-start.11 = (bf16[256,1024]{1,0:T(8,128)(2,1)}, bf16[256,1024]{1,0:T(8,128)(2,1)S(1)}, u32[]{:S(2)}, u32[]{:S(2)}) collective-permute-start(bf16[256,1024]{1,0:T(8,128)(2,1)} %get-tuple-element.57), channel_id=1, source_target_pairs={{0,192},{32,224},{64,128},{96,160},{128,64},{160,96},{192,0},{224,... | collective-permute-start | bytes 1572872 | tf_op jit(solution)/shard_map/ppermute | solution.py:268
  68.9 1.2 %collective-permute-done.6.p_ref = bf16[2,512,1024]{2,1,0:T(8,128)(2,1)} collective-permute-done((bf16[2,512,1024]{2,1,0:T(8,128)(2,1)}, bf16[2,512,1024]{2,1,0:T(8,128)(2,1)}, u32[]{:S(2)}, u32[]{:S(2)}) %collective-permute-start.6) | collective-permute-done | bytes 2097184 | tf_op jit(solution)/shard_map/ppermute | solution.py:264
  70.1 4.7 %own_dot.3 = (bf16[256,1024]{1,0:T(8,128)(2,1)}, bf16[256,1024]{1,0:T(8,128)(2,1)}, bf16[256,1024]{1,0:T(8,128)(2,1)}, bf16[256,1024]{1,0:T(8,128)(2,1)}) custom-call(s32[1]{0:T(128)} %bitcast.t_ref, bf16[512,512]{1,0:T(8,128)(2,1)} %x_ref.5, bf16[512,8192]{1,0:T(8,128)(2,1)} %w_ref.7, bf16[2,512,1024]{2,1,0:T(8,128)(2,1)} %collective-permute-done.6.p_ref), custom_call_target="tpu_custom_call" | custom-call | flops 1073741824 | bytes 6291456 | tf_op jit(solution)/shard_map/own_dot/pallas_call | solution.py:240
  74.8 1.3 %collective-permute-start.10 = (bf16[256,1024]{1,0:T(8,128)(2,1)}, bf16[256,1024]{1,0:T(8,128)(2,1)S(1)}, u32[]{:S(2)}, u32[]{:S(2)}) collective-permute-start(bf16[256,1024]{1,0:T(8,128)(2,1)} %get-tuple-element.55), channel_id=1, source_target_pairs={{0,192},{32,224},{64,128},{96,160},{128,64},{160,96},{192,0},{224,... | collective-permute-start | bytes 1572872 | tf_op jit(solution)/shard_map/ppermute | solution.py:365
  76.1 1.2 %collective-permute-start.7 = (bf16[256,1024]{1,0:T(8,128)(2,1)}, bf16[256,1024]{1,0:T(8,128)(2,1)S(1)}, u32[]{:S(2)}, u32[]{:S(2)}) collective-permute-start(bf16[256,1024]{1,0:T(8,128)(2,1)} %get-tuple-element.52), channel_id=1, source_target_pairs={{0,64},{32,96},{64,0},{96,32},{128,192},{160,224},{192,128},{224,1... | collective-permute-start | bytes 1572872 | tf_op jit(solution)/shard_map/ppermute | solution.py:364
  77.3 3.7 %collective-permute-done.8 = bf16[256,1024]{1,0:T(8,128)(2,1)} collective-permute-done((bf16[256,1024]{1,0:T(8,128)(2,1)}, bf16[256,1024]{1,0:T(8,128)(2,1)}, u32[]{:S(2)}, u32[]{:S(2)}) %collective-permute-start.8) | collective-permute-done | bytes 524320 | tf_op jit(solution)/shard_map/ppermute | solution.py:267
  81.0 1.4 %add_convert_fusion.1 = bf16[256,1024]{1,0:T(8,128)(2,1)S(1)} fusion(bf16[256,1024]{1,0:T(8,128)(2,1)} %collective-permute-done.8, bf16[256,1024]{1,0:T(8,128)(2,1)} %get-tuple-element.53), kind=kLoop, calls=%fused_computation.1 | loop fusion | flops 1048576 | bytes 1572864 | tf_op jit(solution)/shard_map/convert_element_type | solution.py:362
  82.4 1.4 %collective-permute-start.9 = (bf16[256,1024]{1,0:T(8,128)(2,1)S(1)}, bf16[256,1024]{1,0:T(8,128)(2,1)S(1)}, u32[]{:S(2)}, u32[]{:S(2)}) collective-permute-start(bf16[256,1024]{1,0:T(8,128)(2,1)S(1)} %add_convert_fusion.1), channel_id=1, source_target_pairs={{0,192},{32,224},{64,128},{96,160},{128,64},{160,96},{192,0},{224,... | collective-permute-start | bytes 1572872 | tf_op jit(solution)/shard_map/ppermute | solution.py:362
  83.9 1.3 %collective-permute-start.12 = (bf16[256,1024]{1,0:T(8,128)(2,1)S(1)}, bf16[256,1024]{1,0:T(8,128)(2,1)S(1)}, u32[]{:S(2)}, u32[]{:S(2)}) collective-permute-start(bf16[256,1024]{1,0:T(8,128)(2,1)S(1)} %add_convert_fusion), channel_id=1, source_target_pairs={{0,64},{32,96},{64,0},{96,32},{128,192},{160,224},{192,128},{224,1... | collective-permute-start | bytes 1572872 | tf_op jit(solution)/shard_map/ppermute | solution.py:363
  85.2 1.7 %unpack_index.1.row_ref = s32[512,128]{1,0:T(8,128)S(1)} custom-call(s32[1]{0:T(128)} %bitcast.1.me_ref, s32[1,32]{1,0:T(1,128)S(1)} %copy-done.3, s32[32,32]{1,0:T(8,128)S(1)} %copy-done.1, s32[256]{0:T(256)S(1)} %copy-done.2), custom_call_target="tpu_custom_call" | custom-call | flops 4194304 | bytes 262144 | tf_op jit(solution)/shard_map/unpack_index/pallas_call | solution.py:351
  86.9 6.7 %collective-permute-done.10.rb_ref = bf16[256,1024]{1,0:T(8,128)(2,1)S(1)} collective-permute-done((bf16[256,1024]{1,0:T(8,128)(2,1)}, bf16[256,1024]{1,0:T(8,128)(2,1)S(1)}, u32[]{:S(2)}, u32[]{:S(2)}) %collective-permute-start.10) | collective-permute-done | bytes 524320 | tf_op jit(solution)/shard_map/ppermute | solution.py:365
  93.6 10.3 %collective-permute-done.9.za_ref = bf16[256,1024]{1,0:T(8,128)(2,1)S(1)} collective-permute-done((bf16[256,1024]{1,0:T(8,128)(2,1)S(1)}, bf16[256,1024]{1,0:T(8,128)(2,1)S(1)}, u32[]{:S(2)}, u32[]{:S(2)}) %collective-permute-start.9) | collective-permute-done | bytes 524320 | tf_op jit(solution)/shard_map/ppermute | solution.py:362
  103.9 0.8 copy-done.7
  104.9 3.4 %before.1 = (f32[512,512]{1,0:T(8,128)S(1)}, f32[512,512]{1,0:T(8,128)}) custom-call(bf16[512,1024]{1,0:T(8,128)(2,1)} %res_ref.1, bf16[256,1024]{1,0:T(8,128)(2,1)} %get-tuple-element.51.ka_ref, bf16[256,1024]{1,0:T(8,128)(2,1)} %copy-done.6, bf16[256,1024]{1,0:T(8,128)(2,1)} %copy-done.7, bf16[256,1024]{1,0:T(8,128)(2,1)} %get-tuple-element.54.kb_ref, ...), custom_call_target="tpu_custom_call" | custom-call | flops 2097152 | bytes 6291456 | tf_op jit(solution)/shard_map/before/pallas_call | solution.py:368
  108.3 7.8 %all-to-all-done.1 = bf16[32,32,1024]{2,1,0:T(8,128)(2,1)S(1)} async-done(((bf16[32,32,1024]{2,1,0:T(8,128)(2,1)}), bf16[32,32,1024]{2,1,0:T(8,128)(2,1)S(1)}, u32[]{:S(2)}, u32[]{:S(2)}) %all-to-all-start.1) | async-done | bytes 2097184 | tf_op jit(solution)/shard_map/all_to_all | solution.py:347
  116.1 2.8 %final.1 = bf16[512,1024]{1,0:T(8,128)(2,1)} custom-call(s32[512,128]{1,0:T(8,128)S(1)} %unpack_index.1.row_ref, bf16[1024,1024]{1,0:T(8,128)(2,1)S(1)} %bitcast.12, f32[512,512]{1,0:T(8,128)S(1)} %get-tuple-element.63.left_ref, f32[512,512]{1,0:T(8,128)} %get-tuple-element.64.right_ref), custom_call_target="tpu_custom_call" | custom-call | flops 1073741824 | bytes 6291456 | tf_op jit(solution)/shard_map/final/pallas_call | solution.py:377
  (40 shorter events, 3.5 us)
Async XLA Ops:
  6.5 15.3 %collective-permute-start = (bf16[2,512,1024]{2,1,0:T(8,128)(2,1)}, bf16[2,512,1024]{2,1,0:T(8,128)(2,1)S(1)}, u32[]{:S(2)}, u32[]{:S(2)}) collective-permute-start(bf16[2,512,1024]{2,1,0:T(8,128)(2,1)} %pair_dot.2), channel_id=1, source_target_pairs={{0,32},{32,0},{64,96},{96,64},{128,160},{160,128},{192,224},{224,1... | collective-permute-start | bytes 6291464 | tf_op jit(solution)/shard_map/ppermute | solution.py:261
  6.5 40.7 %all-to-all-start = ((bf16[32,32,512]{2,1,0:T(8,128)(2,1)}), bf16[32,32,512]{2,1,0:T(8,128)(2,1)S(1)}, u32[]{:S(2)}, u32[]{:S(2)}) async-start(bf16[32,32,512]{2,1,0:T(8,128)(2,1)} %bitcast.17), calls=%async_computation | async-start | bytes 2097152 | tf_op jit(solution)/shard_map/all_to_all | solution.py:215
  21.8 4.4 %copy-start.2 = (s32[256]{0:T(256)S(1)}, s32[256]{0:T(256)}, u32[]{:S(2)}) copy-start(s32[256]{0:T(256)} %slot_ref.3) | copy-start | bytes 3076
  21.9 4.6 %copy-start.1 = (s32[32,32]{1,0:T(8,128)S(1)}, s32[32,32]{1,0:T(8,128)}, u32[]{:S(2)}) copy-start(s32[32,32]{1,0:T(8,128)} %id_ref.3) | copy-start | bytes 12292
  26.3 21.0 %copy-start = (bf16[8,512,64]{1,2,0:T(8,128)(2,1)S(1)}, bf16[8,512,64]{1,2,0:T(8,128)(2,1)}, u32[]{:S(2)}) copy-start(bf16[8,512,64]{1,2,0:T(8,128)(2,1)} %param.11) | copy-start | bytes 1572868
  47.8 1.3 %collective-permute-start.1 = (bf16[256,128]{1,0:T(8,128)(2,1)S(1)}, bf16[256,128]{1,0:T(8,128)(2,1)S(1)}, u32[]{:S(2)}, u32[]{:S(2)}) collective-permute-start(bf16[256,128]{1,0:T(8,128)(2,1)S(1)} %down.2), channel_id=1, source_target_pairs={{0,32},{32,0},{64,96},{96,64},{128,160},{160,128},{192,224},{224,1... | collective-permute-start | bytes 196616 | tf_op jit(solution)/shard_map/ppermute | solution.py:310
  49.1 5.6 %collective-permute-start.4 = (bf16[256,128]{1,0:T(8,128)(2,1)S(1)}, bf16[256,128]{1,0:T(8,128)(2,1)S(1)}, u32[]{:S(2)}, u32[]{:S(2)}) collective-permute-start(bf16[256,128]{1,0:T(8,128)(2,1)S(1)} %sum_low.2.refs_0_), channel_id=1, source_target_pairs={{0,192},{32,224},{64,128},{96,160},{128,64},{160,96},{192,0},{224,... | collective-permute-start | bytes 196616 | tf_op jit(solution)/shard_map/ppermute | solution.py:327
  49.7 5.0 %collective-permute-start.3 = (bf16[256,128]{1,0:T(8,128)(2,1)S(1)}, bf16[256,128]{1,0:T(8,128)(2,1)S(1)}, u32[]{:S(2)}, u32[]{:S(2)}) collective-permute-start(bf16[256,128]{1,0:T(8,128)(2,1)S(1)} %sum_low.2.refs_0_), channel_id=1, source_target_pairs={{0,64},{32,96},{64,0},{96,32},{128,192},{160,224},{192,128},{224,1... | collective-permute-start | bytes 196616 | tf_op jit(solution)/shard_map/ppermute | solution.py:327
  50.6 6.6 %collective-permute-start.2 = (bf16[256,128]{1,0:T(8,128)(2,1)S(1)}, bf16[256,128]{1,0:T(8,128)(2,1)S(1)}, u32[]{:S(2)}, u32[]{:S(2)}) collective-permute-start(bf16[256,128]{1,0:T(8,128)(2,1)S(1)} %sum_low.2.refs_0_), channel_id=1, source_target_pairs={{0,128},{32,160},{64,192},{96,224},{128,0},{160,32},{192,64},{224,... | collective-permute-start | bytes 196616 | tf_op jit(solution)/shard_map/ppermute | solution.py:327
  57.2 1.6 %collective-permute-start.5 = (bf16[256,128]{1,0:T(8,128)(2,1)S(1)}, bf16[256,128]{1,0:T(8,128)(2,1)S(1)}, u32[]{:S(2)}, u32[]{:S(2)}) collective-permute-start(bf16[256,128]{1,0:T(8,128)(2,1)S(1)} %sum_low.3.low_ref), channel_id=1, source_target_pairs={{0,32},{32,0},{64,96},{96,64},{128,160},{160,128},{192,224},{224,1... | collective-permute-start | bytes 196616 | tf_op jit(solution)/shard_map/ppermute | solution.py:329
  60.3 55.8 %all-to-all-start.1 = ((bf16[32,32,1024]{2,1,0:T(8,128)(2,1)}), bf16[32,32,1024]{2,1,0:T(8,128)(2,1)S(1)}, u32[]{:S(2)}, u32[]{:S(2)}) async-start(bf16[32,32,1024]{2,1,0:T(8,128)(2,1)} %bitcast.15), calls=%async_computation.1 | async-start | bytes 4194304 | tf_op jit(solution)/shard_map/all_to_all | solution.py:347
  65.6 4.6 %collective-permute-start.6 = (bf16[2,512,1024]{2,1,0:T(8,128)(2,1)}, bf16[2,512,1024]{2,1,0:T(8,128)(2,1)}, u32[]{:S(2)}, u32[]{:S(2)}) collective-permute-start(bf16[2,512,1024]{2,1,0:T(8,128)(2,1)} %pair_dot.3), channel_id=1, source_target_pairs={{0,32},{32,0},{64,96},{96,64},{128,160},{160,128},{192,224},{224,1... | collective-permute-start | bytes 6291464 | tf_op jit(solution)/shard_map/ppermute | solution.py:264
  65.8 15.1 %collective-permute-start.8 = (bf16[256,1024]{1,0:T(8,128)(2,1)}, bf16[256,1024]{1,0:T(8,128)(2,1)}, u32[]{:S(2)}, u32[]{:S(2)}) collective-permute-start(bf16[256,1024]{1,0:T(8,128)(2,1)} %get-tuple-element.38), channel_id=1, source_target_pairs={{0,64},{32,96},{64,0},{96,32},{128,192},{160,224},{192,128},{224,1... | collective-permute-start | bytes 1572872 | tf_op jit(solution)/shard_map/ppermute | solution.py:267
  66.2 17.6 %copy-start.4 = (bf16[256,1024]{1,0:T(8,128)(2,1)S(1)}, bf16[256,1024]{1,0:T(8,128)(2,1)}, u32[]{:S(2)}) copy-start(bf16[256,1024]{1,0:T(8,128)(2,1)} %get-tuple-element.56) | copy-start | bytes 1572868
  66.2 17.6 %collective-permute-start.11 = (bf16[256,1024]{1,0:T(8,128)(2,1)}, bf16[256,1024]{1,0:T(8,128)(2,1)S(1)}, u32[]{:S(2)}, u32[]{:S(2)}) collective-permute-start(bf16[256,1024]{1,0:T(8,128)(2,1)} %get-tuple-element.57), channel_id=1, source_target_pairs={{0,192},{32,224},{64,128},{96,160},{128,64},{160,96},{192,0},{224,... | collective-permute-start | bytes 1572872 | tf_op jit(solution)/shard_map/ppermute | solution.py:268
  74.8 10.4 %copy-start.3 = (s32[1,32]{1,0:T(1,128)S(1)}, s32[1,32]{1,0:T(1,128)}, u32[]{:S(2)}) copy-start(s32[1,32]{1,0:T(1,128)} %len_ref.3) | copy-start | bytes 388
  74.8 18.8 %collective-permute-start.10 = (bf16[256,1024]{1,0:T(8,128)(2,1)}, bf16[256,1024]{1,0:T(8,128)(2,1)S(1)}, u32[]{:S(2)}, u32[]{:S(2)}) collective-permute-start(bf16[256,1024]{1,0:T(8,128)(2,1)} %get-tuple-element.55), channel_id=1, source_target_pairs={{0,192},{32,224},{64,128},{96,160},{128,64},{160,96},{192,0},{224,... | collective-permute-start | bytes 1572872 | tf_op jit(solution)/shard_map/ppermute | solution.py:365
  76.1 17.5 %collective-permute-start.7 = (bf16[256,1024]{1,0:T(8,128)(2,1)}, bf16[256,1024]{1,0:T(8,128)(2,1)S(1)}, u32[]{:S(2)}, u32[]{:S(2)}) collective-permute-start(bf16[256,1024]{1,0:T(8,128)(2,1)} %get-tuple-element.52), channel_id=1, source_target_pairs={{0,64},{32,96},{64,0},{96,32},{128,192},{160,224},{192,128},{224,1... | collective-permute-start | bytes 1572872 | tf_op jit(solution)/shard_map/ppermute | solution.py:364
  82.4 21.6 %collective-permute-start.9 = (bf16[256,1024]{1,0:T(8,128)(2,1)S(1)}, bf16[256,1024]{1,0:T(8,128)(2,1)S(1)}, u32[]{:S(2)}, u32[]{:S(2)}) collective-permute-start(bf16[256,1024]{1,0:T(8,128)(2,1)S(1)} %add_convert_fusion.1), channel_id=1, source_target_pairs={{0,192},{32,224},{64,128},{96,160},{128,64},{160,96},{192,0},{224,... | collective-permute-start | bytes 1572872 | tf_op jit(solution)/shard_map/ppermute | solution.py:362
  83.9 20.0 %collective-permute-start.12 = (bf16[256,1024]{1,0:T(8,128)(2,1)S(1)}, bf16[256,1024]{1,0:T(8,128)(2,1)S(1)}, u32[]{:S(2)}, u32[]{:S(2)}) collective-permute-start(bf16[256,1024]{1,0:T(8,128)(2,1)S(1)} %add_convert_fusion), channel_id=1, source_target_pairs={{0,64},{32,96},{64,0},{96,32},{128,192},{160,224},{192,128},{224,1... | collective-permute-start | bytes 1572872 | tf_op jit(solution)/shard_map/ppermute | solution.py:363
  93.6 10.3 %copy-start.5 = (bf16[256,1024]{1,0:T(8,128)(2,1)}, bf16[256,1024]{1,0:T(8,128)(2,1)S(1)}, u32[]{:S(2)}) copy-start(bf16[256,1024]{1,0:T(8,128)(2,1)S(1)} %collective-permute-done.10.rb_ref) | copy-start | bytes 1572868
  93.6 10.3 %copy-start.6 = (bf16[256,1024]{1,0:T(8,128)(2,1)}, bf16[256,1024]{1,0:T(8,128)(2,1)S(1)}, u32[]{:S(2)}) copy-start(bf16[256,1024]{1,0:T(8,128)(2,1)S(1)} %collective-permute-done.7.ra_ref) | copy-start | bytes 1572868
  103.9 0.8 copy-start.7
  103.9 1.0 copy-start.8
